TPU v7x, 128 devices: a whole 4x4x4 slice. The times are simulated.
128 devices in a mesh: sect: 2 (over y_lo), op: 64 (over x, y_hi, z, core).
Axes of the slice: x: 4, y: 4 (y_hi: 2, y_lo: 2; y = y_hi * 2 + y_lo), z: 4, core: 2. Of those that a mesh axis runs over, the one named last changes fastest.
Arguments:
- wave: bfloat16 [2, 8192, 256], P('sect', 'op'), may hold values from -6 to 6
- left_ops: bfloat16 [2, 192, 8, 256, 256], P('sect', 'op'), may hold values from -1 to 1
- right_ops: bfloat16 [2, 192, 8, 256, 256], P('sect', 'op'), may hold values from -0.375 to 0.375
- site_ops: float32 [2, 192, 4, 4], P('sect', 'op'), may hold values from -0.21875 to 0.21875
- reach: int32 [2, 192], P('sect', 'op'), may hold values from 1 to 8
- pairing: int32 [2, 8], P('sect'), may hold values from 0 to 7, each once within a row
- site_tensor: bfloat16 [2, 8, 4, 256, 256], P('sect'), may hold values from -0.25 to 0.25
Outputs:
- first_image: bfloat16 [2, 8192, 256], P('sect', 'op')
- second_image: bfloat16 [2, 8192, 256], P('sect', 'op')
- moved_image: bfloat16 [2, 8192, 256], P('sect', 'op')
Inputs may be any that keep to these rules, and one draw needn't show every extreme that they name: Each term couples the sectors 0 to reach - 1. `pairing`: each row is a permutation of the 8 sectors.
All inputs are finite; a program needn't handle non-finite values.
Results may differ from a plain program's by a relative error of at most 0.008.
Values may be sent and summed in bfloat16 or wider, within the bound.
No kernel may reach another device: no remote copies, remote signals or barrier semaphores. Data moves between devices by JAX's collectives and lax.ppermute only.
A program may use at most 128 MiB of HBM per device.

v0:
```python
import jax
import jax.numpy as jnp
from jax import lax
from jax.sharding import PartitionSpec as P


def from_behind(value, axis, steps):
    count = lax.axis_size(axis)
    pairs = [(source, (source + steps) % count) for source in range(count)]
    return lax.ppermute(value, axis, pairs)


def apply_local(rows, lefts, rights, mixers, limits, pair):
    sectors = lefts.shape[1]
    block = lefts.shape[2]
    local = mixers.shape[1]
    blocks = rows.reshape(sectors, local, block, block)
    sector_ids = jnp.arange(sectors, dtype=jnp.int32)
    total = jnp.zeros(blocks.shape, jnp.float32)
    for term in range(lefts.shape[0]):
        lifted = jnp.einsum(
            "qab,qsbc->qsac", lefts[term], blocks, preferred_element_type=jnp.float32
        ).astype(jnp.bfloat16)
        mask = (sector_ids < limits[term]).astype(jnp.float32)
        mixed = jnp.einsum(
            "xy,qyac->qxac",
            mixers[term],
            lifted.astype(jnp.float32),
            precision=lax.Precision.HIGHEST,
        )
        mixed = (mixed * mask[:, None, None, None]).astype(jnp.bfloat16)
        paired = jnp.take(rights[term], pair, axis=0)
        total = total + jnp.einsum(
            "qsac,qdc->qsad", mixed, paired, preferred_element_type=jnp.float32
        )
    return total.reshape(rows.shape)


def renew_boundary(lefts, tensor, pair):
    sectors = lefts.shape[1]
    onehot = (pair[:, None] == jnp.arange(sectors, dtype=jnp.int32)[None, :]).astype(jnp.bfloat16)
    placed_all = []
    for term in range(lefts.shape[0]):
        lifted = jnp.einsum(
            "qab,qsbc->qsac", lefts[term], tensor, preferred_element_type=jnp.float32
        ).astype(jnp.bfloat16)
        reduced = jnp.einsum(
            "qsad,qsac->qdc", tensor, lifted, preferred_element_type=jnp.float32
        ).astype(jnp.bfloat16)
        placed = jnp.einsum("qj,qdc->jdc", onehot, reduced, preferred_element_type=jnp.float32)
        placed_all.append(placed.astype(jnp.bfloat16))
    renewed = jnp.stack(placed_all)
    return from_behind(renewed, "sect", 1)


def shards(wave, left_ops, right_ops, site_ops, reach, pairing, site_tensor):
    lefts = left_ops[0]
    rights = right_ops[0]
    mixers = site_ops[0]
    limits = reach[0]
    pair = pairing[0]
    count = wave.shape[1]
    whole = lax.all_gather(wave[0], "op", axis=0, tiled=True)
    first_part = apply_local(whole, lefts, rights, mixers, limits, pair)
    first_full = lax.psum(first_part, "op").astype(jnp.bfloat16)
    first_own = lax.dynamic_slice_in_dim(first_full, lax.axis_index("op") * count, count, 0)
    moved_lefts = renew_boundary(lefts, site_tensor[0], pair)
    second_part = apply_local(first_full, lefts, rights, mixers, limits, pair)
    second_own = lax.psum_scatter(second_part, "op", scatter_dimension=0, tiled=True).astype(
        jnp.bfloat16
    )
    moved_part = apply_local(whole, moved_lefts, rights, mixers, limits, pair)
    moved_own = lax.psum_scatter(moved_part, "op", scatter_dimension=0, tiled=True).astype(
        jnp.bfloat16
    )
    return (first_own[None], second_own[None], moved_own[None])


def solution(mesh):
    placed = (
        P("sect", "op", None),
        P("sect", "op", None, None, None),
        P("sect", "op", None, None, None),
        P("sect", "op", None, None),
        P("sect", "op"),
        P("sect", None),
        P("sect", None, None, None, None),
    )
    return jax.shard_map(
        shards,
        mesh=mesh,
        in_specs=placed,
        out_specs=(P("sect", "op", None), P("sect", "op", None), P("sect", "op", None)),
        check_vma=False,
    )
```

profile of v0, /device:TPU:0, one launch (start us, length us, event | category | flops | bytes accessed | tf_op | source)
XLA Modules:
  0.0 1097.3 jit_solution(1055049753114756969)
XLA Ops:
  7.2 0.0 all-gather.3.cloned.1.call-start
  7.2 0.7 all-gather.3.cloned.1.call-update
  7.9 0.0 reduce-scatter.5.cloned.1.call-start
  8.0 7.3 fusion.41
  15.3 2.6 copy.32
  17.9 6.8 fusion.39
  24.8 2.7 copy.33
  27.4 6.9 fusion.43
  34.3 1.9 copy.31
  36.3 1.6 fusion.85
  37.9 0.4 fusion.86
  38.4 0.4 fusion.84
  38.8 2.1 pad_maximum_fusion
  40.9 1.8 collective-permute-start
  42.7 1.3 slice_bitcast_fusion.3
  44.0 0.6 gather_fusion.2
  44.6 0.6 gather_fusion
  45.2 1.8 gather_fusion.1
  47.1 0.6 fusion.160
  47.7 0.6 compare_convert_fusion
  48.3 0.7 compare_convert_fusion.2
  49.0 0.7 compare_convert_fusion.1
  49.7 70.7 %collective-permute-done = bf16[3,8,256,256]{3,1,2,0:T(8,128)(2,1)} collective-permute-done((bf16[3,8,256,256]{3,1,2,0:T(8,128)(2,1)}, bf16[3,8,256,256]{3,1,2,0:T(8,128)(2,1)}, u32[]{:S(2)}, u32[]{:S(2)}) %collective-permute-start) | collective-permute-done | bytes 3145760 | tf_op jit(solution)/shard_map/ppermute | solution.py:10
  120.4 3.6 slice_bitcast_fusion
  124.0 6.2 convert_bitcast_fusion.3
  130.2 3.5 convert_bitcast_fusion.4
  133.7 3.5 convert_bitcast_fusion.5
  137.2 1.3 convolution_convert_fusion
  138.5 1.3 convolution_convert_fusion.1
  139.8 9.4 fusion.36
  149.2 14.6 %fusion.37 = f32[8,256,256,4]{2,3,1,0:T(4,128)S(1)} fusion(bf16[8,256,4,256]{3,1,2,0:T(8,128)(2,1)S(1)} %convolution_convert_fusion.1, f32[1,3,4,4]{3,2,1,0:T(4,128)S(1)} %copy-done.11), kind=kOutput, calls=%fused_computation.45 | convolution fusion | flops 100663296 | bytes 12584960 | tf_op jit(solution)/shard_map/xy,qyac->qxac/dot_general | solution.py:25
  163.8 3.2 convolution_convert_fusion.2
  167.1 11.5 %fusion.38 = f32[8,256,256,4]{2,3,1,0:T(4,128)S(1)} fusion(bf16[8,256,4,256]{3,1,2,0:T(8,128)(2,1)} %convolution_convert_fusion.2, f32[1,3,4,4]{3,2,1,0:T(4,128)S(1)} %copy-done.11), kind=kOutput, calls=%fused_computation.47 | convolution fusion | flops 100663296 | bytes 12584960 | tf_op jit(solution)/shard_map/xy,qyac->qxac/dot_general | solution.py:25
  178.6 4.9 fusion.31
  183.5 4.9 fusion.28
  188.3 14.0 %add_add_fusion = f32[8,4,256,256]{3,2,1,0:T(8,128)} fusion(f32[8,4,256,256]{3,2,1,0:T(8,128)} %fusion.28, f32[8,4,256,256]{3,2,1,0:T(8,128)} %fusion.31, f32[8,256,256,4]{2,3,1,0:T(4,128)} %fusion.36, f32[8]{0:T(128)S(1)} %compare_convert_fusion, bf16[8,256,256]{2,1,0:T(8,128)(2,1)S(1)} %gather_fusion.2, pred[8]{0:T(512)(128)(4,1)S(1)} %compare_and_fusion), kind=kOutput, calls=%fused_computation.21 | convolution fusion | flops 1082654720 | bytes 34603048 | tf_op jit(solution)/shard_map/qsac,qdc->qsad/dot_general | solution.py:33
  202.3 0.0 reduce-scatter.5.cloned.1.call-update
  202.3 0.0 reduce-scatter.3.cloned.1.call-start
  202.4 7.6 copy.21
  210.0 10.5 fusion.136
  220.5 7.5 copy.11
  228.0 7.5 copy.16
  235.4 8.6 fusion.141
  244.1 7.1 fusion.146
  251.2 4.9 fusion.13
  256.1 4.9 fusion.10
  260.9 14.1 %add_add_fusion.2 = f32[8,4,256,256]{3,2,1,0:T(8,128)} fusion(f32[8,4,256,256]{3,2,1,0:T(8,128)} %fusion.10, f32[8,4,256,256]{3,2,1,0:T(8,128)} %fusion.13, f32[8,256,256,4]{2,3,1,0:T(4,128)} %fusion.136, f32[8]{0:T(128)S(1)} %compare_convert_fusion, bf16[8,256,256]{2,1,0:T(8,128)(2,1)S(1)} %gather_fusion.2, pred[8]{0:T(512)(128)(4,1)S(1)} %compare_and_fusion), kind=kOutput, calls=%fused_computation.23 | convolution fusion | flops 1082654720 | bytes 34603048 | tf_op jit(solution)/shard_map/qsac,qdc->qsad/dot_general | solution.py:33
  275.0 383.6 %all-reduce.1 = bf16[8192,256]{1,0:T(8,128)(2,1)} all-reduce(f32[8192,256]{1,0:T(8,128)} %bitcast.278), channel_id=1, replica_groups=mesh['sect'=2,'op'=64] {'op'}, use_global_device_ids=true, to_apply=%region_0.0 | all-reduce | flops 2097152 | bytes 12582912 | tf_op jit(solution)/shard_map/psum | solution.py:65
  658.6 5.9 convert_bitcast_fusion
  664.5 7.4 copy.29
  672.0 5.9 convert_bitcast_fusion.2
  677.9 7.5 copy.25
  685.3 5.9 convert_bitcast_fusion.1
  691.3 7.4 copy.27
  698.7 10.7 fusion.134
  709.4 7.1 fusion.139
  716.5 7.2 fusion.144
  723.7 4.9 fusion.22
  728.6 4.9 fusion.19
  733.5 14.0 %add_add_fusion.1 = f32[8,4,256,256]{3,2,1,0:T(8,128)} fusion(f32[8,4,256,256]{3,2,1,0:T(8,128)} %fusion.19, f32[8,4,256,256]{3,2,1,0:T(8,128)} %fusion.22, f32[8,256,256,4]{2,3,1,0:T(4,128)} %fusion.134, f32[8]{0:T(128)S(1)} %compare_convert_fusion, bf16[8,256,256]{2,1,0:T(8,128)(2,1)S(1)} %gather_fusion.2, pred[8]{0:T(512)(128)(4,1)S(1)} %compare_and_fusion), kind=kOutput, calls=%fused_computation.22 | convolution fusion | flops 1082654720 | bytes 34603048 | tf_op jit(solution)/shard_map/qsac,qdc->qsad/dot_general | solution.py:33
  747.5 1.5 dynamic-slice_bitcast_fusion
  749.0 1.5 convert_bitcast_fusion.6
  750.5 338.5 %reduce-scatter.3.cloned.1.call-done = f32[128,256]{1,0:T(8,128)} async-done(((f32[8192,256]{1,0:T(8,128)}), f32[128,256]{1,0:T(8,128)}) %reduce-scatter.3.cloned.1.call-update) | async-done | bytes 131088 | tf_op jit(solution)/shard_map/reduce_scatter | solution.py:69
  1089.0 1.5 convert_bitcast_fusion.7
  (34 shorter events, 0.1 us)
Async XLA Ops:
  7.2 116.9 %all-gather.3.cloned.1.call-start = ((), (), s32[]{:S(2)}) async-start(), calls=%async_computation.4 | async-start | bytes 4259840 | tf_op jit(solution)/shard_map/all_gather | solution.py:63
  7.9 10.0 copy-start.4
  7.9 741.1 %reduce-scatter.5.cloned.1.call-start = ((), (), s32[]{:S(2)}) async-start(), calls=%async_computation.3 | async-start | bytes 8519680 | tf_op jit(solution)/shard_map/reduce_scatter | solution.py:73
  27.4 8.8 copy-start.12
  34.3 3.6 copy-start.9
  38.3 4.3 copy-start.10
  40.9 79.5 %collective-permute-start = (bf16[3,8,256,256]{3,1,2,0:T(8,128)(2,1)}, bf16[3,8,256,256]{3,1,2,0:T(8,128)(2,1)}, u32[]{:S(2)}, u32[]{:S(2)}) collective-permute-start(bf16[3,8,256,256]{3,1,2,0:T(8,128)(2,1)} %pad_maximum_fusion), channel_id=1, source_target_pairs={{0,64},{64,0},{1,65},{65,1},{2,66},{66,2},{3,67},{67,3},{4,68},{68... | collective-permute-start | bytes 9437192 | tf_op jit(solution)/shard_map/ppermute | solution.py:10
  44.0 3.1 copy-start.13
  124.0 6.2 copy-start
  124.0 6.2 copy-start.5
  133.7 3.5 copy-start.8
  137.2 1.3 copy-start.7
  138.5 1.3 copy-start.11
  149.2 14.6 %copy-start.6 = (bf16[8,256,256,1]{2,0,1,3:T(8,128)(2,1)S(1)}, bf16[8,256,256,1]{2,0,1,3:T(8,128)(2,1)}, u32[]{:S(2)}) copy-start(bf16[8,256,256,1]{2,0,1,3:T(8,128)(2,1)} %get-tuple-element.6) | copy-start | bytes 3145732
  202.3 886.7 %reduce-scatter.3.cloned.1.call-start = ((), (), s32[]{:S(2)}) async-start(), calls=%async_computation.2 | async-start | bytes 8519680 | tf_op jit(solution)/shard_map/reduce_scatter | solution.py:69
  235.4 8.6 copy-start.2
  698.7 10.7 copy-start.3
  709.4 7.1 copy-start.1
Sparse Core Ops, SparseCore 0:
  11.2 81.8 all-gather.2
  202.5 351.5 reduce-scatter.4
  747.6 341.3 reduce-scatter.2
where the time goes:
time: 1110 us; the launch traced here: 1100 us
  waiting for transfers between devices  410 us (37%)
  blocking collectives  384 us (35%)
  matrix products  218 us (20%)
  local copies, waits for them, and re-layouts  62.2 us (6%)
  between operations  14.2 us (1%)
    psum x1, blocking collectives, shards(): first_full = lax.psum(first_part, 'op').astype(jnp.bfloat16)  384 us
    reduce_scatter x1, waiting for transfers between devices, shards(): lax.psum_scatter(second_part, 'op', scatter_dimension=0, tiled=True)  338 us
    dot_general x9, matrix products, apply_local(): jnp.einsum('xy,qyac->qxac', mixers[term], lifted.astype(jnp.float32), pre...  86.7 us
    dot_general x9, matrix products, apply_local(): jnp.einsum('qsac,qdc->qsad', mixed, paired, preferred_element_type=jnp.fl...  71.4 us
    ppermute x1, waiting for transfers between devices, from_behind(): return lax.ppermute(value, axis, pairs)  70.7 us
    convert_element_type x6, local copies, waits for them, and re-layouts, apply_local(): lifted = jnp.einsum('qab,qsbc->qsac', lefts[term], blocks, preferred_elem...  44.9 us
    dot_general x9, matrix products, apply_local(): jnp.einsum('qab,qsbc->qsac', lefts[term], blocks, preferred_element_type=...  36.7 us
  transfers between devices with their start and end apart: 4, of which 2 were waited for; matrix products, arithmetic and copies ran while one was open for 19% of the time, Pallas kernels for 0%

commit v1 on v0

v1 whole, which is shorter than its diff:
```python
import jax
import jax.numpy as jnp
from jax import lax
from jax.experimental import pallas as pl
from jax.experimental.pallas import tpu as pltpu
from jax.sharding import PartitionSpec as P

NX, NY, NZ, NC = 4, 2, 4, 2
SECTORS = 8
LOCAL = 4
BLOCK = 256
CHUNK = 128
BF16 = jnp.bfloat16
F32 = jnp.float32


def device_at(x, y, z, c):
    return ((x * NY + y) * NZ + z) * NC + c


ALONG_X = [
    [device_at(x, y, z, c) for x in range(NX) for c in range(NC)]
    for y in range(NY)
    for z in range(NZ)
]
ALONG_Z = [
    [device_at(x, y, z, c) for z in range(NZ) for c in range(NC)]
    for x in range(NX)
    for y in range(NY)
]
HOLDERS = [
    [device_at(x, y, (half - x) % NZ, c) for x in range(NX) for y in range(NY)]
    for half in range(SECTORS // NC)
    for c in range(NC)
]
OWNERS = [[q * 8 + k for k in range(8)] for q in range(SECTORS)]
TO_HOLDERS = [(OWNERS[q][k], HOLDERS[q][k]) for q in range(SECTORS) for k in range(8)]
TO_OWNERS = [(HOLDERS[q][k], OWNERS[q][k]) for q in range(SECTORS) for k in range(8)]


def exchange(value, groups):
    return lax.all_to_all(value, "op", 0, 0, axis_index_groups=groups)


def pack_kernel(qx, px, qz, pz, lx, rx, lz, rz, out_x, out_z):
    out_x[0, 0:2] = lx[:, 0]
    out_x[0, 2:4] = rx[:, 0]
    out_z[0, 0:1] = lz[:, 0]
    out_z[0, 1:2] = rz[:, 0]


def pack(lefts, rights, qx, px, qz, pz):
    two = (2, 1, BLOCK, BLOCK)
    one = (1, 1, BLOCK, BLOCK)
    grid_spec = pltpu.PrefetchScalarGridSpec(
        num_scalar_prefetch=4,
        grid=(SECTORS,),
        in_specs=[
            pl.BlockSpec(two, lambda j, qx, px, qz, pz: (0, qx[j], 0, 0)),
            pl.BlockSpec(two, lambda j, qx, px, qz, pz: (0, px[j], 0, 0)),
            pl.BlockSpec(one, lambda j, qx, px, qz, pz: (2, qz[j], 0, 0)),
            pl.BlockSpec(one, lambda j, qx, px, qz, pz: (2, pz[j], 0, 0)),
        ],
        out_specs=[
            pl.BlockSpec((1, 4, BLOCK, BLOCK), lambda j, *_: (j, 0, 0, 0)),
            pl.BlockSpec((1, 2, BLOCK, BLOCK), lambda j, *_: (j, 0, 0, 0)),
        ],
    )
    return pl.pallas_call(
        pack_kernel,
        grid_spec=grid_spec,
        out_shape=[
            jax.ShapeDtypeStruct((SECTORS, 4, BLOCK, BLOCK), BF16),
            jax.ShapeDtypeStruct((SECTORS, 2, BLOCK, BLOCK), BF16),
        ],
        name="pack",
        cost_estimate=pl.CostEstimate(flops=0, bytes_accessed=12 << 20, transcendentals=0),
    )(qx, px, qz, pz, lefts, rights, lefts, rights)


def renew_kernel(slot_x, slot_z, left, tensor, out_x, out_z):
    lefts = left[:, 0].reshape(3 * BLOCK, BLOCK)
    total = [jnp.zeros((BLOCK, BLOCK), F32) for _ in range(3)]
    for s in range(LOCAL):
        site = tensor[0, s]
        lifted = jnp.dot(lefts, site, preferred_element_type=F32).astype(BF16)
        site_t = site.astype(F32).T.astype(BF16)
        for t in range(3):
            total[t] += jnp.dot(
                site_t, lifted[t * BLOCK : (t + 1) * BLOCK], preferred_element_type=F32
            )
    out_x[0, 0] = total[0].astype(BF16)
    out_x[0, 1] = total[1].astype(BF16)
    out_z[0, 0] = total[2].astype(BF16)


def renew(lefts, tensor, slot_x, slot_z):
    grid_spec = pltpu.PrefetchScalarGridSpec(
        num_scalar_prefetch=2,
        grid=(SECTORS,),
        in_specs=[
            pl.BlockSpec((3, 1, BLOCK, BLOCK), lambda q, *_: (0, q, 0, 0)),
            pl.BlockSpec((1, LOCAL, BLOCK, BLOCK), lambda q, *_: (q, 0, 0, 0)),
        ],
        out_specs=[
            pl.BlockSpec((1, 2, BLOCK, BLOCK), lambda q, sx, sz: (sx[q], 0, 0, 0)),
            pl.BlockSpec((1, 1, BLOCK, BLOCK), lambda q, sx, sz: (sz[q], 0, 0, 0)),
        ],
    )
    return pl.pallas_call(
        renew_kernel,
        grid_spec=grid_spec,
        out_shape=[
            jax.ShapeDtypeStruct((SECTORS, 2, BLOCK, BLOCK), BF16),
            jax.ShapeDtypeStruct((SECTORS, 1, BLOCK, BLOCK), BF16),
        ],
        name="renew",
        cost_estimate=pl.CostEstimate(
            flops=24 * 8 * 2 * BLOCK**3, bytes_accessed=10 << 20, transcendentals=0
        ),
    )(slot_x, slot_z, lefts, tensor)


def apply_kernel(mix, left_x, left_z, right_x, right_z, field, out, total):
    step = pl.program_id(0)

    @pl.when(step == 0)
    def _():
        total[...] = jnp.zeros_like(total)

    lefts = [left_x[0, 0], left_x[0, 1], left_z[0, 0]]
    rights = [right_x[0, 0], right_x[0, 1], right_z[0, 0]]
    for t in range(3):
        lifted = [
            jnp.dot(
                lefts[t], field[s * BLOCK : (s + 1) * BLOCK], preferred_element_type=F32
            )
            .astype(BF16)
            .astype(F32)
            for s in range(LOCAL)
        ]
        base = (step * 3 + t) * LOCAL * LOCAL
        for s in range(LOCAL):
            mixed = mix[base + s * LOCAL] * lifted[0]
            for s2 in range(1, LOCAL):
                mixed += mix[base + s * LOCAL + s2] * lifted[s2]
            rows = slice(s * BLOCK, (s + 1) * BLOCK)
            total[rows] += lax.dot_general(
                mixed.astype(BF16),
                rights[t],
                (((1,), (1,)), ((), ())),
                preferred_element_type=F32,
            )

    @pl.when(step == pl.num_programs(0) - 1)
    def _():
        out[...] = total[...].astype(BF16)


def apply_terms(mix, left_x, left_z, right_x, right_z, right_at, field):
    grid_spec = pltpu.PrefetchScalarGridSpec(
        num_scalar_prefetch=1,
        grid=(8,),
        in_specs=[
            pl.BlockSpec((1, 2, BLOCK, BLOCK), lambda j, *_: (j, 0, 0, 0)),
            pl.BlockSpec((1, 1, BLOCK, BLOCK), lambda j, *_: (j, 0, 0, 0)),
            pl.BlockSpec((1, 2, BLOCK, BLOCK), lambda j, *_: (j, right_at, 0, 0)),
            pl.BlockSpec((1, 1, BLOCK, BLOCK), lambda j, *_: (j, right_at, 0, 0)),
            pl.BlockSpec((LOCAL * BLOCK, BLOCK), lambda j, *_: (0, 0)),
        ],
        out_specs=pl.BlockSpec((LOCAL * BLOCK, BLOCK), lambda j, *_: (0, 0)),
        scratch_shapes=[pltpu.VMEM((LOCAL * BLOCK, BLOCK), F32)],
    )
    return pl.pallas_call(
        apply_kernel,
        grid_spec=grid_spec,
        out_shape=jax.ShapeDtypeStruct((LOCAL * BLOCK, BLOCK), BF16),
        name="apply_terms",
        cost_estimate=pl.CostEstimate(
            flops=24 * 8 * 2 * BLOCK**3, bytes_accessed=8 << 20, transcendentals=0
        ),
    )(mix, left_x, left_z, right_x, right_z, field)


def reduce_chunks(partial):
    parts = exchange(partial.reshape(8, CHUNK, BLOCK), HOLDERS)
    return jnp.sum(parts.astype(F32), axis=0).astype(BF16)


def shards(wave, left_ops, right_ops, site_ops, reach, pairing, site_tensor):
    lefts = left_ops[0]
    rights = right_ops[0]
    pair = pairing[0]
    me = lax.axis_index("op")
    x, y, z, c = me // 16, (me // 8) % 2, (me // 2) % 4, me % 2
    sector = ((x + z) % 4) * 2 + c
    slots = jnp.arange(SECTORS, dtype=jnp.int32)
    qx = ((slots // 2 + z) % 4) * 2 + slots % 2
    qz = ((slots // 2 + x) % 4) * 2 + slots % 2
    slot_x = ((pair // 2 - z) % 4) * 2 + pair % 2
    slot_z = ((pair // 2 - x) % 4) * 2 + pair % 2

    packed_x, packed_z = pack(lefts, rights, qx, pair[qx], qz, pair[qz])
    ops_x = exchange(packed_x, ALONG_X)
    ops_z = exchange(packed_z, ALONG_Z)

    mine = jnp.concatenate(
        [site_ops[0].reshape(3, LOCAL * LOCAL), reach[0].astype(F32)[:, None]], axis=1
    )
    table = lax.all_gather(mine, "op", axis=0)
    source_x = device_at(slots // 2, y, z, slots % 2)
    source_z = device_at(x, y, slots // 2, slots % 2)
    rows = jnp.concatenate([table[source_x, 0:2], table[source_z, 2:3]], axis=1)
    mix = rows[:, :, :16] * (sector.astype(F32) < rows[:, :, 16:]).astype(F32)
    mix = mix.reshape(-1)

    sector_rows = lax.all_gather(wave[0], "op", axis=0, tiled=True, axis_index_groups=OWNERS)
    field = lax.ppermute(sector_rows, "op", TO_HOLDERS)

    renewed_x, renewed_z = renew(lefts, site_tensor[0], slot_x, slot_z)
    renewed_x = lax.ppermute(renewed_x, "sect", [(0, 1), (1, 0)])
    renewed_z = lax.ppermute(renewed_z, "sect", [(0, 1), (1, 0)])

    first = reduce_chunks(apply_terms(mix, ops_x, ops_z, ops_x, ops_z, 1, field))
    first_own = lax.ppermute(first, "op", TO_OWNERS)
    first_field = exchange(jnp.broadcast_to(first[None], (8, CHUNK, BLOCK)), HOLDERS)
    first_field = first_field.reshape(LOCAL * BLOCK, BLOCK)
    second = reduce_chunks(apply_terms(mix, ops_x, ops_z, ops_x, ops_z, 1, first_field))
    second_own = lax.ppermute(second, "op", TO_OWNERS)

    moved_x = exchange(renewed_x, ALONG_X)
    moved_z = exchange(renewed_z, ALONG_Z)
    moved = reduce_chunks(apply_terms(mix, moved_x, moved_z, ops_x, ops_z, 1, field))
    moved_own = lax.ppermute(moved, "op", TO_OWNERS)
    return first_own[None], second_own[None], moved_own[None]


def solution(mesh):
    placed = (
        P("sect", "op", None),
        P("sect", "op", None, None, None),
        P("sect", "op", None, None, None),
        P("sect", "op", None, None),
        P("sect", "op"),
        P("sect", None),
        P("sect", None, None, None, None),
    )
    return jax.shard_map(
        shards,
        mesh=mesh,
        in_specs=placed,
        out_specs=(P("sect", "op", None), P("sect", "op", None), P("sect", "op", None)),
        check_vma=False,
    )
```

time: 1110 us -> 391 us (0.35)
  the two profiles are of different devices: /device:TPU:0 before, /device:TPU:120 now
where the time goes in v1:
time: 391 us; the launch traced here: 388 us
  blocking collectives  179 us (46%)
  starting transfers between devices  77.3 us (20%)
  Pallas kernels  70.9 us (18%)
  waiting for transfers between devices  48.7 us (12%)
  local copies, waits for them, and re-layouts  9.29 us (2%)
    all_gather x1, blocking collectives, shards(): table = lax.all_gather(mine, 'op', axis=0)  135 us
    all_to_all x7, starting transfers between devices, exchange(): return lax.all_to_all(value, 'op', 0, 0, axis_index_groups=groups)  54.8 us
    pallas_call x3, Pallas kernels, apply_terms(): pl.pallas_call(apply_kernel, grid_spec=grid_spec, out_shape=jax.ShapeDtyp...  47.8 us
    all_to_all x7, waiting for transfers between devices, exchange(): return lax.all_to_all(value, 'op', 0, 0, axis_index_groups=groups)  39 us
    all_to_all x1, blocking collectives, exchange(): return lax.all_to_all(value, 'op', 0, 0, axis_index_groups=groups)  30 us
    pallas_call x1, Pallas kernels, renew(): pl.pallas_call(renew_kernel, grid_spec=grid_spec, out_shape=[jax.ShapeDty...  14.6 us
    all_gather x1, blocking collectives, shards(): lax.all_gather(wave[0], 'op', axis=0, tiled=True, axis_index_groups=OWNERS)  13.1 us
    pallas_call x1, Pallas kernels, pack(): pl.pallas_call(pack_kernel, grid_spec=grid_spec, out_shape=[jax.ShapeDtyp...  8.49 us
  transfers between devices with their start and end apart: 13, of which 4 were waited for; matrix products, arithmetic and copies ran while one was open for 1% of the time, Pallas kernels for 16%

profile of v1, /device:TPU:120, one launch (start us, length us, event | category | flops | bytes accessed | tf_op | source)
XLA Modules:
  0.0 388.4 jit_solution(7946003451328699107)
XLA Ops:
  0.7 0.5 fusion.2.qx
  1.2 1.2 fusion.12
  2.4 1.8 gather_fusion.2
  4.2 1.9 gather_fusion.3
  6.1 8.5 %pack.1 = (bf16[8,4,256,256]{3,2,1,0:T(8,128)(2,1)}, bf16[8,2,256,256]{3,2,1,0:T(8,128)(2,1)}) custom-call(s32[8]{0:T(128)} %fusion.2.qx, s32[8]{0:T(128)} %gather_fusion.2, s32[8]{0:T(128)} %get-tuple-element.14.qz, s32[8]{0:T(128)} %gather_fusion.3, bf16[3,8,256,256]{3,2,1,0:T(8,128)(2,1)} %bitcast.33, bf16[3,8,256,256]{3,2,1,0:T(8,128)(2,1)} %bitcast.31, ...), custom_call_target="tpu_custom_call" | custom-call | bytes 12582912 | tf_op jit(solution)/shard_map/pack/pallas_call | solution.py:69
  14.6 30.0 %all_to_all.40.left_z.right_z = bf16[8,2,256,256]{3,2,1,0:T(8,128)(2,1)} all-to-all(bf16[8,2,256,256]{3,2,1,0:T(8,128)(2,1)} %get-tuple-element.8), channel_id=1, replica_groups={{0,1,2,3,4,5,6,7},{8,9,10,11,12,13,14,15},{16,17,18,19,20,21,22,23},{24..., dimensions={0} | all-to-all | bytes 4194304 | tf_op jit(solution)/shard_map/all_to_all | solution.py:42
  44.6 4.6 %all-to-all-start = ((bf16[8,4,256,256]{3,2,1,0:T(8,128)(2,1)}), bf16[8,4,256,256]{3,2,1,0:T(8,128)(2,1)}, u32[]{:S(2)}, u32[]{:S(2)}) async-start(bf16[8,4,256,256]{3,2,1,0:T(8,128)(2,1)} %get-tuple-element.7), calls=%async_computation | async-start | bytes 8388608 | tf_op jit(solution)/shard_map/all_to_all | solution.py:42
  49.2 0.5 fusion.10.slot_x
  49.7 0.0 copy-start.3
  49.7 0.0 copy-start.6
  49.7 0.0 copy-start.4
  49.7 14.6 %renew.1 = (bf16[8,2,256,256]{3,2,1,0:T(8,128)(2,1)}, bf16[8,1,256,256]{3,2,1,0:T(8,128)(2,1)}) custom-call(s32[8]{0:T(128)} %fusion.10.slot_x, s32[8]{0:T(128)} %get-tuple-element.11.slot_z, bf16[3,8,256,256]{3,2,1,0:T(8,128)(2,1)} %bitcast.35, bf16[8,4,256,256]{3,2,1,0:T(8,128)(2,1)} %bitcast.46), custom_call_target="tpu_custom_call" | custom-call | flops 6442450944 | bytes 10485760 | tf_op jit(solution)/shard_map/renew/pallas_call | solution.py:110
  64.3 0.8 collective-permute-start.4
  65.1 1.2 collective-permute-start.3
  66.4 0.0 copy-done.3
  66.4 13.1 %all-gather.1 = bf16[1,1024,256]{2,1,0:T(8,128)(2,1)S(1)} all-gather(bf16[1,128,256]{2,1,0:T(8,128)(2,1)S(1)} %copy-done.3), channel_id=3, replica_groups={{0,1,2,3,4,5,6,7},{8,9,10,11,12,13,14,15},{16,17,18,19,20,21,22,23},{24..., dimensions={1}, use_global_device_ids=true | all-gather | bytes 589824 | tf_op jit(solution)/shard_map/all_gather | solution.py:217
  79.5 6.5 %collective-permute-start = (bf16[1024,256]{1,0:T(8,128)(2,1)S(1)}, bf16[1024,256]{1,0:T(8,128)(2,1)S(1)}, u32[]{:S(2)}, u32[]{:S(2)}) collective-permute-start(bf16[1024,256]{1,0:T(8,128)(2,1)S(1)} %bitcast.36), channel_id=1, source_target_pairs={{0,0},{1,8},{2,22},{3,30},{4,36},{5,44},{6,50},{7,58},{8,1},{9,9},... | collective-permute-start | bytes 1572872 | tf_op jit(solution)/shard_map/ppermute | solution.py:218
  86.1 0.0 copy-done.6
  86.1 0.1 copy.15
  86.2 0.0 copy-done.4
  86.2 0.1 reshape_squeeze.3
  86.3 0.1 maximum_bitcast_fusion
  86.3 135.4 %all-gather.2 = f32[64,3,17]{2,1,0:T(4,128)S(1)} all-gather(f32[1,3,17]{2,1,0:T(4,128)S(1)} %maximum_bitcast_fusion), channel_id=2, replica_groups=mesh['sect'=2,'op'=64] {'op'}, dimensions={0}, use_global_device_ids=true | all-gather | bytes 13260 | tf_op jit(solution)/shard_map/all_gather | solution.py:210
  221.8 0.6 gather_fusion
  222.4 0.0 collective-permute-done.4
  222.4 0.0 all-to-all-done.left_x.right_x
  222.4 9.4 %all-to-all-start.6 = ((bf16[8,1,256,256]{3,2,1,0:T(8,128)(2,1)}), bf16[8,1,256,256]{3,2,1,0:T(8,128)(2,1)S(1)}, u32[]{:S(2)}, u32[]{:S(2)}) async-start(bf16[8,1,256,256]{3,2,1,0:T(8,128)(2,1)} %collective-permute-done.4), calls=%async_computation.6 | async-start | bytes 2097152 | tf_op jit(solution)/shard_map/all_to_all | solution.py:42
  231.8 0.6 gather_fusion.1
  232.4 0.2 convert_reduce_fusion
  232.6 0.1 maximum_multiply_fusion
  232.7 0.7 reshape.232.mix
  233.3 0.0 collective-permute-done.field
  233.3 0.8 copy-done.5
  234.2 15.9 %apply_terms.3 = bf16[1024,256]{1,0:T(8,128)(2,1)} custom-call(f32[384]{0:T(512)} %reshape.232.mix, bf16[8,4,256,256]{3,2,1,0:T(8,128)(2,1)} %all-to-all-done.left_x.right_x, bf16[8,2,256,256]{3,2,1,0:T(8,128)(2,1)} %all_to_all.40.left_z.right_z, bf16[8,4,256,256]{3,2,1,0:T(8,128)(2,1)} %all-to-all-done.left_x.right_x, ...), custom_call_target="tpu_custom_call" | custom-call | flops 6442450944 | bytes 8388608 | tf_op jit(solution)/shard_map/apply_terms/pallas_call | solution.py:174
  250.1 0.0 all-to-all-done.6.left_z
  250.1 12.4 %all-to-all-start.2 = ((bf16[8,128,256]{2,1,0:T(8,128)(2,1)}), bf16[8,128,256]{2,1,0:T(8,128)(2,1)S(1)}, u32[]{:S(2)}, u32[]{:S(2)}) async-start(bf16[8,128,256]{2,1,0:T(8,128)(2,1)} %bitcast.40), calls=%async_computation.2 | async-start | bytes 1048576 | tf_op jit(solution)/shard_map/all_to_all | solution.py:42
  262.5 0.0 collective-permute-done.3
  262.5 11.9 %all-to-all-done.2 = bf16[8,128,256]{2,1,0:T(8,128)(2,1)S(1)} async-done(((bf16[8,128,256]{2,1,0:T(8,128)(2,1)}), bf16[8,128,256]{2,1,0:T(8,128)(2,1)S(1)}, u32[]{:S(2)}, u32[]{:S(2)}) %all-to-all-start.2) | async-done | bytes 524320 | tf_op jit(solution)/shard_map/all_to_all | solution.py:42
  274.4 0.0 copy-done.1
  274.4 3.6 all-to-all-start.5
  278.0 0.1 reduce_sum.36
  278.1 27.0 %all-to-all-done.5.left_x = bf16[8,2,256,256]{3,2,1,0:T(8,128)(2,1)S(1)} async-done(((bf16[8,2,256,256]{3,2,1,0:T(8,128)(2,1)}), bf16[8,2,256,256]{3,2,1,0:T(8,128)(2,1)S(1)}, u32[]{:S(2)}, u32[]{:S(2)}) %all-to-all-start.5) | async-done | bytes 2097184 | tf_op jit(solution)/shard_map/all_to_all | solution.py:42
  305.2 0.9 broadcast_in_dim.9
  306.0 5.6 %all-to-all-start.3 = ((bf16[8,128,256]{2,1,0:T(8,128)(2,1)}), bf16[8,128,256]{2,1,0:T(8,128)(2,1)S(1)}, u32[]{:S(2)}, u32[]{:S(2)}) async-start(bf16[8,128,256]{2,1,0:T(8,128)(2,1)} %broadcast_in_dim.9), calls=%async_computation.3 | async-start | bytes 1048576 | tf_op jit(solution)/shard_map/all_to_all | solution.py:42
  311.6 0.0 copy-done
  311.6 16.0 %apply_terms.5 = bf16[1024,256]{1,0:T(8,128)(2,1)} custom-call(f32[384]{0:T(512)} %reshape.232.mix, bf16[8,2,256,256]{3,2,1,0:T(8,128)(2,1)} %copy-done, bf16[8,1,256,256]{3,2,1,0:T(8,128)(2,1)} %copy-done.1, bf16[8,4,256,256]{3,2,1,0:T(8,128)(2,1)} %all-to-all-done.left_x.right_x, bf16[8,2,256,256]{3,2,1,0:T(8,128)(2,1)} %all_to_all.40.left_z.right_z, ...), custom_call_target="tpu_custom_call" | custom-call | flops 6442450944 | bytes 8388608 | tf_op jit(solution)/shard_map/apply_terms/pallas_call | solution.py:174
  327.6 0.0 all-to-all-done.3
  327.6 9.6 %all-to-all-start.7 = ((bf16[8,128,256]{2,1,0:T(8,128)(2,1)}), bf16[8,128,256]{2,1,0:T(8,128)(2,1)S(1)}, u32[]{:S(2)}, u32[]{:S(2)}) async-start(bf16[8,128,256]{2,1,0:T(8,128)(2,1)} %bitcast.39), calls=%async_computation.7 | async-start | bytes 1048576 | tf_op jit(solution)/shard_map/all_to_all | solution.py:42
  337.3 0.0 copy-done.2
  337.3 15.9 %apply_terms.4 = bf16[1024,256]{1,0:T(8,128)(2,1)} custom-call(f32[384]{0:T(512)} %reshape.232.mix, bf16[8,4,256,256]{3,2,1,0:T(8,128)(2,1)} %all-to-all-done.left_x.right_x, bf16[8,2,256,256]{3,2,1,0:T(8,128)(2,1)} %all_to_all.40.left_z.right_z, bf16[8,4,256,256]{3,2,1,0:T(8,128)(2,1)} %all-to-all-done.left_x.right_x, ...), custom_call_target="tpu_custom_call" | custom-call | flops 6442450944 | bytes 8388608 | tf_op jit(solution)/shard_map/apply_terms/pallas_call | solution.py:174
  353.1 0.0 all-to-all-done.7
  353.1 9.6 %all-to-all-start.4 = ((bf16[8,128,256]{2,1,0:T(8,128)(2,1)}), bf16[8,128,256]{2,1,0:T(8,128)(2,1)S(1)}, u32[]{:S(2)}, u32[]{:S(2)}) async-start(bf16[8,128,256]{2,1,0:T(8,128)(2,1)} %bitcast.37), calls=%async_computation.4 | async-start | bytes 1048576 | tf_op jit(solution)/shard_map/all_to_all | solution.py:42
  362.7 4.5 %collective-permute-start.1 = (bf16[128,256]{1,0:T(8,128)(2,1)S(1)}, bf16[128,256]{1,0:T(8,128)(2,1)S(1)}, u32[]{:S(2)}, u32[]{:S(2)}) collective-permute-start(bf16[128,256]{1,0:T(8,128)(2,1)S(1)} %reduce_sum.36), channel_id=1, source_target_pairs={{0,0},{8,1},{22,2},{30,3},{36,4},{44,5},{50,6},{58,7},{1,8},{9,9},... | collective-permute-start | bytes 196616 | tf_op jit(solution)/shard_map/ppermute | solution.py:225
  367.3 0.1 reduce_sum.38
  367.4 7.4 %collective-permute-start.5 = (bf16[128,256]{1,0:T(8,128)(2,1)S(1)}, bf16[128,256]{1,0:T(8,128)(2,1)S(1)}, u32[]{:S(2)}, u32[]{:S(2)}) collective-permute-start(bf16[128,256]{1,0:T(8,128)(2,1)S(1)} %reduce_sum.38), channel_id=1, source_target_pairs={{0,0},{8,1},{22,2},{30,3},{36,4},{44,5},{50,6},{58,7},{1,8},{9,9},... | collective-permute-start | bytes 196616 | tf_op jit(solution)/shard_map/ppermute | solution.py:234
  374.8 0.0 all-to-all-done.4
  374.8 0.1 reduce_sum.37
  374.9 1.9 collective-permute-start.2
  376.8 0.0 collective-permute-done.1
  376.8 2.5 collective-permute-done.5
  379.3 7.2 %collective-permute-done.2 = bf16[128,256]{1,0:T(8,128)(2,1)S(1)} collective-permute-done((bf16[128,256]{1,0:T(8,128)(2,1)S(1)}, bf16[128,256]{1,0:T(8,128)(2,1)S(1)}, u32[]{:S(2)}, u32[]{:S(2)}) %collective-permute-start.2) | collective-permute-done | bytes 65568 | tf_op jit(solution)/shard_map/ppermute | solution.py:229
  386.5 0.6 copy.22
  387.1 0.6 copy.23
  387.8 0.6 copy.24
  (13 shorter events, 0.1 us)
Async XLA Ops:
  44.6 177.8 %all-to-all-start = ((bf16[8,4,256,256]{3,2,1,0:T(8,128)(2,1)}), bf16[8,4,256,256]{3,2,1,0:T(8,128)(2,1)}, u32[]{:S(2)}, u32[]{:S(2)}) async-start(bf16[8,4,256,256]{3,2,1,0:T(8,128)(2,1)} %get-tuple-element.7), calls=%async_computation | async-start | bytes 8388608 | tf_op jit(solution)/shard_map/all_to_all | solution.py:42
  49.7 16.7 %copy-start.3 = (bf16[1,128,256]{2,1,0:T(8,128)(2,1)S(1)}, bf16[1,128,256]{2,1,0:T(8,128)(2,1)}, u32[]{:S(2)}) copy-start(bf16[1,128,256]{2,1,0:T(8,128)(2,1)} %param.7) | copy-start | bytes 196612
  49.7 36.4 %copy-start.6 = (s32[1,3]{1,0:T(1,128)S(1)}, s32[1,3]{1,0:T(1,128)}, u32[]{:S(2)}) copy-start(s32[1,3]{1,0:T(1,128)} %param.11) | copy-start | bytes 40
  49.7 36.5 %copy-start.4 = (f32[1,3,4,4]{3,2,1,0:T(4,128)S(1)}, f32[1,3,4,4]{3,2,1,0:T(4,128)}, u32[]{:S(2)}) copy-start(f32[1,3,4,4]{3,2,1,0:T(4,128)} %param.10) | copy-start | bytes 580
  64.3 158.0 %collective-permute-start.4 = (bf16[8,1,256,256]{3,2,1,0:T(8,128)(2,1)}, bf16[8,1,256,256]{3,2,1,0:T(8,128)(2,1)}, u32[]{:S(2)}, u32[]{:S(2)}) collective-permute-start(bf16[8,1,256,256]{3,2,1,0:T(8,128)(2,1)} %get-tuple-element.10), channel_id=1, source_target_pairs={{0,64},{64,0},{1,65},{65,1},{2,66},{66,2},{3,67},{67,3},{4,68},{68... | collective-permute-start | bytes 3145736 | tf_op jit(solution)/shard_map/ppermute | solution.py:222
  65.1 197.3 %collective-permute-start.3 = (bf16[8,2,256,256]{3,2,1,0:T(8,128)(2,1)}, bf16[8,2,256,256]{3,2,1,0:T(8,128)(2,1)}, u32[]{:S(2)}, u32[]{:S(2)}) collective-permute-start(bf16[8,2,256,256]{3,2,1,0:T(8,128)(2,1)} %get-tuple-element.9), channel_id=1, source_target_pairs={{0,64},{64,0},{1,65},{65,1},{2,66},{66,2},{3,67},{67,3},{4,68},{68... | collective-permute-start | bytes 6291464 | tf_op jit(solution)/shard_map/ppermute | solution.py:221
  79.5 153.9 %collective-permute-start = (bf16[1024,256]{1,0:T(8,128)(2,1)S(1)}, bf16[1024,256]{1,0:T(8,128)(2,1)S(1)}, u32[]{:S(2)}, u32[]{:S(2)}) collective-permute-start(bf16[1024,256]{1,0:T(8,128)(2,1)S(1)} %bitcast.36), channel_id=1, source_target_pairs={{0,0},{1,8},{2,22},{3,30},{4,36},{5,44},{6,50},{7,58},{8,1},{9,9},... | collective-permute-start | bytes 1572872 | tf_op jit(solution)/shard_map/ppermute | solution.py:218
  222.4 27.7 %all-to-all-start.6 = ((bf16[8,1,256,256]{3,2,1,0:T(8,128)(2,1)}), bf16[8,1,256,256]{3,2,1,0:T(8,128)(2,1)S(1)}, u32[]{:S(2)}, u32[]{:S(2)}) async-start(bf16[8,1,256,256]{3,2,1,0:T(8,128)(2,1)} %collective-permute-done.4), calls=%async_computation.6 | async-start | bytes 2097152 | tf_op jit(solution)/shard_map/all_to_all | solution.py:42
  233.3 0.8 copy-start.5
  250.1 24.4 %copy-start.1 = (bf16[8,1,256,256]{3,2,1,0:T(8,128)(2,1)}, bf16[8,1,256,256]{3,2,1,0:T(8,128)(2,1)S(1)}, u32[]{:S(2)}) copy-start(bf16[8,1,256,256]{3,2,1,0:T(8,128)(2,1)S(1)} %all-to-all-done.6.left_z) | copy-start | bytes 3145732
  250.1 24.3 %all-to-all-start.2 = ((bf16[8,128,256]{2,1,0:T(8,128)(2,1)}), bf16[8,128,256]{2,1,0:T(8,128)(2,1)S(1)}, u32[]{:S(2)}, u32[]{:S(2)}) async-start(bf16[8,128,256]{2,1,0:T(8,128)(2,1)} %bitcast.40), calls=%async_computation.2 | async-start | bytes 1048576 | tf_op jit(solution)/shard_map/all_to_all | solution.py:42
  274.4 30.7 %all-to-all-start.5 = ((bf16[8,2,256,256]{3,2,1,0:T(8,128)(2,1)}), bf16[8,2,256,256]{3,2,1,0:T(8,128)(2,1)S(1)}, u32[]{:S(2)}, u32[]{:S(2)}) async-start(bf16[8,2,256,256]{3,2,1,0:T(8,128)(2,1)} %collective-permute-done.3), calls=%async_computation.5 | async-start | bytes 4194304 | tf_op jit(solution)/shard_map/all_to_all | solution.py:42
  305.1 6.5 %copy-start = (bf16[8,2,256,256]{3,2,1,0:T(8,128)(2,1)}, bf16[8,2,256,256]{3,2,1,0:T(8,128)(2,1)S(1)}, u32[]{:S(2)}) copy-start(bf16[8,2,256,256]{3,2,1,0:T(8,128)(2,1)S(1)} %all-to-all-done.5.left_x) | copy-start | bytes 6291460
  306.0 21.6 %all-to-all-start.3 = ((bf16[8,128,256]{2,1,0:T(8,128)(2,1)}), bf16[8,128,256]{2,1,0:T(8,128)(2,1)S(1)}, u32[]{:S(2)}, u32[]{:S(2)}) async-start(bf16[8,128,256]{2,1,0:T(8,128)(2,1)} %broadcast_in_dim.9), calls=%async_computation.3 | async-start | bytes 1048576 | tf_op jit(solution)/shard_map/all_to_all | solution.py:42
  327.6 9.7 %copy-start.2 = (bf16[8,128,256]{2,1,0:T(8,128)(2,1)}, bf16[8,128,256]{2,1,0:T(8,128)(2,1)S(1)}, u32[]{:S(2)}) copy-start(bf16[8,128,256]{2,1,0:T(8,128)(2,1)S(1)} %all-to-all-done.3) | copy-start | bytes 1572868
  327.6 25.5 %all-to-all-start.7 = ((bf16[8,128,256]{2,1,0:T(8,128)(2,1)}), bf16[8,128,256]{2,1,0:T(8,128)(2,1)S(1)}, u32[]{:S(2)}, u32[]{:S(2)}) async-start(bf16[8,128,256]{2,1,0:T(8,128)(2,1)} %bitcast.39), calls=%async_computation.7 | async-start | bytes 1048576 | tf_op jit(solution)/shard_map/all_to_all | solution.py:42
  353.1 21.7 %all-to-all-start.4 = ((bf16[8,128,256]{2,1,0:T(8,128)(2,1)}), bf16[8,128,256]{2,1,0:T(8,128)(2,1)S(1)}, u32[]{:S(2)}, u32[]{:S(2)}) async-start(bf16[8,128,256]{2,1,0:T(8,128)(2,1)} %bitcast.37), calls=%async_computation.4 | async-start | bytes 1048576 | tf_op jit(solution)/shard_map/all_to_all | solution.py:42
  362.7 14.1 %collective-permute-start.1 = (bf16[128,256]{1,0:T(8,128)(2,1)S(1)}, bf16[128,256]{1,0:T(8,128)(2,1)S(1)}, u32[]{:S(2)}, u32[]{:S(2)}) collective-permute-start(bf16[128,256]{1,0:T(8,128)(2,1)S(1)} %reduce_sum.36), channel_id=1, source_target_pairs={{0,0},{8,1},{22,2},{30,3},{36,4},{44,5},{50,6},{58,7},{1,8},{9,9},... | collective-permute-start | bytes 196616 | tf_op jit(solution)/shard_map/ppermute | solution.py:225
  367.4 12.0 %collective-permute-start.5 = (bf16[128,256]{1,0:T(8,128)(2,1)S(1)}, bf16[128,256]{1,0:T(8,128)(2,1)S(1)}, u32[]{:S(2)}, u32[]{:S(2)}) collective-permute-start(bf16[128,256]{1,0:T(8,128)(2,1)S(1)} %reduce_sum.38), channel_id=1, source_target_pairs={{0,0},{8,1},{22,2},{30,3},{36,4},{44,5},{50,6},{58,7},{1,8},{9,9},... | collective-permute-start | bytes 196616 | tf_op jit(solution)/shard_map/ppermute | solution.py:234
  374.9 11.6 %collective-permute-start.2 = (bf16[128,256]{1,0:T(8,128)(2,1)S(1)}, bf16[128,256]{1,0:T(8,128)(2,1)S(1)}, u32[]{:S(2)}, u32[]{:S(2)}) collective-permute-start(bf16[128,256]{1,0:T(8,128)(2,1)S(1)} %reduce_sum.37), channel_id=1, source_target_pairs={{0,0},{8,1},{22,2},{30,3},{36,4},{44,5},{50,6},{58,7},{1,8},{9,9},... | collective-permute-start | bytes 196616 | tf_op jit(solution)/shard_map/ppermute | solution.py:229

commit v2 on v0

v2 whole, which is shorter than its diff:
```python
import functools

import jax
import jax.numpy as jnp
from jax import lax
from jax.experimental import pallas as pl
from jax.experimental.pallas import tpu as pltpu
from jax.sharding import PartitionSpec as P

NX, NY, NZ, NC = 4, 2, 4, 2
DEVICES = NX * NY * NZ * NC
SECTORS = 8
LOCAL = 4
BLOCK = 256
CHUNK = 128
TERMS = 3
STACK = TERMS * BLOCK
MIX_ROWS = 16
ROWS = 2 * STACK + MIX_ROWS
BF16 = jnp.bfloat16
F32 = jnp.float32
ANY = pl.BlockSpec(memory_space=pl.ANY)
SMEM = pl.BlockSpec(memory_space=pltpu.SMEM)
VMEM = pl.BlockSpec(memory_space=pltpu.VMEM)


def device_at(x, y, z, c):
    return (((x % NX) * NY + y) * NZ + z % NZ) * NC + c


PLACES = [
    (x, y, z, c) for x in range(NX) for y in range(NY) for z in range(NZ) for c in range(NC)
]
HOLDERS = [
    [device_at(x, y, half - x, c) for x in range(NX) for y in range(NY)]
    for half in range(SECTORS // NC)
    for c in range(NC)
]
OWNERS = [[q * 8 + k for k in range(8)] for q in range(SECTORS)]
TO_HOLDERS = [(OWNERS[q][k], HOLDERS[q][k]) for q in range(SECTORS) for k in range(8)]
TO_OWNERS = [(HOLDERS[q][k], OWNERS[q][k]) for q in range(SECTORS) for k in range(8)]
LINES = [[device_at(x, y, z, 0) for x in range(NX)] for y in range(NY) for z in range(NZ)]
LINES += [[device_at(x, y, z, 1) for z in range(NZ)] for x in range(NX) for y in range(NY)]


def along(d, flip):
    return [
        (
            device_at(x, y, z, c),
            device_at(x + d * (1 - c), y, z + d * c, c ^ flip),
        )
        for x, y, z, c in PLACES
    ]


def exchange(value, groups):
    return lax.all_to_all(value, "op", 0, 0, axis_index_groups=groups)


def mixer_rows(row, held, sector):
    value = jnp.where(sector < held, row, 0.0)
    high = value.astype(BF16).astype(F32)
    middle = (value - high).astype(BF16).astype(F32)
    low = value - high - middle
    at = lax.broadcasted_iota(jnp.int32, (MIX_ROWS, BLOCK), 0)
    parts = jnp.where(at == 0, high, jnp.where(at == 1, middle, jnp.where(at == 2, low, 0.0)))
    return parts.astype(BF16)


def pack_kernel(place, pair, site, reach, left, right, *refs):
    outs = refs[:5]
    left_buf, right_buf, mix_buf, load_sems, sems = refs[5:]
    x, z, c = place[0], place[1], place[2]
    loads = []
    for t in range(TERMS):
        loads.append(pltpu.make_async_copy(left.at[0, t], left_buf.at[t], load_sems.at[t, 0]))
        loads.append(pltpu.make_async_copy(right.at[0, t], right_buf.at[t], load_sems.at[t, 1]))
    for copy in loads:
        copy.start()
    lane = lax.broadcasted_iota(jnp.int32, (1, BLOCK), 1)
    row = jnp.zeros((1, BLOCK), F32)
    held = jnp.zeros((1, BLOCK), jnp.int32)
    for t in range(TERMS):
        held = jnp.where(lane // 16 == t, reach[t], held)
        for e in range(LOCAL * LOCAL):
            row = jnp.where(lane == t * 16 + e, site[t * 16 + e], row)
    sectors = [lax.rem(i + jnp.where(c == 0, z, x), 4) * 2 + c for i in range(4)]
    sectors += [lax.rem(x + z + d, 4) * 2 + 1 - c for d in range(4)]
    places = [outs[0].at[i] for i in range(4)] + list(outs[1:])
    stores = []

    def store(src, dst):
        stores.append(pltpu.make_async_copy(src, dst, sems.at[len(stores)]))
        stores[-1].start()

    for i, q in enumerate(sectors):
        mix_buf[i] = mixer_rows(row, held, q)
    for i in range(8):
        store(mix_buf.at[i], places[i].at[2 * STACK : ROWS])
    for copy in loads:
        copy.wait()
    for i, q in enumerate(sectors):
        for t in range(TERMS):
            store(left_buf.at[t, q], places[i].at[t * BLOCK : (t + 1) * BLOCK])
            store(right_buf.at[t, pair[q]], places[i].at[STACK + t * BLOCK : STACK + (t + 1) * BLOCK])
    for copy in stores:
        copy.wait()


def pack(place, pair, site, reach, left_ops, right_ops):
    return pl.pallas_call(
        pack_kernel,
        in_specs=[SMEM, SMEM, SMEM, SMEM, ANY, ANY],
        out_specs=[ANY] * 5,
        out_shape=[jax.ShapeDtypeStruct((4, ROWS, BLOCK), BF16)]
        + [jax.ShapeDtypeStruct((ROWS, BLOCK), BF16)] * 4,
        scratch_shapes=[
            pltpu.VMEM((TERMS, SECTORS, BLOCK, BLOCK), BF16),
            pltpu.VMEM((TERMS, SECTORS, BLOCK, BLOCK), BF16),
            pltpu.VMEM((8, MIX_ROWS, BLOCK), BF16),
            pltpu.SemaphoreType.DMA((TERMS, 2)),
            pltpu.SemaphoreType.DMA((56,)),
        ],
        compiler_params=pltpu.CompilerParams(vmem_limit_bytes=56 << 20),
        name="pack",
        cost_estimate=pl.CostEstimate(flops=1 << 20, bytes_accessed=1 << 16, transcendentals=0),
    )(place, pair, site, reach, left_ops, right_ops)


def renew_kernel(place, pair, left, tensor, out):
    lefts = left[0, :, 0].reshape(STACK, BLOCK)
    lifted = []
    sites = []
    for s in range(LOCAL):
        site = tensor[0, 0, s]
        lifted.append(jnp.dot(lefts, site, preferred_element_type=F32).astype(BF16))
        sites.append(site.T)
    sites = jnp.concatenate(sites, axis=1)
    for t in range(TERMS):
        stacked = jnp.concatenate([lifted[s][t * BLOCK : (t + 1) * BLOCK] for s in range(LOCAL)])
        out[0, t] = jnp.dot(sites, stacked, preferred_element_type=F32).astype(BF16)


def renew(kept, place, pair, left_ops, tensor):
    def left_sector(i, place, pair):
        x, z, c = place[0], place[1], place[2]
        wanted = lax.rem(x + z + i, 4) * 2 + (c if kept else 1 - c)
        q = jnp.int32(0)
        for k in range(1, SECTORS):
            q = jnp.where(pair[k] == wanted, k, q)
        return q

    grid_spec = pltpu.PrefetchScalarGridSpec(
        num_scalar_prefetch=2,
        grid=(4,),
        in_specs=[
            pl.BlockSpec((1, TERMS, 1, BLOCK, BLOCK), lambda d, *s: (0, 0, left_sector(d, *s), 0, 0)),
            pl.BlockSpec((1, 1, LOCAL, BLOCK, BLOCK), lambda d, *s: (0, left_sector(d, *s), 0, 0, 0)),
        ],
        out_specs=pl.BlockSpec((1, TERMS, BLOCK, BLOCK), lambda d, *s: (d, 0, 0, 0)),
    )
    return pl.pallas_call(
        renew_kernel,
        grid_spec=grid_spec,
        out_shape=jax.ShapeDtypeStruct((4, TERMS, BLOCK, BLOCK), BF16),
        name="renew_kept" if kept else "renew_swapped",
        cost_estimate=pl.CostEstimate(
            flops=12 * 8 * 2 * BLOCK**3, bytes_accessed=20 << 20, transcendentals=0
        ),
    )(place, pair, left_ops, tensor)


def apply_kernel(groups, renewed, starts, place, field, *refs):
    out, left_buf, right_buf, mix_buf, total, sems = refs[-6:]
    start = refs[-7] if starts else None

    here = jnp.where(place[2] == 0, place[0], place[1])

    def view(at):
        ref, slot = at
        if slot is None:
            return refs[ref]
        if isinstance(slot, tuple):
            slot = lax.rem(here + 4 - slot[0], 4)
        return refs[ref].at[slot]

    def copies(i, g):
        ops = view(groups[i])
        parts = (
            (view(renewed[i]) if renewed else ops.at[0:STACK], left_buf.at[g]),
            (ops.at[STACK : 2 * STACK], right_buf.at[g]),
            (ops.at[2 * STACK : ROWS], mix_buf.at[g]),
        )
        return [pltpu.make_async_copy(a, b, sems.at[g, k]) for k, (a, b) in enumerate(parts)]

    for i in range(len(groups)):
        for copy in copies(i, i):
            copy.start()
    total[...] = start[...] if starts else jnp.zeros_like(total)

    def body(g, carry):
        for copy in copies(0, g):
            copy.wait()
        left = left_buf[g]
        lifted = [
            jnp.dot(left, field[s * BLOCK : (s + 1) * BLOCK], preferred_element_type=F32)
            for s in range(LOCAL)
        ]
        parts = mix_buf[g].astype(F32)
        mix = parts[0:1] + parts[1:2] + parts[2:3]
        columns = [[] for _ in range(LOCAL)]
        for t in range(TERMS):
            rows = slice(t * BLOCK, (t + 1) * BLOCK)
            for s in range(LOCAL):
                mixed = None
                for s2 in range(LOCAL):
                    at = t * 16 + s * LOCAL + s2
                    term = mix[:, at : at + 1] * lifted[s2][rows]
                    mixed = term if mixed is None else mixed + term
                columns[s].append(mixed.astype(BF16))
        right = jnp.concatenate(
            [right_buf[g, t * BLOCK : (t + 1) * BLOCK] for t in range(TERMS)], axis=1
        )
        for s in range(LOCAL):
            total[s * BLOCK : (s + 1) * BLOCK] += lax.dot_general(
                jnp.concatenate(columns[s], axis=1),
                right,
                (((1,), (1,)), ((), ())),
                preferred_element_type=F32,
            )
        return carry

    lax.fori_loop(0, len(groups), body, 0)
    out[...] = total[...].astype(out.dtype)


def listed(arrays, base, distances):
    out = []
    for n, value in enumerate(arrays):
        slots = [None]
        if value.ndim == 3:
            slots = [(1,), (2,), (3,), (0,)] if distances else [0, 1, 2, 3]
        out += [(base + n, slot) for slot in slots]
    return out


def apply_terms(place, field, ops, renewed=(), start=None, kind=BF16):
    at_ops = listed(ops, 0, bool(renewed))
    groups = len(at_ops)
    at_renewed = listed(renewed, len(ops), False)
    starts = start is not None
    name = "apply_moved" if renewed else "apply_terms"
    return pl.pallas_call(
        functools.partial(apply_kernel, at_ops, at_renewed, starts),
        in_specs=[SMEM, VMEM] + [ANY] * (len(ops) + len(renewed)) + [VMEM] * starts,
        out_specs=VMEM,
        out_shape=jax.ShapeDtypeStruct((LOCAL * BLOCK, BLOCK), kind),
        scratch_shapes=[
            pltpu.VMEM((groups, STACK, BLOCK), BF16),
            pltpu.VMEM((groups, STACK, BLOCK), BF16),
            pltpu.VMEM((groups, MIX_ROWS, BLOCK), BF16),
            pltpu.VMEM((LOCAL * BLOCK, BLOCK), F32),
            pltpu.SemaphoreType.DMA((groups, 3)),
        ],
        compiler_params=pltpu.CompilerParams(vmem_limit_bytes=60 << 20),
        name=f"{name}_{groups}_{int(starts)}",
        cost_estimate=pl.CostEstimate(flops=1 << 20, bytes_accessed=1 << 16, transcendentals=0),
    )(place, field, *ops, *renewed, *([start] if starts else []))


def reduce_chunks(partial):
    parts = exchange(partial.reshape(8, CHUNK, BLOCK), HOLDERS)
    return jnp.sum(parts.astype(F32), axis=0).astype(BF16)


def after(value, *others):
    return lax.optimization_barrier((value, *others))[0]


def spread(rows):
    whole = exchange(jnp.broadcast_to(rows[None], (8, CHUNK, BLOCK)), HOLDERS)
    return whole.reshape(LOCAL * BLOCK, BLOCK)


def shards(wave, left_ops, right_ops, site_ops, reach, pairing, site_tensor):
    pair = pairing[0]
    me = lax.axis_index("op")
    place = jnp.stack([me >> 4, (me >> 1) & 3, me & 1]).astype(jnp.int32)

    own_rows = lax.ppermute(wave[0], "op", TO_HOLDERS)
    kept, *passed = pack(place, pair, site_ops.reshape(-1), reach[0], left_ops, right_ops)
    field = spread(own_rows)
    kept, *passed = lax.optimization_barrier((kept, *passed, field))[:5]
    packed = after(place, kept)
    kept = exchange(kept, LINES)
    passed = [lax.ppermute(passed[d], "op", along(d, 1)) for d in (1, 2, 3, 0)]
    renewed_passed = renew(False, packed, pair, left_ops, site_tensor)
    renewed_kept = renew(True, after(place, renewed_passed), pair, left_ops, site_tensor)
    renewed = []
    for value, flip in ((renewed_kept, 0), (renewed_passed, 1)):
        hop = lax.ppermute(value, "sect", [(0, 1), (1, 0)]).reshape(4, STACK, BLOCK)
        renewed += [
            lax.ppermute(hop[d], "op", along(d, flip)) if d + flip else hop[d] for d in (1, 2, 3, 0)
        ]

    partial = apply_terms(place, field, [kept, *passed])
    first = reduce_chunks(partial)
    first_own = lax.ppermute(first, "op", TO_OWNERS)
    first_field = spread(first)
    first_field, *renewed = lax.optimization_barrier((first_field, *renewed))
    partial = apply_terms(place, first_field, [kept, *passed])
    second = reduce_chunks(partial)
    second_own = lax.ppermute(second, "op", TO_OWNERS)

    partial = apply_terms(place, after(field, partial), [kept, *passed], renewed)
    moved = reduce_chunks(after(partial, second))
    moved_own = lax.ppermute(moved, "op", TO_OWNERS)
    return first_own[None], second_own[None], moved_own[None]


def solution(mesh):
    placed = (
        P("sect", "op", None),
        P("sect", "op", None, None, None),
        P("sect", "op", None, None, None),
        P("sect", "op", None, None),
        P("sect", "op"),
        P("sect", None),
        P("sect", None, None, None, None),
    )
    return jax.shard_map(
        shards,
        mesh=mesh,
        in_specs=placed,
        out_specs=(P("sect", "op", None), P("sect", "op", None), P("sect", "op", None)),
        check_vma=False,
    )
```

time: 1110 us -> 230 us (0.21)
  the two profiles are of different devices: /device:TPU:0 before, /device:TPU:120 now
where the time goes in v2:
time: 230 us; the launch traced here: 229 us
  starting transfers between devices  80.6 us (35%)
  waiting for transfers between devices  67.4 us (29%)
  Pallas kernels  65.9 us (29%)
  local copies, waits for them, and re-layouts  13 us (6%)
    pallas_call x3, Pallas kernels, apply_terms(): pl.pallas_call(functools.partial(apply_kernel, at_ops, at_renewed, starts...  44.7 us
    all_to_all x6, starting transfers between devices, exchange(): return lax.all_to_all(value, 'op', 0, 0, axis_index_groups=groups)  39 us
    all_to_all x6, waiting for transfers between devices, exchange(): return lax.all_to_all(value, 'op', 0, 0, axis_index_groups=groups)  23.8 us
    ppermute x4, waiting for transfers between devices, shards(): passed = [lax.ppermute(passed[d], 'op', along(d, 1)) for d in (1, 2, 3, 0)]  14.6 us
    pallas_call x2, Pallas kernels, renew(): pl.pallas_call(renew_kernel, grid_spec=grid_spec, out_shape=jax.ShapeDtyp...  14.4 us
    ppermute x7, starting transfers between devices, shards(): lax.ppermute(hop[d], 'op', along(d, flip))  12.4 us
    ppermute x7, waiting for transfers between devices, shards(): lax.ppermute(hop[d], 'op', along(d, flip))  11.7 us
    ppermute x4, starting transfers between devices, shards(): passed = [lax.ppermute(passed[d], 'op', along(d, 1)) for d in (1, 2, 3, 0)]  7.81 us
  transfers between devices with their start and end apart: 23, of which 9 were waited for; matrix products, arithmetic and copies ran while one was open for 3% of the time, Pallas kernels for 22%

profile of v2, /device:TPU:120, one launch (start us, length us, event | category | flops | bytes accessed | tf_op | source)
XLA Modules:
  0.0 228.6 jit_solution(12541380599343686558)
XLA Ops:
  0.6 4.8 %collective-permute-start = (bf16[128,256]{1,0:T(8,128)(2,1)}, bf16[128,256]{1,0:T(8,128)(2,1)S(1)}, u32[]{:S(2)}, u32[]{:S(2)}) collective-permute-start(bf16[128,256]{1,0:T(8,128)(2,1)} %bitcast.43), channel_id=1, source_target_pairs={{0,0},{1,8},{2,22},{3,30},{4,36},{5,44},{6,50},{7,58},{8,1},{9,9},... | collective-permute-start | bytes 196616 | tf_op jit(solution)/shard_map/ppermute | solution.py:290
  5.4 7.7 %collective-permute-done = bf16[128,256]{1,0:T(8,128)(2,1)S(1)} collective-permute-done((bf16[128,256]{1,0:T(8,128)(2,1)}, bf16[128,256]{1,0:T(8,128)(2,1)S(1)}, u32[]{:S(2)}, u32[]{:S(2)}) %collective-permute-start) | collective-permute-done | bytes 65568 | tf_op jit(solution)/shard_map/ppermute | solution.py:290
  13.1 0.8 broadcast_in_dim.10
  13.9 4.8 %all-to-all-start = ((bf16[8,128,256]{2,1,0:T(8,128)(2,1)}), bf16[8,128,256]{2,1,0:T(8,128)(2,1)S(1)}, u32[]{:S(2)}, u32[]{:S(2)}) async-start(bf16[8,128,256]{2,1,0:T(8,128)(2,1)} %broadcast_in_dim.10), calls=%async_computation | async-start | bytes 1048576 | tf_op jit(solution)/shard_map/all_to_all | solution.py:57
  18.7 0.7 reshape.45.site
  19.4 0.6 pad_add_fusion.place
  20.0 6.8 %pack.1 = (bf16[4,1552,256]{2,1,0:T(8,128)(2,1)}, bf16[1552,256]{1,0:T(8,128)(2,1)}, bf16[1552,256]{1,0:T(8,128)(2,1)}, bf16[1552,256]{1,0:T(8,128)(2,1)}, bf16[1552,256]{1,0:T(8,128)(2,1)}) custom-call(s32[3]{0:T(128)} %pad_add_fusion.place, s32[8]{0:T(128)} %bitcast.40, f32[48]{0:T(128)} %reshape.45.site, s32[3]{0:T(128)} %bitcast.39, ...), custom_call_target="tpu_custom_call" | custom-call | flops 1048576 | bytes 65536 | tf_op jit(solution)/shard_map/pack/pallas_call | solution.py:111
  26.8 3.6 %all-to-all-done = bf16[8,128,256]{2,1,0:T(8,128)(2,1)S(1)} async-done(((bf16[8,128,256]{2,1,0:T(8,128)(2,1)}), bf16[8,128,256]{2,1,0:T(8,128)(2,1)S(1)}, u32[]{:S(2)}, u32[]{:S(2)}) %all-to-all-start) | async-done | bytes 524320 | tf_op jit(solution)/shard_map/all_to_all | solution.py:57
  30.4 0.8 copy-done.3
  31.2 3.7 %all-to-all-start.1 = ((bf16[4,1552,256]{2,1,0:T(8,128)(2,1)}), bf16[4,1552,256]{2,1,0:T(8,128)(2,1)S(1)}, u32[]{:S(2)}, u32[]{:S(2)}) async-start(bf16[4,1552,256]{2,1,0:T(8,128)(2,1)} %get-tuple-element.31), calls=%async_computation.1 | async-start | bytes 6356992 | tf_op jit(solution)/shard_map/all_to_all | solution.py:57
  34.9 0.1 collective-permute-start.1
  35.0 7.2 %renew_swapped.1 = bf16[4,3,256,256]{3,2,1,0:T(8,128)(2,1)} custom-call(s32[3]{0:T(128)} %pad_add_fusion.place, s32[8]{0:T(128)} %bitcast.41, bf16[1,3,8,256,256]{4,3,2,1,0:T(8,128)(2,1)} %left.5, bf16[1,8,4,256,256]{4,3,2,1,0:T(8,128)(2,1)} %tensor.3), custom_call_target="tpu_custom_call" | custom-call | flops 3221225472 | bytes 20971520 | tf_op jit(solution)/shard_map/renew_swapped/pallas_call | solution.py:162
  42.2 7.2 %renew_kept.1 = bf16[4,3,256,256]{3,2,1,0:T(8,128)(2,1)} custom-call(s32[3]{0:T(128)} %pad_add_fusion.place, s32[8]{0:T(128)} %bitcast.42, bf16[1,3,8,256,256]{4,3,2,1,0:T(8,128)(2,1)} %left.5, bf16[1,8,4,256,256]{4,3,2,1,0:T(8,128)(2,1)} %tensor.3), custom_call_target="tpu_custom_call" | custom-call | flops 3221225472 | bytes 20971520 | tf_op jit(solution)/shard_map/renew_kept/pallas_call | solution.py:162
  49.4 0.8 collective-permute-start.6
  50.2 1.3 collective-permute-start.10
  51.4 3.9 %collective-permute-start.2 = (bf16[1552,256]{1,0:T(8,128)(2,1)}, bf16[1552,256]{1,0:T(8,128)(2,1)S(1)}, u32[]{:S(2)}, u32[]{:S(2)}) collective-permute-start(bf16[1552,256]{1,0:T(8,128)(2,1)} %get-tuple-element.33), channel_id=1, source_target_pairs={{0,33},{1,4},{2,35},{3,6},{4,37},{5,0},{6,39},{7,2},{8,41},{9,12},... | collective-permute-start | bytes 2383880 | tf_op jit(solution)/shard_map/ppermute | solution.py:296
  55.3 0.2 collective-permute-start.3
  55.5 6.4 %collective-permute-done.1.refs_1_ = bf16[1552,256]{1,0:T(8,128)(2,1)} collective-permute-done((bf16[1552,256]{1,0:T(8,128)(2,1)}, bf16[1552,256]{1,0:T(8,128)(2,1)}, u32[]{:S(2)}, u32[]{:S(2)}) %collective-permute-start.1) | collective-permute-done | bytes 794656 | tf_op jit(solution)/shard_map/ppermute | solution.py:296
  61.9 3.6 %collective-permute-start.4 = (bf16[1552,256]{1,0:T(8,128)(2,1)}, bf16[1552,256]{1,0:T(8,128)(2,1)}, u32[]{:S(2)}, u32[]{:S(2)}) collective-permute-start(bf16[1552,256]{1,0:T(8,128)(2,1)} %get-tuple-element.35), channel_id=1, source_target_pairs={{0,1},{1,0},{2,3},{3,2},{4,5},{5,4},{6,7},{7,6},{8,9},{9,8},{10,11... | collective-permute-start | bytes 2383880 | tf_op jit(solution)/shard_map/ppermute | solution.py:296
  65.5 4.9 %collective-permute-done.2.refs_2_ = bf16[1552,256]{1,0:T(8,128)(2,1)S(1)} collective-permute-done((bf16[1552,256]{1,0:T(8,128)(2,1)}, bf16[1552,256]{1,0:T(8,128)(2,1)S(1)}, u32[]{:S(2)}, u32[]{:S(2)}) %collective-permute-start.2) | collective-permute-done | bytes 794656 | tf_op jit(solution)/shard_map/ppermute | solution.py:296
  70.4 3.3 %collective-permute-done.3.refs_3_ = bf16[1552,256]{1,0:T(8,128)(2,1)S(1)} collective-permute-done((bf16[1552,256]{1,0:T(8,128)(2,1)}, bf16[1552,256]{1,0:T(8,128)(2,1)S(1)}, u32[]{:S(2)}, u32[]{:S(2)}) %collective-permute-start.3) | collective-permute-done | bytes 794656 | tf_op jit(solution)/shard_map/ppermute | solution.py:296
  73.7 0.9 copy-done.2
  74.6 0.0 collective-permute-done.4.refs_4_
  74.6 1.6 copy-done
  76.3 14.9 %apply_terms_8_0.2 = bf16[1024,256]{1,0:T(8,128)(2,1)} custom-call(s32[3]{0:T(128)} %pad_add_fusion.place, bf16[1024,256]{1,0:T(8,128)(2,1)} %bitcast.22, bf16[4,1552,256]{2,1,0:T(8,128)(2,1)} %copy-done, bf16[1552,256]{1,0:T(8,128)(2,1)} %collective-permute-done.1.refs_1_, bf16[1552,256]{1,0:T(8,128)(2,1)} %copy-done.1, bf16[1552,256]{1,0:T(8,128)(2,1)} %copy-done.2, ...), custom_call_target="tpu_custom_call" | custom-call | flops 1048576 | bytes 65536 | tf_op jit(solution)/shard_map/apply_terms_8_0/pallas_call | solution.py:253
  91.2 7.6 %all-to-all-start.2 = ((bf16[8,128,256]{2,1,0:T(8,128)(2,1)}), bf16[8,128,256]{2,1,0:T(8,128)(2,1)S(1)}, u32[]{:S(2)}, u32[]{:S(2)}) async-start(bf16[8,128,256]{2,1,0:T(8,128)(2,1)} %bitcast.25), calls=%async_computation.2 | async-start | bytes 1048576 | tf_op jit(solution)/shard_map/all_to_all | solution.py:57
  98.7 2.3 fusion.1
  101.0 3.0 %collective-permute-start.9 = (bf16[768,256]{1,0:T(8,128)(2,1)S(1)}, bf16[768,256]{1,0:T(8,128)(2,1)S(1)}, u32[]{:S(2)}, u32[]{:S(2)}) collective-permute-start(bf16[768,256]{1,0:T(8,128)(2,1)S(1)} %bitcast.31), channel_id=1, source_target_pairs={{0,48},{1,7},{2,50},{3,1},{4,52},{5,3},{6,54},{7,5},{8,56},{9,15},... | collective-permute-start | bytes 1179656 | tf_op jit(solution)/shard_map/ppermute | solution.py:303
  104.0 1.9 collective-permute-start.8
  105.9 1.4 collective-permute-start.7
  107.3 20.2 %all-to-all-done.2 = bf16[8,128,256]{2,1,0:T(8,128)(2,1)S(1)} async-done(((bf16[8,128,256]{2,1,0:T(8,128)(2,1)}), bf16[8,128,256]{2,1,0:T(8,128)(2,1)S(1)}, u32[]{:S(2)}, u32[]{:S(2)}) %all-to-all-start.2) | async-done | bytes 524320 | tf_op jit(solution)/shard_map/all_to_all | solution.py:57
  127.6 0.1 reduce_sum.36
  127.7 0.9 broadcast_in_dim.23
  128.5 7.4 %all-to-all-start.3 = ((bf16[8,128,256]{2,1,0:T(8,128)(2,1)}), bf16[8,128,256]{2,1,0:T(8,128)(2,1)S(1)}, u32[]{:S(2)}, u32[]{:S(2)}) async-start(bf16[8,128,256]{2,1,0:T(8,128)(2,1)} %broadcast_in_dim.23), calls=%async_computation.3 | async-start | bytes 1048576 | tf_op jit(solution)/shard_map/all_to_all | solution.py:57
  135.9 0.0 collective-permute-done.10
  136.0 1.5 fusion
  137.4 2.6 %collective-permute-start.13 = (bf16[768,256]{1,0:T(8,128)(2,1)S(1)}, bf16[768,256]{1,0:T(8,128)(2,1)S(1)}, u32[]{:S(2)}, u32[]{:S(2)}) collective-permute-start(bf16[768,256]{1,0:T(8,128)(2,1)S(1)} %bitcast.35), channel_id=1, source_target_pairs={{0,49},{1,6},{2,51},{3,0},{4,53},{5,2},{6,55},{7,4},{8,57},{9,14},... | collective-permute-start | bytes 1179656 | tf_op jit(solution)/shard_map/ppermute | solution.py:303
  140.1 0.0 collective-permute-start.14
  140.1 0.0 collective-permute-done.9.refs_7_
  140.1 3.2 %collective-permute-start.12 = (bf16[768,256]{1,0:T(8,128)(2,1)S(1)}, bf16[768,256]{1,0:T(8,128)(2,1)S(1)}, u32[]{:S(2)}, u32[]{:S(2)}) collective-permute-start(bf16[768,256]{1,0:T(8,128)(2,1)S(1)} %bitcast.33), channel_id=1, source_target_pairs={{0,33},{1,4},{2,35},{3,6},{4,37},{5,0},{6,39},{7,2},{8,41},{9,12},... | collective-permute-start | bytes 1179656 | tf_op jit(solution)/shard_map/ppermute | solution.py:303
  143.3 0.0 collective-permute-done.8.refs_6_
  143.3 0.1 collective-permute-start.11
  143.5 0.0 collective-permute-done.7.refs_5_
  143.5 11.7 %collective-permute-done.13.refs_11_ = bf16[768,256]{1,0:T(8,128)(2,1)S(1)} collective-permute-done((bf16[768,256]{1,0:T(8,128)(2,1)S(1)}, bf16[768,256]{1,0:T(8,128)(2,1)S(1)}, u32[]{:S(2)}, u32[]{:S(2)}) %collective-permute-start.13) | collective-permute-done | bytes 393248 | tf_op jit(solution)/shard_map/ppermute | solution.py:303
  155.1 0.0 collective-permute-done.14.refs_12_
  155.2 0.8 copy-done.9
  155.9 0.0 collective-permute-done.11.refs_9_
  155.9 0.0 all-to-all-done.3
  156.0 0.8 copy-done.4
  156.8 14.9 %apply_terms_8_0.3 = bf16[1024,256]{1,0:T(8,128)(2,1)} custom-call(s32[3]{0:T(128)} %pad_add_fusion.place, bf16[1024,256]{1,0:T(8,128)(2,1)} %bitcast.24, bf16[4,1552,256]{2,1,0:T(8,128)(2,1)} %copy-done, bf16[1552,256]{1,0:T(8,128)(2,1)} %collective-permute-done.1.refs_1_, bf16[1552,256]{1,0:T(8,128)(2,1)} %copy-done.1, bf16[1552,256]{1,0:T(8,128)(2,1)} %copy-done.2, ...), custom_call_target="tpu_custom_call" | custom-call | flops 1048576 | bytes 65536 | tf_op jit(solution)/shard_map/apply_terms_8_0/pallas_call | solution.py:253
  171.7 5.9 %all-to-all-start.4 = ((bf16[8,128,256]{2,1,0:T(8,128)(2,1)}), bf16[8,128,256]{2,1,0:T(8,128)(2,1)S(1)}, u32[]{:S(2)}, u32[]{:S(2)}) async-start(bf16[8,128,256]{2,1,0:T(8,128)(2,1)} %bitcast.26), calls=%async_computation.4 | async-start | bytes 1048576 | tf_op jit(solution)/shard_map/all_to_all | solution.py:57
  177.6 15.0 %apply_moved_8_0.1 = bf16[1024,256]{1,0:T(8,128)(2,1)} custom-call(s32[3]{0:T(128)} %pad_add_fusion.place, bf16[1024,256]{1,0:T(8,128)(2,1)} %bitcast.23, bf16[4,1552,256]{2,1,0:T(8,128)(2,1)} %copy-done, bf16[1552,256]{1,0:T(8,128)(2,1)} %collective-permute-done.1.refs_1_, bf16[1552,256]{1,0:T(8,128)(2,1)} %copy-done.1, bf16[1552,256]{1,0:T(8,128)(2,1)} %copy-done.2, ...), custom_call_target="tpu_custom_call" | custom-call | flops 1048576 | bytes 65536 | tf_op jit(solution)/shard_map/apply_moved_8_0/pallas_call | solution.py:253
  192.6 0.1 reduce_sum.37
  192.7 9.6 %all-to-all-start.5 = ((bf16[8,128,256]{2,1,0:T(8,128)(2,1)}), bf16[8,128,256]{2,1,0:T(8,128)(2,1)S(1)}, u32[]{:S(2)}, u32[]{:S(2)}) async-start(bf16[8,128,256]{2,1,0:T(8,128)(2,1)} %bitcast.27), calls=%async_computation.5 | async-start | bytes 1048576 | tf_op jit(solution)/shard_map/all_to_all | solution.py:57
  202.3 5.4 %collective-permute-start.5 = (bf16[128,256]{1,0:T(8,128)(2,1)S(1)}, bf16[128,256]{1,0:T(8,128)(2,1)S(1)}, u32[]{:S(2)}, u32[]{:S(2)}) collective-permute-start(bf16[128,256]{1,0:T(8,128)(2,1)S(1)} %reduce_sum.36), channel_id=1, source_target_pairs={{0,0},{8,1},{22,2},{30,3},{36,4},{44,5},{50,6},{58,7},{1,8},{9,9},... | collective-permute-start | bytes 196616 | tf_op jit(solution)/shard_map/ppermute | solution.py:308
  207.7 7.3 %collective-permute-start.15 = (bf16[128,256]{1,0:T(8,128)(2,1)S(1)}, bf16[128,256]{1,0:T(8,128)(2,1)S(1)}, u32[]{:S(2)}, u32[]{:S(2)}) collective-permute-start(bf16[128,256]{1,0:T(8,128)(2,1)S(1)} %reduce_sum.37), channel_id=1, source_target_pairs={{0,0},{8,1},{22,2},{30,3},{36,4},{44,5},{50,6},{58,7},{1,8},{9,9},... | collective-permute-start | bytes 196616 | tf_op jit(solution)/shard_map/ppermute | solution.py:313
  215.0 0.0 all-to-all-done.5
  215.0 0.1 reduce_sum.38
  215.1 1.9 collective-permute-start.16
  217.1 2.4 %collective-permute-done.15 = bf16[128,256]{1,0:T(8,128)(2,1)S(1)} collective-permute-done((bf16[128,256]{1,0:T(8,128)(2,1)S(1)}, bf16[128,256]{1,0:T(8,128)(2,1)S(1)}, u32[]{:S(2)}, u32[]{:S(2)}) %collective-permute-start.15) | collective-permute-done | bytes 65568 | tf_op jit(solution)/shard_map/ppermute | solution.py:313
  219.5 7.3 %collective-permute-done.16 = bf16[128,256]{1,0:T(8,128)(2,1)S(1)} collective-permute-done((bf16[128,256]{1,0:T(8,128)(2,1)S(1)}, bf16[128,256]{1,0:T(8,128)(2,1)S(1)}, u32[]{:S(2)}, u32[]{:S(2)}) %collective-permute-start.16) | collective-permute-done | bytes 65568 | tf_op jit(solution)/shard_map/ppermute | solution.py:317
  226.7 0.6 copy.13
  227.4 0.6 copy.14
  228.0 0.6 copy.15
  (26 shorter events, 0.1 us)
Async XLA Ops:
  0.6 18.1 %copy-start.12 = (f32[1,3,4,4]{3,2,1,0:T(4,128)S(1)}, f32[1,3,4,4]{3,2,1,0:T(4,128)}, u32[]{:S(2)}) copy-start(f32[1,3,4,4]{3,2,1,0:T(4,128)} %param.10) | copy-start | bytes 580
  0.6 12.5 %collective-permute-start = (bf16[128,256]{1,0:T(8,128)(2,1)}, bf16[128,256]{1,0:T(8,128)(2,1)S(1)}, u32[]{:S(2)}, u32[]{:S(2)}) collective-permute-start(bf16[128,256]{1,0:T(8,128)(2,1)} %bitcast.43), channel_id=1, source_target_pairs={{0,0},{1,8},{2,22},{3,30},{4,36},{5,44},{6,50},{7,58},{8,1},{9,9},... | collective-permute-start | bytes 196616 | tf_op jit(solution)/shard_map/ppermute | solution.py:290
  13.9 16.5 %all-to-all-start = ((bf16[8,128,256]{2,1,0:T(8,128)(2,1)}), bf16[8,128,256]{2,1,0:T(8,128)(2,1)S(1)}, u32[]{:S(2)}, u32[]{:S(2)}) async-start(bf16[8,128,256]{2,1,0:T(8,128)(2,1)} %broadcast_in_dim.10), calls=%async_computation | async-start | bytes 1048576 | tf_op jit(solution)/shard_map/all_to_all | solution.py:57
  30.4 0.8 copy-start.3
  31.2 43.4 %all-to-all-start.1 = ((bf16[4,1552,256]{2,1,0:T(8,128)(2,1)}), bf16[4,1552,256]{2,1,0:T(8,128)(2,1)S(1)}, u32[]{:S(2)}, u32[]{:S(2)}) async-start(bf16[4,1552,256]{2,1,0:T(8,128)(2,1)} %get-tuple-element.31), calls=%async_computation.1 | async-start | bytes 6356992 | tf_op jit(solution)/shard_map/all_to_all | solution.py:57
  34.9 27.0 %collective-permute-start.1 = (bf16[1552,256]{1,0:T(8,128)(2,1)}, bf16[1552,256]{1,0:T(8,128)(2,1)}, u32[]{:S(2)}, u32[]{:S(2)}) collective-permute-start(bf16[1552,256]{1,0:T(8,128)(2,1)} %get-tuple-element.32), channel_id=1, source_target_pairs={{0,17},{1,2},{2,19},{3,4},{4,21},{5,6},{6,23},{7,0},{8,25},{9,10},... | collective-permute-start | bytes 2383880 | tf_op jit(solution)/shard_map/ppermute | solution.py:296
  49.4 49.3 %collective-permute-start.6 = (bf16[4,3,256,256]{3,2,1,0:T(8,128)(2,1)}, bf16[4,3,256,256]{3,2,1,0:T(8,128)(2,1)}, u32[]{:S(2)}, u32[]{:S(2)}) collective-permute-start(bf16[4,3,256,256]{3,2,1,0:T(8,128)(2,1)} %renew_kept.1), channel_id=1, source_target_pairs={{0,64},{64,0},{1,65},{65,1},{2,66},{66,2},{3,67},{67,3},{4,68},{68... | collective-permute-start | bytes 4718600 | tf_op jit(solution)/shard_map/ppermute | solution.py:301
  50.2 85.8 %collective-permute-start.10 = (bf16[4,3,256,256]{3,2,1,0:T(8,128)(2,1)}, bf16[4,3,256,256]{3,2,1,0:T(8,128)(2,1)}, u32[]{:S(2)}, u32[]{:S(2)}) collective-permute-start(bf16[4,3,256,256]{3,2,1,0:T(8,128)(2,1)} %renew_swapped.1), channel_id=1, source_target_pairs={{0,64},{64,0},{1,65},{65,1},{2,66},{66,2},{3,67},{67,3},{4,68},{68... | collective-permute-start | bytes 4718600 | tf_op jit(solution)/shard_map/ppermute | solution.py:301
  51.4 19.0 %collective-permute-start.2 = (bf16[1552,256]{1,0:T(8,128)(2,1)}, bf16[1552,256]{1,0:T(8,128)(2,1)S(1)}, u32[]{:S(2)}, u32[]{:S(2)}) collective-permute-start(bf16[1552,256]{1,0:T(8,128)(2,1)} %get-tuple-element.33), channel_id=1, source_target_pairs={{0,33},{1,4},{2,35},{3,6},{4,37},{5,0},{6,39},{7,2},{8,41},{9,12},... | collective-permute-start | bytes 2383880 | tf_op jit(solution)/shard_map/ppermute | solution.py:296
  55.3 18.4 %collective-permute-start.3 = (bf16[1552,256]{1,0:T(8,128)(2,1)}, bf16[1552,256]{1,0:T(8,128)(2,1)S(1)}, u32[]{:S(2)}, u32[]{:S(2)}) collective-permute-start(bf16[1552,256]{1,0:T(8,128)(2,1)} %get-tuple-element.34), channel_id=1, source_target_pairs={{0,49},{1,6},{2,51},{3,0},{4,53},{5,2},{6,55},{7,4},{8,57},{9,14},... | collective-permute-start | bytes 2383880 | tf_op jit(solution)/shard_map/ppermute | solution.py:296
  61.9 12.7 %collective-permute-start.4 = (bf16[1552,256]{1,0:T(8,128)(2,1)}, bf16[1552,256]{1,0:T(8,128)(2,1)}, u32[]{:S(2)}, u32[]{:S(2)}) collective-permute-start(bf16[1552,256]{1,0:T(8,128)(2,1)} %get-tuple-element.35), channel_id=1, source_target_pairs={{0,1},{1,0},{2,3},{3,2},{4,5},{5,4},{6,7},{7,6},{8,9},{9,8},{10,11... | collective-permute-start | bytes 2383880 | tf_op jit(solution)/shard_map/ppermute | solution.py:296
  70.4 3.3 %copy-start.1 = (bf16[1552,256]{1,0:T(8,128)(2,1)}, bf16[1552,256]{1,0:T(8,128)(2,1)S(1)}, u32[]{:S(2)}) copy-start(bf16[1552,256]{1,0:T(8,128)(2,1)S(1)} %collective-permute-done.2.refs_2_) | copy-start | bytes 2383876
  73.7 0.9 copy-start.2
  74.6 1.6 copy-start
  91.2 36.4 %all-to-all-start.2 = ((bf16[8,128,256]{2,1,0:T(8,128)(2,1)}), bf16[8,128,256]{2,1,0:T(8,128)(2,1)S(1)}, u32[]{:S(2)}, u32[]{:S(2)}) async-start(bf16[8,128,256]{2,1,0:T(8,128)(2,1)} %bitcast.25), calls=%async_computation.2 | async-start | bytes 1048576 | tf_op jit(solution)/shard_map/all_to_all | solution.py:57
  101.0 39.1 %collective-permute-start.9 = (bf16[768,256]{1,0:T(8,128)(2,1)S(1)}, bf16[768,256]{1,0:T(8,128)(2,1)S(1)}, u32[]{:S(2)}, u32[]{:S(2)}) collective-permute-start(bf16[768,256]{1,0:T(8,128)(2,1)S(1)} %bitcast.31), channel_id=1, source_target_pairs={{0,48},{1,7},{2,50},{3,1},{4,52},{5,3},{6,54},{7,5},{8,56},{9,15},... | collective-permute-start | bytes 1179656 | tf_op jit(solution)/shard_map/ppermute | solution.py:303
  104.0 39.3 %collective-permute-start.8 = (bf16[768,256]{1,0:T(8,128)(2,1)S(1)}, bf16[768,256]{1,0:T(8,128)(2,1)S(1)}, u32[]{:S(2)}, u32[]{:S(2)}) collective-permute-start(bf16[768,256]{1,0:T(8,128)(2,1)S(1)} %bitcast.30), channel_id=1, source_target_pairs={{0,32},{1,5},{2,34},{3,7},{4,36},{5,1},{6,38},{7,3},{8,40},{9,13},... | collective-permute-start | bytes 1179656 | tf_op jit(solution)/shard_map/ppermute | solution.py:303
  105.9 37.5 %collective-permute-start.7 = (bf16[768,256]{1,0:T(8,128)(2,1)S(1)}, bf16[768,256]{1,0:T(8,128)(2,1)S(1)}, u32[]{:S(2)}, u32[]{:S(2)}) collective-permute-start(bf16[768,256]{1,0:T(8,128)(2,1)S(1)} %bitcast.29), channel_id=1, source_target_pairs={{0,16},{1,3},{2,18},{3,5},{4,20},{5,7},{6,22},{7,1},{8,24},{9,11},... | collective-permute-start | bytes 1179656 | tf_op jit(solution)/shard_map/ppermute | solution.py:303
  128.5 27.4 %all-to-all-start.3 = ((bf16[8,128,256]{2,1,0:T(8,128)(2,1)}), bf16[8,128,256]{2,1,0:T(8,128)(2,1)S(1)}, u32[]{:S(2)}, u32[]{:S(2)}) async-start(bf16[8,128,256]{2,1,0:T(8,128)(2,1)} %broadcast_in_dim.23), calls=%async_computation.3 | async-start | bytes 1048576 | tf_op jit(solution)/shard_map/all_to_all | solution.py:57
  137.4 17.7 %collective-permute-start.13 = (bf16[768,256]{1,0:T(8,128)(2,1)S(1)}, bf16[768,256]{1,0:T(8,128)(2,1)S(1)}, u32[]{:S(2)}, u32[]{:S(2)}) collective-permute-start(bf16[768,256]{1,0:T(8,128)(2,1)S(1)} %bitcast.35), channel_id=1, source_target_pairs={{0,49},{1,6},{2,51},{3,0},{4,53},{5,2},{6,55},{7,4},{8,57},{9,14},... | collective-permute-start | bytes 1179656 | tf_op jit(solution)/shard_map/ppermute | solution.py:303
  140.1 15.1 %collective-permute-start.14 = (bf16[768,256]{1,0:T(8,128)(2,1)S(1)}, bf16[768,256]{1,0:T(8,128)(2,1)S(1)}, u32[]{:S(2)}, u32[]{:S(2)}) collective-permute-start(bf16[768,256]{1,0:T(8,128)(2,1)S(1)} %bitcast.34), channel_id=1, source_target_pairs={{0,1},{1,0},{2,3},{3,2},{4,5},{5,4},{6,7},{7,6},{8,9},{9,8},{10,11... | collective-permute-start | bytes 1179656 | tf_op jit(solution)/shard_map/ppermute | solution.py:303
  140.1 37.5 %copy-start.5 = (bf16[768,256]{1,0:T(8,128)(2,1)}, bf16[768,256]{1,0:T(8,128)(2,1)S(1)}, u32[]{:S(2)}) copy-start(bf16[768,256]{1,0:T(8,128)(2,1)S(1)} %collective-permute-done.9.refs_7_) | copy-start | bytes 1179652
  140.1 15.1 %collective-permute-start.12 = (bf16[768,256]{1,0:T(8,128)(2,1)S(1)}, bf16[768,256]{1,0:T(8,128)(2,1)S(1)}, u32[]{:S(2)}, u32[]{:S(2)}) collective-permute-start(bf16[768,256]{1,0:T(8,128)(2,1)S(1)} %bitcast.33), channel_id=1, source_target_pairs={{0,33},{1,4},{2,35},{3,6},{4,37},{5,0},{6,39},{7,2},{8,41},{9,12},... | collective-permute-start | bytes 1179656 | tf_op jit(solution)/shard_map/ppermute | solution.py:303
  143.3 34.2 %copy-start.6 = (bf16[768,256]{1,0:T(8,128)(2,1)}, bf16[768,256]{1,0:T(8,128)(2,1)S(1)}, u32[]{:S(2)}) copy-start(bf16[768,256]{1,0:T(8,128)(2,1)S(1)} %collective-permute-done.8.refs_6_) | copy-start | bytes 1179652
  143.3 12.6 %collective-permute-start.11 = (bf16[768,256]{1,0:T(8,128)(2,1)S(1)}, bf16[768,256]{1,0:T(8,128)(2,1)S(1)}, u32[]{:S(2)}, u32[]{:S(2)}) collective-permute-start(bf16[768,256]{1,0:T(8,128)(2,1)S(1)} %bitcast.32), channel_id=1, source_target_pairs={{0,17},{1,2},{2,19},{3,4},{4,21},{5,6},{6,23},{7,0},{8,25},{9,10},... | collective-permute-start | bytes 1179656 | tf_op jit(solution)/shard_map/ppermute | solution.py:303
  143.5 34.1 %copy-start.7 = (bf16[768,256]{1,0:T(8,128)(2,1)}, bf16[768,256]{1,0:T(8,128)(2,1)S(1)}, u32[]{:S(2)}) copy-start(bf16[768,256]{1,0:T(8,128)(2,1)S(1)} %collective-permute-done.7.refs_5_) | copy-start | bytes 1179652
  155.1 22.4 %copy-start.8 = (bf16[768,256]{1,0:T(8,128)(2,1)}, bf16[768,256]{1,0:T(8,128)(2,1)S(1)}, u32[]{:S(2)}) copy-start(bf16[768,256]{1,0:T(8,128)(2,1)S(1)} %collective-permute-done.13.refs_11_) | copy-start | bytes 1179652
  155.1 0.8 copy-start.9
  155.9 21.6 %copy-start.10 = (bf16[768,256]{1,0:T(8,128)(2,1)}, bf16[768,256]{1,0:T(8,128)(2,1)S(1)}, u32[]{:S(2)}) copy-start(bf16[768,256]{1,0:T(8,128)(2,1)S(1)} %collective-permute-done.12.refs_10_) | copy-start | bytes 1179652
  155.9 21.6 %copy-start.11 = (bf16[768,256]{1,0:T(8,128)(2,1)}, bf16[768,256]{1,0:T(8,128)(2,1)S(1)}, u32[]{:S(2)}) copy-start(bf16[768,256]{1,0:T(8,128)(2,1)S(1)} %collective-permute-done.11.refs_9_) | copy-start | bytes 1179652
  156.0 0.8 copy-start.4
  171.7 20.9 %all-to-all-start.4 = ((bf16[8,128,256]{2,1,0:T(8,128)(2,1)}), bf16[8,128,256]{2,1,0:T(8,128)(2,1)S(1)}, u32[]{:S(2)}, u32[]{:S(2)}) async-start(bf16[8,128,256]{2,1,0:T(8,128)(2,1)} %bitcast.26), calls=%async_computation.4 | async-start | bytes 1048576 | tf_op jit(solution)/shard_map/all_to_all | solution.py:57
  192.7 22.4 %all-to-all-start.5 = ((bf16[8,128,256]{2,1,0:T(8,128)(2,1)}), bf16[8,128,256]{2,1,0:T(8,128)(2,1)S(1)}, u32[]{:S(2)}, u32[]{:S(2)}) async-start(bf16[8,128,256]{2,1,0:T(8,128)(2,1)} %bitcast.27), calls=%async_computation.5 | async-start | bytes 1048576 | tf_op jit(solution)/shard_map/all_to_all | solution.py:57
  202.3 14.8 %collective-permute-start.5 = (bf16[128,256]{1,0:T(8,128)(2,1)S(1)}, bf16[128,256]{1,0:T(8,128)(2,1)S(1)}, u32[]{:S(2)}, u32[]{:S(2)}) collective-permute-start(bf16[128,256]{1,0:T(8,128)(2,1)S(1)} %reduce_sum.36), channel_id=1, source_target_pairs={{0,0},{8,1},{22,2},{30,3},{36,4},{44,5},{50,6},{58,7},{1,8},{9,9},... | collective-permute-start | bytes 196616 | tf_op jit(solution)/shard_map/ppermute | solution.py:308
  207.7 11.8 %collective-permute-start.15 = (bf16[128,256]{1,0:T(8,128)(2,1)S(1)}, bf16[128,256]{1,0:T(8,128)(2,1)S(1)}, u32[]{:S(2)}, u32[]{:S(2)}) collective-permute-start(bf16[128,256]{1,0:T(8,128)(2,1)S(1)} %reduce_sum.37), channel_id=1, source_target_pairs={{0,0},{8,1},{22,2},{30,3},{36,4},{44,5},{50,6},{58,7},{1,8},{9,9},... | collective-permute-start | bytes 196616 | tf_op jit(solution)/shard_map/ppermute | solution.py:313
  215.1 11.6 %collective-permute-start.16 = (bf16[128,256]{1,0:T(8,128)(2,1)S(1)}, bf16[128,256]{1,0:T(8,128)(2,1)S(1)}, u32[]{:S(2)}, u32[]{:S(2)}) collective-permute-start(bf16[128,256]{1,0:T(8,128)(2,1)S(1)} %reduce_sum.38), channel_id=1, source_target_pairs={{0,0},{8,1},{22,2},{30,3},{36,4},{44,5},{50,6},{58,7},{1,8},{9,9},... | collective-permute-start | bytes 196616 | tf_op jit(solution)/shard_map/ppermute | solution.py:317

commit v3 on v2

--- a/solution.py
+++ b/solution.py
@@ -264,7 +264,9 @@
         ],
         compiler_params=pltpu.CompilerParams(vmem_limit_bytes=60 << 20),
         name=f"{name}_{groups}_{int(starts)}",
-        cost_estimate=pl.CostEstimate(flops=1 << 20, bytes_accessed=1 << 16, transcendentals=0),
+        cost_estimate=pl.CostEstimate(
+            flops=3 * groups * 8 * 2 * BLOCK**3, bytes_accessed=48 << 20, transcendentals=0
+        ),
     )(place, field, *ops, *renewed, *([start] if starts else []))
 
 
@@ -288,34 +290,40 @@
     place = jnp.stack([me >> 4, (me >> 1) & 3, me & 1]).astype(jnp.int32)
 
     own_rows = lax.ppermute(wave[0], "op", TO_HOLDERS)
-    kept, *passed = pack(place, pair, site_ops.reshape(-1), reach[0], left_ops, right_ops)
-    field = spread(own_rows)
-    kept, *passed = lax.optimization_barrier((kept, *passed, field))[:5]
-    packed = after(place, kept)
+    renewed_kept = renew(True, place, pair, left_ops, site_tensor)
+    field = spread(after(own_rows, renewed_kept))
+    kept, *passed = pack(
+        after(place, renewed_kept, own_rows),
+        pair,
+        site_ops.reshape(-1),
+        reach[0],
+        left_ops,
+        right_ops,
+    )
+    kept, *passed, renewed_kept, later, field = lax.optimization_barrier(
+        (kept, *passed, renewed_kept, place, field)
+    )
     kept = exchange(kept, LINES)
     passed = [lax.ppermute(passed[d], "op", along(d, 1)) for d in (1, 2, 3, 0)]
-    renewed_passed = renew(False, packed, pair, left_ops, site_tensor)
-    renewed_kept = renew(True, after(place, renewed_passed), pair, left_ops, site_tensor)
-    renewed = []
-    for value, flip in ((renewed_kept, 0), (renewed_passed, 1)):
-        hop = lax.ppermute(value, "sect", [(0, 1), (1, 0)]).reshape(4, STACK, BLOCK)
-        renewed += [
-            lax.ppermute(hop[d], "op", along(d, flip)) if d + flip else hop[d] for d in (1, 2, 3, 0)
-        ]
+    renewed_passed = renew(False, later, pair, left_ops, site_tensor)
+    near, far = [
+        lax.ppermute(value, "sect", [(0, 1), (1, 0)]).reshape(4, STACK, BLOCK)
+        for value in (renewed_kept, renewed_passed)
+    ]
+    near = [lax.ppermute(near[d], "op", along(d, 0)) for d in (1, 2, 3)] + [near[0]]
+    far = [lax.ppermute(far[d], "op", along(d, 1)) for d in (1, 2, 3, 0)]
 
     partial = apply_terms(place, field, [kept, *passed])
-    first = reduce_chunks(partial)
+    first = reduce_chunks(after(partial, *near))
     first_own = lax.ppermute(first, "op", TO_OWNERS)
-    first_field = spread(first)
-    first_field, *renewed = lax.optimization_barrier((first_field, *renewed))
+    first_field, first_own = lax.optimization_barrier((spread(first), first_own))
     partial = apply_terms(place, first_field, [kept, *passed])
     second = reduce_chunks(partial)
-    second_own = lax.ppermute(second, "op", TO_OWNERS)
-
-    partial = apply_terms(place, after(field, partial), [kept, *passed], renewed)
+
+    partial = apply_terms(place, after(field, partial), [kept, *passed], near + far)
     moved = reduce_chunks(after(partial, second))
-    moved_own = lax.ppermute(moved, "op", TO_OWNERS)
-    return first_own[None], second_own[None], moved_own[None]
+    last = lax.ppermute(jnp.stack([second, moved]), "op", TO_OWNERS)
+    return first_own[None], last[0:1], last[1:2]
 
 
 def solution(mesh):

time: 230 us -> 211 us (0.917)
  blocking collectives: 0 us -> 38.3 us
  starting transfers between devices: 80.6 us -> 50.6 us
  waiting for transfers between devices: 67.4 us -> 41.9 us
    all_to_all x0 -> x2, blocking collectives: none -> 38.3 us  [exchange(): return lax.all_to_all(value, 'op', 0, 0, axis_index_groups=groups)]
    all_to_all x6 -> x4, waiting for transfers between devices: 23.8 us -> 4.01 us  [exchange(): return lax.all_to_all(value, 'op', 0, 0, axis_index_groups=groups)]
    ppermute x4, waiting for transfers between devices: 14.6 us -> 0.01 us  [shards(): passed = [lax.ppermute(passed[d], 'op', along(d, 1)) for d in (1, 2, 3, 0)]]
    ppermute x11 -> x10, starting transfers between devices: 23.7 us -> 10.1 us  [the longest x3 3.17 us: shards(): lax.ppermute(near[d], 'op', along(d, 0))]
    ppermute x11 -> x10, waiting for transfers between devices: 21.4 us -> 34.4 us  [the longest x2 22.8 us: shards(): lax.ppermute(value, 'sect', [(0, 1), (1, 0)]).reshape(4, STACK, BLOCK)]
    all_to_all x6 -> x4, starting transfers between devices: 39 us -> 26.1 us  [exchange(): return lax.all_to_all(value, 'op', 0, 0, axis_index_groups=groups)]
    ppermute x1, waiting for transfers between devices: 7.69 us -> 0.01 us  [shards(): own_rows = lax.ppermute(wave[0], 'op', TO_HOLDERS)]
    ppermute x1, waiting for transfers between devices: 0.01 us -> 3.53 us  [shards(): first_own = lax.ppermute(first, 'op', TO_OWNERS)]
  transfers between devices with their start and end apart: 23 -> 20, of which waited for: 9 -> 4; matrix products, arithmetic and copies ran while one was open for 3% -> 3% of each run, Pallas kernels for 22% -> 31%
where the time goes in v3:
time: 211 us; the launch traced here: 210 us
  Pallas kernels  66 us (31%)
  starting transfers between devices  50.6 us (24%)
  waiting for transfers between devices  41.9 us (20%)
  blocking collectives  38.3 us (18%)
  local copies, waits for them, and re-layouts  11.9 us (6%)
    pallas_call x3, Pallas kernels, apply_terms(): pl.pallas_call(functools.partial(apply_kernel, at_ops, at_renewed, starts...  44.7 us
    all_to_all x2, blocking collectives, exchange(): return lax.all_to_all(value, 'op', 0, 0, axis_index_groups=groups)  38.3 us
    all_to_all x4, starting transfers between devices, exchange(): return lax.all_to_all(value, 'op', 0, 0, axis_index_groups=groups)  26.1 us
    ppermute x2, waiting for transfers between devices, shards(): lax.ppermute(value, 'sect', [(0, 1), (1, 0)]).reshape(4, STACK, BLOCK)  22.8 us
    pallas_call x2, Pallas kernels, renew(): pl.pallas_call(renew_kernel, grid_spec=grid_spec, out_shape=jax.ShapeDtyp...  14.4 us
    ppermute x1, waiting for transfers between devices, shards(): last = lax.ppermute(jnp.stack([second, moved]), 'op', TO_OWNERS)  11.5 us
    pallas_call x1, Pallas kernels, pack(): pl.pallas_call(pack_kernel, in_specs=[SMEM, SMEM, SMEM, SMEM, ANY, ANY],...  6.87 us
    ppermute x4, starting transfers between devices, shards(): passed = [lax.ppermute(passed[d], 'op', along(d, 1)) for d in (1, 2, 3, 0)]  5.27 us
  transfers between devices with their start and end apart: 20, of which 4 were waited for; matrix products, arithmetic and copies ran while one was open for 3% of the time, Pallas kernels for 31%

profile of v3, /device:TPU:120, one launch (start us, length us, event | category | flops | bytes accessed | tf_op | source)
XLA Modules:
  0.0 210.3 jit_solution(12259719689478460171)
XLA Ops:
  0.6 4.8 %collective-permute-start = (bf16[128,256]{1,0:T(8,128)(2,1)}, bf16[128,256]{1,0:T(8,128)(2,1)S(1)}, u32[]{:S(2)}, u32[]{:S(2)}) collective-permute-start(bf16[128,256]{1,0:T(8,128)(2,1)} %bitcast.40), channel_id=1, source_target_pairs={{0,0},{1,8},{2,22},{3,30},{4,36},{5,44},{6,50},{7,58},{8,1},{9,9},... | collective-permute-start | bytes 196616 | tf_op jit(solution)/shard_map/ppermute | solution.py:292
  5.4 0.6 pad_add_fusion.place
  6.0 7.2 %renew_kept.1 = bf16[4,3,256,256]{3,2,1,0:T(8,128)(2,1)} custom-call(s32[3]{0:T(128)} %pad_add_fusion.place, s32[8]{0:T(128)} %bitcast.37, bf16[1,3,8,256,256]{4,3,2,1,0:T(8,128)(2,1)} %left.5, bf16[1,8,4,256,256]{4,3,2,1,0:T(8,128)(2,1)} %tensor.3), custom_call_target="tpu_custom_call" | custom-call | flops 3221225472 | bytes 20971520 | tf_op jit(solution)/shard_map/renew_kept/pallas_call | solution.py:162
  13.2 0.0 collective-permute-done
  13.2 0.8 broadcast_in_dim.6
  14.1 6.8 %all-to-all-start = ((bf16[8,128,256]{2,1,0:T(8,128)(2,1)}), bf16[8,128,256]{2,1,0:T(8,128)(2,1)S(1)}, u32[]{:S(2)}, u32[]{:S(2)}) async-start(bf16[8,128,256]{2,1,0:T(8,128)(2,1)} %broadcast_in_dim.6), calls=%async_computation | async-start | bytes 1048576 | tf_op jit(solution)/shard_map/all_to_all | solution.py:57
  20.9 0.6 reshape.44.site
  21.5 6.9 %pack.1 = (bf16[4,1552,256]{2,1,0:T(8,128)(2,1)}, bf16[1552,256]{1,0:T(8,128)(2,1)}, bf16[1552,256]{1,0:T(8,128)(2,1)}, bf16[1552,256]{1,0:T(8,128)(2,1)}, bf16[1552,256]{1,0:T(8,128)(2,1)}) custom-call(s32[3]{0:T(128)} %pad_add_fusion.place, s32[8]{0:T(128)} %bitcast.38, f32[48]{0:T(128)} %reshape.44.site, s32[3]{0:T(128)} %bitcast.36, ...), custom_call_target="tpu_custom_call" | custom-call | flops 1048576 | bytes 65536 | tf_op jit(solution)/shard_map/pack/pallas_call | solution.py:111
  28.4 4.0 %all-to-all-done = bf16[8,128,256]{2,1,0:T(8,128)(2,1)S(1)} async-done(((bf16[8,128,256]{2,1,0:T(8,128)(2,1)}), bf16[8,128,256]{2,1,0:T(8,128)(2,1)S(1)}, u32[]{:S(2)}, u32[]{:S(2)}) %all-to-all-start) | async-done | bytes 524320 | tf_op jit(solution)/shard_map/all_to_all | solution.py:57
  32.4 0.8 copy-done.1
  33.2 3.7 %all-to-all-start.1 = ((bf16[4,1552,256]{2,1,0:T(8,128)(2,1)}), bf16[4,1552,256]{2,1,0:T(8,128)(2,1)S(1)}, u32[]{:S(2)}, u32[]{:S(2)}) async-start(bf16[4,1552,256]{2,1,0:T(8,128)(2,1)} %get-tuple-element.31), calls=%async_computation.1 | async-start | bytes 6356992 | tf_op jit(solution)/shard_map/all_to_all | solution.py:57
  36.9 0.9 collective-permute-start.5
  37.8 0.9 collective-permute-start.1
  38.7 3.0 %collective-permute-start.2 = (bf16[1552,256]{1,0:T(8,128)(2,1)}, bf16[1552,256]{1,0:T(8,128)(2,1)}, u32[]{:S(2)}, u32[]{:S(2)}) collective-permute-start(bf16[1552,256]{1,0:T(8,128)(2,1)} %get-tuple-element.33), channel_id=1, source_target_pairs={{0,33},{1,4},{2,35},{3,6},{4,37},{5,0},{6,39},{7,2},{8,41},{9,12},... | collective-permute-start | bytes 2383880 | tf_op jit(solution)/shard_map/ppermute | solution.py:307
  41.7 0.9 collective-permute-start.3
  42.6 0.5 collective-permute-start.4
  43.1 7.2 %renew_swapped.1 = bf16[4,3,256,256]{3,2,1,0:T(8,128)(2,1)} custom-call(s32[3]{0:T(128)} %pad_add_fusion.place, s32[8]{0:T(128)} %bitcast.39, bf16[1,3,8,256,256]{4,3,2,1,0:T(8,128)(2,1)} %left.5, bf16[1,8,4,256,256]{4,3,2,1,0:T(8,128)(2,1)} %tensor.3), custom_call_target="tpu_custom_call" | custom-call | flops 3221225472 | bytes 20971520 | tf_op jit(solution)/shard_map/renew_swapped/pallas_call | solution.py:162
  50.3 22.8 %collective-permute-done.5 = bf16[4,3,256,256]{3,2,1,0:T(8,128)(2,1)} collective-permute-done((bf16[4,3,256,256]{3,2,1,0:T(8,128)(2,1)}, bf16[4,3,256,256]{3,2,1,0:T(8,128)(2,1)}, u32[]{:S(2)}, u32[]{:S(2)}) %collective-permute-start.5) | collective-permute-done | bytes 1572896 | tf_op jit(solution)/shard_map/ppermute | solution.py:310
  73.1 1.7 collective-permute-start.10
  74.8 2.5 %fusion.1 = (bf16[1,3,256,256]{3,2,1,0:T(8,128)(2,1)}, bf16[1,3,256,256]{3,2,1,0:T(8,128)(2,1)}, bf16[1,3,256,256]{3,2,1,0:T(8,128)(2,1)}, bf16[1,3,256,256]{3,2,1,0:T(8,128)(2,1)}) fusion(bf16[4,3,256,256]{3,2,1,0:T(8,128)(2,1)} %collective-permute-done.5), kind=kLoop, calls=%fused_computation.3 | loop fusion | bytes 3145728 | tf_op jit(solution)/shard_map/slice | solution.py:313
  77.4 0.0 collective-permute-done.1.refs_1_
  77.4 1.4 collective-permute-start.8
  78.7 0.0 collective-permute-done.2.refs_2_
  78.7 1.8 collective-permute-start.7
  80.5 0.0 collective-permute-done.3.refs_3_
  80.5 0.0 collective-permute-start.6
  80.6 0.0 collective-permute-done.4.refs_4_
  80.6 0.0 all-to-all-done.1.refs_0_
  80.6 1.6 copy-done
  82.2 14.9 %apply_terms_8_0.2 = bf16[1024,256]{1,0:T(8,128)(2,1)} custom-call(s32[3]{0:T(128)} %pad_add_fusion.place, bf16[1024,256]{1,0:T(8,128)(2,1)} %bitcast.22, bf16[4,1552,256]{2,1,0:T(8,128)(2,1)} %copy-done, bf16[1552,256]{1,0:T(8,128)(2,1)} %collective-permute-done.1.refs_1_, bf16[1552,256]{1,0:T(8,128)(2,1)} %collective-permute-done.2.refs_2_, ...), custom_call_target="tpu_custom_call" | custom-call | flops 6442450944 | bytes 50331648 | tf_op jit(solution)/shard_map/apply_terms_8_0/pallas_call | solution.py:253
  97.1 0.0 collective-permute-done.8.refs_7_
  97.1 0.0 collective-permute-done.7.refs_6_
  97.1 0.0 collective-permute-done.6.refs_5_
  97.1 18.8 %all_to_all.30 = bf16[8,128,256]{2,1,0:T(8,128)(2,1)S(1)} all-to-all(bf16[8,128,256]{2,1,0:T(8,128)(2,1)} %bitcast.27), channel_id=1, replica_groups={{0,8,22,30,36,44,50,58},{1,9,23,31,37,45,51,59},{2,10,16,24,38,46,52,60..., dimensions={0} | all-to-all | bytes 1048576 | tf_op jit(solution)/shard_map/all_to_all | solution.py:57
  115.9 0.1 reduce_sum.36
  116.0 0.9 broadcast_in_dim.7
  116.8 6.2 %all-to-all-start.3 = ((bf16[8,128,256]{2,1,0:T(8,128)(2,1)}), bf16[8,128,256]{2,1,0:T(8,128)(2,1)S(1)}, u32[]{:S(2)}, u32[]{:S(2)}) async-start(bf16[8,128,256]{2,1,0:T(8,128)(2,1)} %broadcast_in_dim.7), calls=%async_computation.3 | async-start | bytes 1048576 | tf_op jit(solution)/shard_map/all_to_all | solution.py:57
  123.0 4.3 %collective-permute-start.9 = (bf16[128,256]{1,0:T(8,128)(2,1)S(1)}, bf16[128,256]{1,0:T(8,128)(2,1)S(1)}, u32[]{:S(2)}, u32[]{:S(2)}) collective-permute-start(bf16[128,256]{1,0:T(8,128)(2,1)S(1)} %reduce_sum.36), channel_id=1, source_target_pairs={{0,0},{8,1},{22,2},{30,3},{36,4},{44,5},{50,6},{58,7},{1,8},{9,9},... | collective-permute-start | bytes 196616 | tf_op jit(solution)/shard_map/ppermute | solution.py:318
  127.3 0.0 collective-permute-done.10
  127.3 1.5 fusion
  128.7 0.1 collective-permute-start.13
  128.8 1.2 collective-permute-start.14
  130.0 1.1 collective-permute-start.12
  131.1 0.0 collective-permute-start.11
  131.1 3.5 %collective-permute-done.9 = bf16[128,256]{1,0:T(8,128)(2,1)S(1)} collective-permute-done((bf16[128,256]{1,0:T(8,128)(2,1)S(1)}, bf16[128,256]{1,0:T(8,128)(2,1)S(1)}, u32[]{:S(2)}, u32[]{:S(2)}) %collective-permute-start.9) | collective-permute-done | bytes 65568 | tf_op jit(solution)/shard_map/ppermute | solution.py:318
  134.7 0.0 all-to-all-done.3
  134.7 0.8 copy-done.2
  135.5 14.8 %apply_terms_8_0.3 = bf16[1024,256]{1,0:T(8,128)(2,1)} custom-call(s32[3]{0:T(128)} %pad_add_fusion.place, bf16[1024,256]{1,0:T(8,128)(2,1)} %bitcast.24, bf16[4,1552,256]{2,1,0:T(8,128)(2,1)} %copy-done, bf16[1552,256]{1,0:T(8,128)(2,1)} %collective-permute-done.1.refs_1_, bf16[1552,256]{1,0:T(8,128)(2,1)} %collective-permute-done.2.refs_2_, ...), custom_call_target="tpu_custom_call" | custom-call | flops 6442450944 | bytes 50331648 | tf_op jit(solution)/shard_map/apply_terms_8_0/pallas_call | solution.py:253
  150.3 9.4 %all-to-all-start.4 = ((bf16[8,128,256]{2,1,0:T(8,128)(2,1)}), bf16[8,128,256]{2,1,0:T(8,128)(2,1)S(1)}, u32[]{:S(2)}, u32[]{:S(2)}) async-start(bf16[8,128,256]{2,1,0:T(8,128)(2,1)} %bitcast.25), calls=%async_computation.4 | async-start | bytes 1048576 | tf_op jit(solution)/shard_map/all_to_all | solution.py:57
  159.8 0.0 collective-permute-done.13.refs_11_
  159.8 0.0 collective-permute-done.14.refs_12_
  159.8 0.0 collective-permute-done.12.refs_10_
  159.8 0.0 collective-permute-done.11.refs_9_
  159.8 0.7 copy-done.4
  160.6 0.1 copy-done.5
  160.7 0.1 copy-done.6
  160.9 15.0 %apply_moved_8_0.1 = bf16[1024,256]{1,0:T(8,128)(2,1)} custom-call(s32[3]{0:T(128)} %pad_add_fusion.place, bf16[1024,256]{1,0:T(8,128)(2,1)} %bitcast.23, bf16[4,1552,256]{2,1,0:T(8,128)(2,1)} %copy-done, bf16[1552,256]{1,0:T(8,128)(2,1)} %collective-permute-done.1.refs_1_, bf16[1552,256]{1,0:T(8,128)(2,1)} %collective-permute-done.2.refs_2_, ...), custom_call_target="tpu_custom_call" | custom-call | flops 6442450944 | bytes 50331648 | tf_op jit(solution)/shard_map/apply_moved_8_0/pallas_call | solution.py:253
  175.9 0.1 reduce_sum.37
  175.9 19.5 %all_to_all.31 = bf16[8,128,256]{2,1,0:T(8,128)(2,1)S(1)} all-to-all(bf16[8,128,256]{2,1,0:T(8,128)(2,1)} %bitcast.26), channel_id=1, replica_groups={{0,8,22,30,36,44,50,58},{1,9,23,31,37,45,51,59},{2,10,16,24,38,46,52,60..., dimensions={0} | all-to-all | bytes 1048576 | tf_op jit(solution)/shard_map/all_to_all | solution.py:57
  195.5 0.1 reduce_sum.38
  195.6 1.9 collective-permute-start.15
  197.5 11.5 %collective-permute-done.15 = bf16[2,128,256]{2,1,0:T(8,128)(2,1)S(1)} collective-permute-done((bf16[2,128,256]{2,1,0:T(8,128)(2,1)S(1)}, bf16[2,128,256]{2,1,0:T(8,128)(2,1)S(1)}, u32[]{:S(2)}, u32[]{:S(2)}) %collective-permute-start.15) | collective-permute-done | bytes 131104 | tf_op jit(solution)/shard_map/ppermute | solution.py:325
  209.0 0.7 fusion.2
  209.7 0.6 copy.11
  (10 shorter events, 0.0 us)
Async XLA Ops:
  0.6 12.6 %collective-permute-start = (bf16[128,256]{1,0:T(8,128)(2,1)}, bf16[128,256]{1,0:T(8,128)(2,1)S(1)}, u32[]{:S(2)}, u32[]{:S(2)}) collective-permute-start(bf16[128,256]{1,0:T(8,128)(2,1)} %bitcast.40), channel_id=1, source_target_pairs={{0,0},{1,8},{2,22},{3,30},{4,36},{5,44},{6,50},{7,58},{8,1},{9,9},... | collective-permute-start | bytes 196616 | tf_op jit(solution)/shard_map/ppermute | solution.py:292
  13.2 7.7 %copy-start.3 = (f32[1,3,4,4]{3,2,1,0:T(4,128)S(1)}, f32[1,3,4,4]{3,2,1,0:T(4,128)}, u32[]{:S(2)}) copy-start(f32[1,3,4,4]{3,2,1,0:T(4,128)} %param.10) | copy-start | bytes 580
  14.1 18.3 %all-to-all-start = ((bf16[8,128,256]{2,1,0:T(8,128)(2,1)}), bf16[8,128,256]{2,1,0:T(8,128)(2,1)S(1)}, u32[]{:S(2)}, u32[]{:S(2)}) async-start(bf16[8,128,256]{2,1,0:T(8,128)(2,1)} %broadcast_in_dim.6), calls=%async_computation | async-start | bytes 1048576 | tf_op jit(solution)/shard_map/all_to_all | solution.py:57
  32.4 0.8 copy-start.1
  33.2 47.3 %all-to-all-start.1 = ((bf16[4,1552,256]{2,1,0:T(8,128)(2,1)}), bf16[4,1552,256]{2,1,0:T(8,128)(2,1)S(1)}, u32[]{:S(2)}, u32[]{:S(2)}) async-start(bf16[4,1552,256]{2,1,0:T(8,128)(2,1)} %get-tuple-element.31), calls=%async_computation.1 | async-start | bytes 6356992 | tf_op jit(solution)/shard_map/all_to_all | solution.py:57
  36.9 36.2 %collective-permute-start.5 = (bf16[4,3,256,256]{3,2,1,0:T(8,128)(2,1)}, bf16[4,3,256,256]{3,2,1,0:T(8,128)(2,1)}, u32[]{:S(2)}, u32[]{:S(2)}) collective-permute-start(bf16[4,3,256,256]{3,2,1,0:T(8,128)(2,1)} %renew_kept.1), channel_id=1, source_target_pairs={{0,64},{64,0},{1,65},{65,1},{2,66},{66,2},{3,67},{67,3},{4,68},{68... | collective-permute-start | bytes 4718600 | tf_op jit(solution)/shard_map/ppermute | solution.py:310
  37.8 39.6 %collective-permute-start.1 = (bf16[1552,256]{1,0:T(8,128)(2,1)}, bf16[1552,256]{1,0:T(8,128)(2,1)}, u32[]{:S(2)}, u32[]{:S(2)}) collective-permute-start(bf16[1552,256]{1,0:T(8,128)(2,1)} %get-tuple-element.32), channel_id=1, source_target_pairs={{0,17},{1,2},{2,19},{3,4},{4,21},{5,6},{6,23},{7,0},{8,25},{9,10},... | collective-permute-start | bytes 2383880 | tf_op jit(solution)/shard_map/ppermute | solution.py:307
  38.7 40.1 %collective-permute-start.2 = (bf16[1552,256]{1,0:T(8,128)(2,1)}, bf16[1552,256]{1,0:T(8,128)(2,1)}, u32[]{:S(2)}, u32[]{:S(2)}) collective-permute-start(bf16[1552,256]{1,0:T(8,128)(2,1)} %get-tuple-element.33), channel_id=1, source_target_pairs={{0,33},{1,4},{2,35},{3,6},{4,37},{5,0},{6,39},{7,2},{8,41},{9,12},... | collective-permute-start | bytes 2383880 | tf_op jit(solution)/shard_map/ppermute | solution.py:307
  41.7 38.9 %collective-permute-start.3 = (bf16[1552,256]{1,0:T(8,128)(2,1)}, bf16[1552,256]{1,0:T(8,128)(2,1)}, u32[]{:S(2)}, u32[]{:S(2)}) collective-permute-start(bf16[1552,256]{1,0:T(8,128)(2,1)} %get-tuple-element.34), channel_id=1, source_target_pairs={{0,49},{1,6},{2,51},{3,0},{4,53},{5,2},{6,55},{7,4},{8,57},{9,14},... | collective-permute-start | bytes 2383880 | tf_op jit(solution)/shard_map/ppermute | solution.py:307
  42.6 38.0 %collective-permute-start.4 = (bf16[1552,256]{1,0:T(8,128)(2,1)}, bf16[1552,256]{1,0:T(8,128)(2,1)}, u32[]{:S(2)}, u32[]{:S(2)}) collective-permute-start(bf16[1552,256]{1,0:T(8,128)(2,1)} %get-tuple-element.35), channel_id=1, source_target_pairs={{0,1},{1,0},{2,3},{3,2},{4,5},{5,4},{6,7},{7,6},{8,9},{9,8},{10,11... | collective-permute-start | bytes 2383880 | tf_op jit(solution)/shard_map/ppermute | solution.py:307
  73.1 54.2 %collective-permute-start.10 = (bf16[4,3,256,256]{3,2,1,0:T(8,128)(2,1)}, bf16[4,3,256,256]{3,2,1,0:T(8,128)(2,1)}, u32[]{:S(2)}, u32[]{:S(2)}) collective-permute-start(bf16[4,3,256,256]{3,2,1,0:T(8,128)(2,1)} %renew_swapped.1), channel_id=1, source_target_pairs={{0,64},{64,0},{1,65},{65,1},{2,66},{66,2},{3,67},{67,3},{4,68},{68... | collective-permute-start | bytes 4718600 | tf_op jit(solution)/shard_map/ppermute | solution.py:310
  77.4 19.7 %collective-permute-start.8 = (bf16[768,256]{1,0:T(8,128)(2,1)}, bf16[768,256]{1,0:T(8,128)(2,1)}, u32[]{:S(2)}, u32[]{:S(2)}) collective-permute-start(bf16[768,256]{1,0:T(8,128)(2,1)} %bitcast.9), channel_id=1, source_target_pairs={{0,48},{1,7},{2,50},{3,1},{4,52},{5,3},{6,54},{7,5},{8,56},{9,15},... | collective-permute-start | bytes 1179656 | tf_op jit(solution)/shard_map/ppermute | solution.py:313
  78.7 18.4 %collective-permute-start.7 = (bf16[768,256]{1,0:T(8,128)(2,1)}, bf16[768,256]{1,0:T(8,128)(2,1)}, u32[]{:S(2)}, u32[]{:S(2)}) collective-permute-start(bf16[768,256]{1,0:T(8,128)(2,1)} %bitcast.8), channel_id=1, source_target_pairs={{0,32},{1,5},{2,34},{3,7},{4,36},{5,1},{6,38},{7,3},{8,40},{9,13},... | collective-permute-start | bytes 1179656 | tf_op jit(solution)/shard_map/ppermute | solution.py:313
  80.5 16.6 %collective-permute-start.6 = (bf16[768,256]{1,0:T(8,128)(2,1)}, bf16[768,256]{1,0:T(8,128)(2,1)}, u32[]{:S(2)}, u32[]{:S(2)}) collective-permute-start(bf16[768,256]{1,0:T(8,128)(2,1)} %bitcast.7), channel_id=1, source_target_pairs={{0,16},{1,3},{2,18},{3,5},{4,20},{5,7},{6,22},{7,1},{8,24},{9,11},... | collective-permute-start | bytes 1179656 | tf_op jit(solution)/shard_map/ppermute | solution.py:313
  80.6 1.6 copy-start
  116.8 17.9 %all-to-all-start.3 = ((bf16[8,128,256]{2,1,0:T(8,128)(2,1)}), bf16[8,128,256]{2,1,0:T(8,128)(2,1)S(1)}, u32[]{:S(2)}, u32[]{:S(2)}) async-start(bf16[8,128,256]{2,1,0:T(8,128)(2,1)} %broadcast_in_dim.7), calls=%async_computation.3 | async-start | bytes 1048576 | tf_op jit(solution)/shard_map/all_to_all | solution.py:57
  123.0 11.7 %collective-permute-start.9 = (bf16[128,256]{1,0:T(8,128)(2,1)S(1)}, bf16[128,256]{1,0:T(8,128)(2,1)S(1)}, u32[]{:S(2)}, u32[]{:S(2)}) collective-permute-start(bf16[128,256]{1,0:T(8,128)(2,1)S(1)} %reduce_sum.36), channel_id=1, source_target_pairs={{0,0},{8,1},{22,2},{30,3},{36,4},{44,5},{50,6},{58,7},{1,8},{9,9},... | collective-permute-start | bytes 196616 | tf_op jit(solution)/shard_map/ppermute | solution.py:318
  128.7 31.0 %collective-permute-start.13 = (bf16[768,256]{1,0:T(8,128)(2,1)S(1)}, bf16[768,256]{1,0:T(8,128)(2,1)S(1)}, u32[]{:S(2)}, u32[]{:S(2)}) collective-permute-start(bf16[768,256]{1,0:T(8,128)(2,1)S(1)} %bitcast.32), channel_id=1, source_target_pairs={{0,49},{1,6},{2,51},{3,0},{4,53},{5,2},{6,55},{7,4},{8,57},{9,14},... | collective-permute-start | bytes 1179656 | tf_op jit(solution)/shard_map/ppermute | solution.py:314
  128.8 31.0 %collective-permute-start.14 = (bf16[768,256]{1,0:T(8,128)(2,1)S(1)}, bf16[768,256]{1,0:T(8,128)(2,1)S(1)}, u32[]{:S(2)}, u32[]{:S(2)}) collective-permute-start(bf16[768,256]{1,0:T(8,128)(2,1)S(1)} %bitcast.31), channel_id=1, source_target_pairs={{0,1},{1,0},{2,3},{3,2},{4,5},{5,4},{6,7},{7,6},{8,9},{9,8},{10,11... | collective-permute-start | bytes 1179656 | tf_op jit(solution)/shard_map/ppermute | solution.py:314
  130.0 29.8 %collective-permute-start.12 = (bf16[768,256]{1,0:T(8,128)(2,1)S(1)}, bf16[768,256]{1,0:T(8,128)(2,1)S(1)}, u32[]{:S(2)}, u32[]{:S(2)}) collective-permute-start(bf16[768,256]{1,0:T(8,128)(2,1)S(1)} %bitcast.30), channel_id=1, source_target_pairs={{0,33},{1,4},{2,35},{3,6},{4,37},{5,0},{6,39},{7,2},{8,41},{9,12},... | collective-permute-start | bytes 1179656 | tf_op jit(solution)/shard_map/ppermute | solution.py:314
  131.1 28.7 %collective-permute-start.11 = (bf16[768,256]{1,0:T(8,128)(2,1)S(1)}, bf16[768,256]{1,0:T(8,128)(2,1)}, u32[]{:S(2)}, u32[]{:S(2)}) collective-permute-start(bf16[768,256]{1,0:T(8,128)(2,1)S(1)} %bitcast.29), channel_id=1, source_target_pairs={{0,17},{1,2},{2,19},{3,4},{4,21},{5,6},{6,23},{7,0},{8,25},{9,10},... | collective-permute-start | bytes 1179656 | tf_op jit(solution)/shard_map/ppermute | solution.py:314
  134.7 0.8 copy-start.2
  150.3 25.5 %all-to-all-start.4 = ((bf16[8,128,256]{2,1,0:T(8,128)(2,1)}), bf16[8,128,256]{2,1,0:T(8,128)(2,1)S(1)}, u32[]{:S(2)}, u32[]{:S(2)}) async-start(bf16[8,128,256]{2,1,0:T(8,128)(2,1)} %bitcast.25), calls=%async_computation.4 | async-start | bytes 1048576 | tf_op jit(solution)/shard_map/all_to_all | solution.py:57
  159.8 0.8 copy-start.4
  159.8 0.9 copy-start.5
  159.8 1.0 copy-start.6
  195.6 13.4 %collective-permute-start.15 = (bf16[2,128,256]{2,1,0:T(8,128)(2,1)S(1)}, bf16[2,128,256]{2,1,0:T(8,128)(2,1)S(1)}, u32[]{:S(2)}, u32[]{:S(2)}) collective-permute-start(bf16[2,128,256]{2,1,0:T(8,128)(2,1)S(1)} %pad_maximum_fusion), channel_id=1, source_target_pairs={{0,0},{8,1},{22,2},{30,3},{36,4},{44,5},{50,6},{58,7},{1,8},{9,9},... | collective-permute-start | bytes 393224 | tf_op jit(solution)/shard_map/ppermute | solution.py:325

commit v4 on v3

--- a/solution.py
+++ b/solution.py
@@ -170,9 +170,8 @@
     )(place, pair, left_ops, tensor)
 
 
-def apply_kernel(groups, renewed, starts, place, field, *refs):
+def apply_kernel(groups, renewed, starts, joins, place, field, *refs):
     out, left_buf, right_buf, mix_buf, total, sems = refs[-6:]
-    start = refs[-7] if starts else None
 
     here = jnp.where(place[2] == 0, place[0], place[1])
 
@@ -196,7 +195,7 @@
     for i in range(len(groups)):
         for copy in copies(i, i):
             copy.start()
-    total[...] = start[...] if starts else jnp.zeros_like(total)
+    total[...] = refs[-7 - joins][...] if starts else jnp.zeros_like(total)
 
     def body(g, carry):
         for copy in copies(0, g):
@@ -231,7 +230,14 @@
         return carry
 
     lax.fori_loop(0, len(groups), body, 0)
-    out[...] = total[...].astype(out.dtype)
+    if joins:
+        other = refs[-7]
+        for k in range(8):
+            rows = slice(k * CHUNK, (k + 1) * CHUNK)
+            out[k, 0] = other[rows]
+            out[k, 1] = total[rows].astype(BF16)
+    else:
+        out[...] = total[...].astype(out.dtype)
 
 
 def listed(arrays, base, distances):
@@ -244,17 +250,19 @@
     return out
 
 
-def apply_terms(place, field, ops, renewed=(), start=None, kind=BF16):
+def apply_terms(place, field, ops, renewed=(), start=None, other=None, kind=BF16):
     at_ops = listed(ops, 0, bool(renewed))
     groups = len(at_ops)
     at_renewed = listed(renewed, len(ops), False)
-    starts = start is not None
+    starts, joins = start is not None, other is not None
+    extra = [value for value in (start, other) if value is not None]
+    shape = (8, 2, CHUNK, BLOCK) if joins else (LOCAL * BLOCK, BLOCK)
     name = "apply_moved" if renewed else "apply_terms"
     return pl.pallas_call(
-        functools.partial(apply_kernel, at_ops, at_renewed, starts),
-        in_specs=[SMEM, VMEM] + [ANY] * (len(ops) + len(renewed)) + [VMEM] * starts,
+        functools.partial(apply_kernel, at_ops, at_renewed, starts, joins),
+        in_specs=[SMEM, VMEM] + [ANY] * (len(ops) + len(renewed)) + [VMEM] * len(extra),
         out_specs=VMEM,
-        out_shape=jax.ShapeDtypeStruct((LOCAL * BLOCK, BLOCK), kind),
+        out_shape=jax.ShapeDtypeStruct(shape, kind),
         scratch_shapes=[
             pltpu.VMEM((groups, STACK, BLOCK), BF16),
             pltpu.VMEM((groups, STACK, BLOCK), BF16),
@@ -263,15 +271,15 @@
             pltpu.SemaphoreType.DMA((groups, 3)),
         ],
         compiler_params=pltpu.CompilerParams(vmem_limit_bytes=60 << 20),
-        name=f"{name}_{groups}_{int(starts)}",
+        name=f"{name}_{groups}",
         cost_estimate=pl.CostEstimate(
             flops=3 * groups * 8 * 2 * BLOCK**3, bytes_accessed=48 << 20, transcendentals=0
         ),
-    )(place, field, *ops, *renewed, *([start] if starts else []))
+    )(place, field, *ops, *renewed, *extra)
 
 
 def reduce_chunks(partial):
-    parts = exchange(partial.reshape(8, CHUNK, BLOCK), HOLDERS)
+    parts = exchange(partial, HOLDERS)
     return jnp.sum(parts.astype(F32), axis=0).astype(BF16)
 
 
@@ -314,16 +322,15 @@
     far = [lax.ppermute(far[d], "op", along(d, 1)) for d in (1, 2, 3, 0)]
 
     partial = apply_terms(place, field, [kept, *passed])
-    first = reduce_chunks(after(partial, *near))
-    first_own = lax.ppermute(first, "op", TO_OWNERS)
-    first_field, first_own = lax.optimization_barrier((spread(first), first_own))
+    half = apply_terms(place, field, [kept], near, kind=F32)
+    first = reduce_chunks(after(partial, *near).reshape(8, 1, CHUNK, BLOCK))
+    first, half = lax.optimization_barrier((first, half))
+    first_field = spread(first[0])
     partial = apply_terms(place, first_field, [kept, *passed])
-    second = reduce_chunks(partial)
-
-    partial = apply_terms(place, after(field, partial), [kept, *passed], near + far)
-    moved = reduce_chunks(after(partial, second))
-    last = lax.ppermute(jnp.stack([second, moved]), "op", TO_OWNERS)
-    return first_own[None], last[0:1], last[1:2]
+    partial = apply_terms(place, after(field, partial), passed, far, half, partial)
+    images = jnp.concatenate([first, reduce_chunks(partial)])
+    images = lax.ppermute(images, "op", TO_OWNERS)
+    return images[0:1], images[1:2], images[2:3]
 
 
 def solution(mesh):

time: 211 us -> 200 us (0.948)
  blocking collectives: 38.3 us -> 21.8 us
  Pallas kernels: 66 us -> 69.8 us
    all_to_all x2 -> x1, blocking collectives: 38.3 us -> 21.8 us  [exchange(): return lax.all_to_all(value, 'op', 0, 0, axis_index_groups=groups)]
    ppermute x2 -> x1, starting transfers between devices: 6.21 us -> 1.92 us  [shards(): images = lax.ppermute(images, 'op', TO_OWNERS)]
    ppermute x4, starting transfers between devices: 2.39 us -> 6.4 us  [shards(): far = [lax.ppermute(far[d], 'op', along(d, 1)) for d in (1, 2, 3, 0)]]
    pallas_call x3 -> x4, Pallas kernels: 44.7 us -> 48.5 us  [apply_terms(): pl.pallas_call(functools.partial(apply_kernel, at_ops, at_renewed, starts...]
    all_to_all x4, waiting for transfers between devices: 4.01 us -> 7.53 us  [exchange(): return lax.all_to_all(value, 'op', 0, 0, axis_index_groups=groups)]
    ppermute x2 -> x1, waiting for transfers between devices: 15 us -> 12.9 us  [shards(): images = lax.ppermute(images, 'op', TO_OWNERS)]
    unnamed x15 -> x14, local copies, waits for them, and re-layouts: 4.93 us -> 4.25 us
  transfers between devices with their start and end apart: 20 -> 19, of which waited for: 4 -> 5; matrix products, arithmetic and copies ran while one was open for 3% -> 3% of each run, Pallas kernels for 31% -> 30%
where the time goes in v4:
time: 200 us; the launch traced here: 199 us
  Pallas kernels  69.8 us (35%)
  starting transfers between devices  51.1 us (26%)
  waiting for transfers between devices  43.3 us (22%)
  blocking collectives  21.8 us (11%)
  local copies, waits for them, and re-layouts  11.2 us (6%)
    pallas_call x4, Pallas kernels, apply_terms(): pl.pallas_call(functools.partial(apply_kernel, at_ops, at_renewed, starts...  48.5 us
    all_to_all x4, starting transfers between devices, exchange(): return lax.all_to_all(value, 'op', 0, 0, axis_index_groups=groups)  26.1 us
    ppermute x2, waiting for transfers between devices, shards(): lax.ppermute(value, 'sect', [(0, 1), (1, 0)]).reshape(4, STACK, BLOCK)  22.8 us
    all_to_all x1, blocking collectives, exchange(): return lax.all_to_all(value, 'op', 0, 0, axis_index_groups=groups)  21.8 us
    pallas_call x2, Pallas kernels, renew(): pl.pallas_call(renew_kernel, grid_spec=grid_spec, out_shape=jax.ShapeDtyp...  14.4 us
    ppermute x1, waiting for transfers between devices, shards(): images = lax.ppermute(images, 'op', TO_OWNERS)  12.9 us
    all_to_all x4, waiting for transfers between devices, exchange(): return lax.all_to_all(value, 'op', 0, 0, axis_index_groups=groups)  7.53 us
    pallas_call x1, Pallas kernels, pack(): pl.pallas_call(pack_kernel, in_specs=[SMEM, SMEM, SMEM, SMEM, ANY, ANY],...  6.83 us
  transfers between devices with their start and end apart: 19, of which 5 were waited for; matrix products, arithmetic and copies ran while one was open for 3% of the time, Pallas kernels for 30%

profile of v4, /device:TPU:120, one launch (start us, length us, event | category | flops | bytes accessed | tf_op | source)
XLA Modules:
  0.0 198.8 jit_solution(12641290717027064792)
XLA Ops:
  0.6 4.8 %collective-permute-start = (bf16[128,256]{1,0:T(8,128)(2,1)}, bf16[128,256]{1,0:T(8,128)(2,1)S(1)}, u32[]{:S(2)}, u32[]{:S(2)}) collective-permute-start(bf16[128,256]{1,0:T(8,128)(2,1)} %bitcast.36), channel_id=1, source_target_pairs={{0,0},{1,8},{2,22},{3,30},{4,36},{5,44},{6,50},{7,58},{8,1},{9,9},... | collective-permute-start | bytes 196616 | tf_op jit(solution)/shard_map/ppermute | solution.py:300
  5.4 0.6 pad_add_fusion.place
  6.0 7.2 %renew_kept.1 = bf16[4,3,256,256]{3,2,1,0:T(8,128)(2,1)} custom-call(s32[3]{0:T(128)} %pad_add_fusion.place, s32[8]{0:T(128)} %bitcast.33, bf16[1,3,8,256,256]{4,3,2,1,0:T(8,128)(2,1)} %left.5, bf16[1,8,4,256,256]{4,3,2,1,0:T(8,128)(2,1)} %tensor.3), custom_call_target="tpu_custom_call" | custom-call | flops 3221225472 | bytes 20971520 | tf_op jit(solution)/shard_map/renew_kept/pallas_call | solution.py:162
  13.2 0.0 collective-permute-done
  13.2 0.8 broadcast_in_dim.6
  14.0 6.8 %all-to-all-start = ((bf16[8,128,256]{2,1,0:T(8,128)(2,1)}), bf16[8,128,256]{2,1,0:T(8,128)(2,1)S(1)}, u32[]{:S(2)}, u32[]{:S(2)}) async-start(bf16[8,128,256]{2,1,0:T(8,128)(2,1)} %broadcast_in_dim.6), calls=%async_computation | async-start | bytes 1048576 | tf_op jit(solution)/shard_map/all_to_all | solution.py:57
  20.9 0.0 copy-done.3
  20.9 0.6 reshape.38.site
  21.5 6.8 %pack.1 = (bf16[4,1552,256]{2,1,0:T(8,128)(2,1)}, bf16[1552,256]{1,0:T(8,128)(2,1)}, bf16[1552,256]{1,0:T(8,128)(2,1)}, bf16[1552,256]{1,0:T(8,128)(2,1)}, bf16[1552,256]{1,0:T(8,128)(2,1)}) custom-call(s32[3]{0:T(128)} %pad_add_fusion.place, s32[8]{0:T(128)} %bitcast.34, f32[48]{0:T(128)} %reshape.38.site, s32[3]{0:T(128)} %bitcast.32, ...), custom_call_target="tpu_custom_call" | custom-call | flops 1048576 | bytes 65536 | tf_op jit(solution)/shard_map/pack/pallas_call | solution.py:111
  28.3 4.0 %all-to-all-done = bf16[8,128,256]{2,1,0:T(8,128)(2,1)S(1)} async-done(((bf16[8,128,256]{2,1,0:T(8,128)(2,1)}), bf16[8,128,256]{2,1,0:T(8,128)(2,1)S(1)}, u32[]{:S(2)}, u32[]{:S(2)}) %all-to-all-start) | async-done | bytes 524320 | tf_op jit(solution)/shard_map/all_to_all | solution.py:57
  32.4 0.8 copy-done.1
  33.2 3.7 %all-to-all-start.1 = ((bf16[4,1552,256]{2,1,0:T(8,128)(2,1)}), bf16[4,1552,256]{2,1,0:T(8,128)(2,1)S(1)}, u32[]{:S(2)}, u32[]{:S(2)}) async-start(bf16[4,1552,256]{2,1,0:T(8,128)(2,1)} %get-tuple-element.30), calls=%async_computation.1 | async-start | bytes 6356992 | tf_op jit(solution)/shard_map/all_to_all | solution.py:57
  36.9 0.9 collective-permute-start.5
  37.8 0.7 collective-permute-start.1
  38.4 3.2 %collective-permute-start.2 = (bf16[1552,256]{1,0:T(8,128)(2,1)}, bf16[1552,256]{1,0:T(8,128)(2,1)}, u32[]{:S(2)}, u32[]{:S(2)}) collective-permute-start(bf16[1552,256]{1,0:T(8,128)(2,1)} %get-tuple-element.32), channel_id=1, source_target_pairs={{0,33},{1,4},{2,35},{3,6},{4,37},{5,0},{6,39},{7,2},{8,41},{9,12},... | collective-permute-start | bytes 2383880 | tf_op jit(solution)/shard_map/ppermute | solution.py:315
  41.6 0.9 collective-permute-start.3
  42.6 0.5 collective-permute-start.4
  43.0 7.2 %renew_swapped.1 = bf16[4,3,256,256]{3,2,1,0:T(8,128)(2,1)} custom-call(s32[3]{0:T(128)} %pad_add_fusion.place, s32[8]{0:T(128)} %bitcast.35, bf16[1,3,8,256,256]{4,3,2,1,0:T(8,128)(2,1)} %left.5, bf16[1,8,4,256,256]{4,3,2,1,0:T(8,128)(2,1)} %tensor.3), custom_call_target="tpu_custom_call" | custom-call | flops 3221225472 | bytes 20971520 | tf_op jit(solution)/shard_map/renew_swapped/pallas_call | solution.py:162
  50.2 22.8 %collective-permute-done.5 = bf16[4,3,256,256]{3,2,1,0:T(8,128)(2,1)} collective-permute-done((bf16[4,3,256,256]{3,2,1,0:T(8,128)(2,1)}, bf16[4,3,256,256]{3,2,1,0:T(8,128)(2,1)}, u32[]{:S(2)}, u32[]{:S(2)}) %collective-permute-start.5) | collective-permute-done | bytes 1572896 | tf_op jit(solution)/shard_map/ppermute | solution.py:318
  73.1 1.7 collective-permute-start.9
  74.8 2.5 %fusion.1 = (bf16[1,3,256,256]{3,2,1,0:T(8,128)(2,1)}, bf16[1,3,256,256]{3,2,1,0:T(8,128)(2,1)}, bf16[1,3,256,256]{3,2,1,0:T(8,128)(2,1)}, bf16[1,3,256,256]{3,2,1,0:T(8,128)(2,1)}) fusion(bf16[4,3,256,256]{3,2,1,0:T(8,128)(2,1)} %collective-permute-done.5), kind=kLoop, calls=%fused_computation.3 | loop fusion | bytes 3145728 | tf_op jit(solution)/shard_map/slice | solution.py:321
  77.3 0.0 collective-permute-done.1.refs_1_.refs_0_
  77.3 0.9 collective-permute-start.6
  78.2 0.0 collective-permute-done.2.refs_2_.refs_1_
  78.2 1.8 collective-permute-start.7
  80.1 0.0 collective-permute-done.3.refs_3_.refs_2_
  80.1 1.3 collective-permute-start.8
  81.4 0.0 collective-permute-done.4.refs_4_.refs_3_
  81.4 0.0 all-to-all-done.1.refs_0_
  81.4 1.6 copy-done
  83.1 14.9 %apply_terms_8.2 = bf16[1024,256]{1,0:T(8,128)(2,1)} custom-call(s32[3]{0:T(128)} %pad_add_fusion.place, bf16[1024,256]{1,0:T(8,128)(2,1)} %bitcast.22, bf16[4,1552,256]{2,1,0:T(8,128)(2,1)} %copy-done, bf16[1552,256]{1,0:T(8,128)(2,1)} %collective-permute-done.1.refs_1_.refs_0_, bf16[1552,256]{1,0:T(8,128)(2,1)} %collective-permute-done.2.refs_2_.refs_1_, ...), custom_call_target="tpu_custom_call" | custom-call | flops 6442450944 | bytes 50331648 | tf_op jit(solution)/shard_map/apply_terms_8/pallas_call | solution.py:261
  97.9 0.0 collective-permute-done.6.refs_1_
  97.9 0.0 collective-permute-done.7.refs_2_
  97.9 0.0 collective-permute-done.8.refs_3_
  98.0 7.2 %all-to-all-start.2 = ((bf16[8,1,128,256]{3,2,1,0:T(8,128)(2,1)}), bf16[8,1,128,256]{3,2,1,0:T(8,128)(2,1)S(1)}, u32[]{:S(2)}, u32[]{:S(2)}) async-start(bf16[8,1,128,256]{3,2,1,0:T(8,128)(2,1)} %bitcast.26), calls=%async_computation.2 | async-start | bytes 1048576 | tf_op jit(solution)/shard_map/all_to_all | solution.py:57
  105.2 9.2 %apply_moved_4.2.refs_8_ = f32[1024,256]{1,0:T(8,128)} custom-call(s32[3]{0:T(128)} %pad_add_fusion.place, bf16[1024,256]{1,0:T(8,128)(2,1)} %bitcast.23, bf16[4,1552,256]{2,1,0:T(8,128)(2,1)} %copy-done, bf16[768,256]{1,0:T(8,128)(2,1)} %collective-permute-done.6.refs_1_, bf16[768,256]{1,0:T(8,128)(2,1)} %collective-permute-done.7.refs_2_, ...), custom_call_target="tpu_custom_call" | custom-call | flops 3221225472 | bytes 50331648 | tf_op jit(solution)/shard_map/apply_moved_4/pallas_call | solution.py:261
  114.4 1.3 all-to-all-done.2
  115.7 0.1 reduce_sum.26
  115.7 0.9 broadcast_in_dim.15
  116.6 8.3 %all-to-all-start.3 = ((bf16[8,128,256]{2,1,0:T(8,128)(2,1)}), bf16[8,128,256]{2,1,0:T(8,128)(2,1)S(1)}, u32[]{:S(2)}, u32[]{:S(2)}) async-start(bf16[8,128,256]{2,1,0:T(8,128)(2,1)} %broadcast_in_dim.15), calls=%async_computation.3 | async-start | bytes 1048576 | tf_op jit(solution)/shard_map/all_to_all | solution.py:57
  124.9 0.0 collective-permute-done.9
  124.9 1.5 fusion
  126.4 0.1 collective-permute-start.10
  126.5 4.5 %collective-permute-start.11 = (bf16[768,256]{1,0:T(8,128)(2,1)S(1)}, bf16[768,256]{1,0:T(8,128)(2,1)S(1)}, u32[]{:S(2)}, u32[]{:S(2)}) collective-permute-start(bf16[768,256]{1,0:T(8,128)(2,1)S(1)} %bitcast.30), channel_id=1, source_target_pairs={{0,33},{1,4},{2,35},{3,6},{4,37},{5,0},{6,39},{7,2},{8,41},{9,12},... | collective-permute-start | bytes 1179656 | tf_op jit(solution)/shard_map/ppermute | solution.py:322
  130.9 1.0 collective-permute-start.12
  131.9 0.9 collective-permute-start.13
  132.8 2.2 %all-to-all-done.3 = bf16[8,128,256]{2,1,0:T(8,128)(2,1)S(1)} async-done(((bf16[8,128,256]{2,1,0:T(8,128)(2,1)}), bf16[8,128,256]{2,1,0:T(8,128)(2,1)S(1)}, u32[]{:S(2)}, u32[]{:S(2)}) %all-to-all-start.3) | async-done | bytes 524320 | tf_op jit(solution)/shard_map/all_to_all | solution.py:57
  135.0 0.8 copy-done.2
  135.8 14.9 %apply_terms_8.3.refs_9_ = bf16[1024,256]{1,0:T(8,128)(2,1)} custom-call(s32[3]{0:T(128)} %pad_add_fusion.place, bf16[1024,256]{1,0:T(8,128)(2,1)} %bitcast.25, bf16[4,1552,256]{2,1,0:T(8,128)(2,1)} %copy-done, bf16[1552,256]{1,0:T(8,128)(2,1)} %collective-permute-done.1.refs_1_.refs_0_, bf16[1552,256]{1,0:T(8,128)(2,1)} %collective-permute-done.2.refs_2_.refs_1_, ...), custom_call_target="tpu_custom_call" | custom-call | flops 6442450944 | bytes 50331648 | tf_op jit(solution)/shard_map/apply_terms_8/pallas_call | solution.py:261
  150.6 0.0 collective-permute-done.10.refs_4_
  150.6 0.0 copy-start.4
  150.7 0.0 collective-permute-done.11.refs_5_
  150.7 0.0 collective-permute-done.12.refs_6_
  150.7 0.0 copy-start.6
  150.7 0.0 collective-permute-done.13.refs_7_
  150.7 0.7 copy-done.4
  151.4 0.1 copy-done.5
  151.5 0.2 copy-done.6
  151.7 9.6 %apply_moved_4.3 = bf16[8,2,128,256]{3,2,1,0:T(8,128)(2,1)} custom-call(s32[3]{0:T(128)} %pad_add_fusion.place, bf16[1024,256]{1,0:T(8,128)(2,1)} %bitcast.24, bf16[1552,256]{1,0:T(8,128)(2,1)} %collective-permute-done.1.refs_1_.refs_0_, bf16[1552,256]{1,0:T(8,128)(2,1)} %collective-permute-done.2.refs_2_.refs_1_, ...), custom_call_target="tpu_custom_call" | custom-call | flops 3221225472 | bytes 50331648 | tf_op jit(solution)/shard_map/apply_moved_4/pallas_call | solution.py:261
  161.3 21.8 %all_to_all.25 = bf16[8,2,128,256]{3,2,1,0:T(8,128)(2,1)S(1)} all-to-all(bf16[8,2,128,256]{3,2,1,0:T(8,128)(2,1)} %apply_moved_4.3), channel_id=1, replica_groups={{0,8,22,30,36,44,50,58},{1,9,23,31,37,45,51,59},{2,10,16,24,38,46,52,60..., dimensions={0} | all-to-all | bytes 2097152 | tf_op jit(solution)/shard_map/all_to_all | solution.py:57
  183.1 0.1 reduce_sum.28
  183.3 1.9 collective-permute-start.14
  185.2 12.9 %collective-permute-done.14 = bf16[3,128,256]{2,1,0:T(8,128)(2,1)S(1)} collective-permute-done((bf16[3,128,256]{2,1,0:T(8,128)(2,1)S(1)}, bf16[3,128,256]{2,1,0:T(8,128)(2,1)S(1)}, u32[]{:S(2)}, u32[]{:S(2)}) %collective-permute-start.14) | collective-permute-done | bytes 196640 | tf_op jit(solution)/shard_map/ppermute | solution.py:332
  198.1 0.7 fusion.2
  (6 shorter events, 0.0 us)
Async XLA Ops:
  0.6 12.6 %collective-permute-start = (bf16[128,256]{1,0:T(8,128)(2,1)}, bf16[128,256]{1,0:T(8,128)(2,1)S(1)}, u32[]{:S(2)}, u32[]{:S(2)}) collective-permute-start(bf16[128,256]{1,0:T(8,128)(2,1)} %bitcast.36), channel_id=1, source_target_pairs={{0,0},{1,8},{2,22},{3,30},{4,36},{5,44},{6,50},{7,58},{8,1},{9,9},... | collective-permute-start | bytes 196616 | tf_op jit(solution)/shard_map/ppermute | solution.py:300
  13.2 7.7 %copy-start.3 = (f32[1,3,4,4]{3,2,1,0:T(4,128)S(1)}, f32[1,3,4,4]{3,2,1,0:T(4,128)}, u32[]{:S(2)}) copy-start(f32[1,3,4,4]{3,2,1,0:T(4,128)} %param.10) | copy-start | bytes 580
  14.0 18.3 %all-to-all-start = ((bf16[8,128,256]{2,1,0:T(8,128)(2,1)}), bf16[8,128,256]{2,1,0:T(8,128)(2,1)S(1)}, u32[]{:S(2)}, u32[]{:S(2)}) async-start(bf16[8,128,256]{2,1,0:T(8,128)(2,1)} %broadcast_in_dim.6), calls=%async_computation | async-start | bytes 1048576 | tf_op jit(solution)/shard_map/all_to_all | solution.py:57
  32.4 0.8 copy-start.1
  33.2 48.2 %all-to-all-start.1 = ((bf16[4,1552,256]{2,1,0:T(8,128)(2,1)}), bf16[4,1552,256]{2,1,0:T(8,128)(2,1)S(1)}, u32[]{:S(2)}, u32[]{:S(2)}) async-start(bf16[4,1552,256]{2,1,0:T(8,128)(2,1)} %get-tuple-element.30), calls=%async_computation.1 | async-start | bytes 6356992 | tf_op jit(solution)/shard_map/all_to_all | solution.py:57
  36.9 36.2 %collective-permute-start.5 = (bf16[4,3,256,256]{3,2,1,0:T(8,128)(2,1)}, bf16[4,3,256,256]{3,2,1,0:T(8,128)(2,1)}, u32[]{:S(2)}, u32[]{:S(2)}) collective-permute-start(bf16[4,3,256,256]{3,2,1,0:T(8,128)(2,1)} %renew_kept.1), channel_id=1, source_target_pairs={{0,64},{64,0},{1,65},{65,1},{2,66},{66,2},{3,67},{67,3},{4,68},{68... | collective-permute-start | bytes 4718600 | tf_op jit(solution)/shard_map/ppermute | solution.py:318
  37.8 39.6 %collective-permute-start.1 = (bf16[1552,256]{1,0:T(8,128)(2,1)}, bf16[1552,256]{1,0:T(8,128)(2,1)}, u32[]{:S(2)}, u32[]{:S(2)}) collective-permute-start(bf16[1552,256]{1,0:T(8,128)(2,1)} %get-tuple-element.31), channel_id=1, source_target_pairs={{0,17},{1,2},{2,19},{3,4},{4,21},{5,6},{6,23},{7,0},{8,25},{9,10},... | collective-permute-start | bytes 2383880 | tf_op jit(solution)/shard_map/ppermute | solution.py:315
  38.4 39.8 %collective-permute-start.2 = (bf16[1552,256]{1,0:T(8,128)(2,1)}, bf16[1552,256]{1,0:T(8,128)(2,1)}, u32[]{:S(2)}, u32[]{:S(2)}) collective-permute-start(bf16[1552,256]{1,0:T(8,128)(2,1)} %get-tuple-element.32), channel_id=1, source_target_pairs={{0,33},{1,4},{2,35},{3,6},{4,37},{5,0},{6,39},{7,2},{8,41},{9,12},... | collective-permute-start | bytes 2383880 | tf_op jit(solution)/shard_map/ppermute | solution.py:315
  41.6 38.5 %collective-permute-start.3 = (bf16[1552,256]{1,0:T(8,128)(2,1)}, bf16[1552,256]{1,0:T(8,128)(2,1)}, u32[]{:S(2)}, u32[]{:S(2)}) collective-permute-start(bf16[1552,256]{1,0:T(8,128)(2,1)} %get-tuple-element.33), channel_id=1, source_target_pairs={{0,49},{1,6},{2,51},{3,0},{4,53},{5,2},{6,55},{7,4},{8,57},{9,14},... | collective-permute-start | bytes 2383880 | tf_op jit(solution)/shard_map/ppermute | solution.py:315
  42.6 38.8 %collective-permute-start.4 = (bf16[1552,256]{1,0:T(8,128)(2,1)}, bf16[1552,256]{1,0:T(8,128)(2,1)}, u32[]{:S(2)}, u32[]{:S(2)}) collective-permute-start(bf16[1552,256]{1,0:T(8,128)(2,1)} %get-tuple-element.34), channel_id=1, source_target_pairs={{0,1},{1,0},{2,3},{3,2},{4,5},{5,4},{6,7},{7,6},{8,9},{9,8},{10,11... | collective-permute-start | bytes 2383880 | tf_op jit(solution)/shard_map/ppermute | solution.py:315
  73.1 51.9 %collective-permute-start.9 = (bf16[4,3,256,256]{3,2,1,0:T(8,128)(2,1)}, bf16[4,3,256,256]{3,2,1,0:T(8,128)(2,1)}, u32[]{:S(2)}, u32[]{:S(2)}) collective-permute-start(bf16[4,3,256,256]{3,2,1,0:T(8,128)(2,1)} %renew_swapped.1), channel_id=1, source_target_pairs={{0,64},{64,0},{1,65},{65,1},{2,66},{66,2},{3,67},{67,3},{4,68},{68... | collective-permute-start | bytes 4718600 | tf_op jit(solution)/shard_map/ppermute | solution.py:318
  77.3 20.6 %collective-permute-start.6 = (bf16[768,256]{1,0:T(8,128)(2,1)}, bf16[768,256]{1,0:T(8,128)(2,1)}, u32[]{:S(2)}, u32[]{:S(2)}) collective-permute-start(bf16[768,256]{1,0:T(8,128)(2,1)} %bitcast.7), channel_id=1, source_target_pairs={{0,16},{1,3},{2,18},{3,5},{4,20},{5,7},{6,22},{7,1},{8,24},{9,11},... | collective-permute-start | bytes 1179656 | tf_op jit(solution)/shard_map/ppermute | solution.py:321
  78.2 19.7 %collective-permute-start.7 = (bf16[768,256]{1,0:T(8,128)(2,1)}, bf16[768,256]{1,0:T(8,128)(2,1)}, u32[]{:S(2)}, u32[]{:S(2)}) collective-permute-start(bf16[768,256]{1,0:T(8,128)(2,1)} %bitcast.8), channel_id=1, source_target_pairs={{0,32},{1,5},{2,34},{3,7},{4,36},{5,1},{6,38},{7,3},{8,40},{9,13},... | collective-permute-start | bytes 1179656 | tf_op jit(solution)/shard_map/ppermute | solution.py:321
  80.1 17.9 %collective-permute-start.8 = (bf16[768,256]{1,0:T(8,128)(2,1)}, bf16[768,256]{1,0:T(8,128)(2,1)}, u32[]{:S(2)}, u32[]{:S(2)}) collective-permute-start(bf16[768,256]{1,0:T(8,128)(2,1)} %bitcast.9), channel_id=1, source_target_pairs={{0,48},{1,7},{2,50},{3,1},{4,52},{5,3},{6,54},{7,5},{8,56},{9,15},... | collective-permute-start | bytes 1179656 | tf_op jit(solution)/shard_map/ppermute | solution.py:321
  81.4 1.6 copy-start
  98.0 17.7 %all-to-all-start.2 = ((bf16[8,1,128,256]{3,2,1,0:T(8,128)(2,1)}), bf16[8,1,128,256]{3,2,1,0:T(8,128)(2,1)S(1)}, u32[]{:S(2)}, u32[]{:S(2)}) async-start(bf16[8,1,128,256]{3,2,1,0:T(8,128)(2,1)} %bitcast.26), calls=%async_computation.2 | async-start | bytes 1048576 | tf_op jit(solution)/shard_map/all_to_all | solution.py:57
  116.6 18.4 %all-to-all-start.3 = ((bf16[8,128,256]{2,1,0:T(8,128)(2,1)}), bf16[8,128,256]{2,1,0:T(8,128)(2,1)S(1)}, u32[]{:S(2)}, u32[]{:S(2)}) async-start(bf16[8,128,256]{2,1,0:T(8,128)(2,1)} %broadcast_in_dim.15), calls=%async_computation.3 | async-start | bytes 1048576 | tf_op jit(solution)/shard_map/all_to_all | solution.py:57
  126.4 24.3 %collective-permute-start.10 = (bf16[768,256]{1,0:T(8,128)(2,1)S(1)}, bf16[768,256]{1,0:T(8,128)(2,1)S(1)}, u32[]{:S(2)}, u32[]{:S(2)}) collective-permute-start(bf16[768,256]{1,0:T(8,128)(2,1)S(1)} %bitcast.31), channel_id=1, source_target_pairs={{0,17},{1,2},{2,19},{3,4},{4,21},{5,6},{6,23},{7,0},{8,25},{9,10},... | collective-permute-start | bytes 1179656 | tf_op jit(solution)/shard_map/ppermute | solution.py:322
  126.5 24.2 %collective-permute-start.11 = (bf16[768,256]{1,0:T(8,128)(2,1)S(1)}, bf16[768,256]{1,0:T(8,128)(2,1)S(1)}, u32[]{:S(2)}, u32[]{:S(2)}) collective-permute-start(bf16[768,256]{1,0:T(8,128)(2,1)S(1)} %bitcast.30), channel_id=1, source_target_pairs={{0,33},{1,4},{2,35},{3,6},{4,37},{5,0},{6,39},{7,2},{8,41},{9,12},... | collective-permute-start | bytes 1179656 | tf_op jit(solution)/shard_map/ppermute | solution.py:322
  130.9 19.8 %collective-permute-start.12 = (bf16[768,256]{1,0:T(8,128)(2,1)S(1)}, bf16[768,256]{1,0:T(8,128)(2,1)S(1)}, u32[]{:S(2)}, u32[]{:S(2)}) collective-permute-start(bf16[768,256]{1,0:T(8,128)(2,1)S(1)} %bitcast.29), channel_id=1, source_target_pairs={{0,49},{1,6},{2,51},{3,0},{4,53},{5,2},{6,55},{7,4},{8,57},{9,14},... | collective-permute-start | bytes 1179656 | tf_op jit(solution)/shard_map/ppermute | solution.py:322
  131.9 18.8 %collective-permute-start.13 = (bf16[768,256]{1,0:T(8,128)(2,1)S(1)}, bf16[768,256]{1,0:T(8,128)(2,1)}, u32[]{:S(2)}, u32[]{:S(2)}) collective-permute-start(bf16[768,256]{1,0:T(8,128)(2,1)S(1)} %bitcast.28), channel_id=1, source_target_pairs={{0,1},{1,0},{2,3},{3,2},{4,5},{5,4},{6,7},{7,6},{8,9},{9,8},{10,11... | collective-permute-start | bytes 1179656 | tf_op jit(solution)/shard_map/ppermute | solution.py:322
  135.0 0.8 copy-start.2
  150.6 0.8 copy-start.4
  150.7 0.9 copy-start.5
  150.7 1.0 copy-start.6
  183.3 14.8 %collective-permute-start.14 = (bf16[3,128,256]{2,1,0:T(8,128)(2,1)S(1)}, bf16[3,128,256]{2,1,0:T(8,128)(2,1)S(1)}, u32[]{:S(2)}, u32[]{:S(2)}) collective-permute-start(bf16[3,128,256]{2,1,0:T(8,128)(2,1)S(1)} %pad_maximum_fusion), channel_id=1, source_target_pairs={{0,0},{8,1},{22,2},{30,3},{36,4},{44,5},{50,6},{58,7},{1,8},{9,9},... | collective-permute-start | bytes 589832 | tf_op jit(solution)/shard_map/ppermute | solution.py:332

commit v5 on v4

--- a/solution.py
+++ b/solution.py
@@ -283,6 +283,30 @@
     return jnp.sum(parts.astype(F32), axis=0).astype(BF16)
 
 
+def sum_kernel(parts, total, copies):
+    value = parts[0, 0].astype(F32)
+    for k in range(1, 8):
+        value += parts[k, 0].astype(F32)
+    value = value.astype(BF16)
+    total[0] = value
+    for k in range(8):
+        copies[k] = value
+
+
+def sum_and_copy(parts):
+    return pl.pallas_call(
+        sum_kernel,
+        in_specs=[VMEM],
+        out_specs=[VMEM, VMEM],
+        out_shape=[
+            jax.ShapeDtypeStruct((1, CHUNK, BLOCK), BF16),
+            jax.ShapeDtypeStruct((8, CHUNK, BLOCK), BF16),
+        ],
+        name="sum_and_copy",
+        cost_estimate=pl.CostEstimate(flops=1 << 18, bytes_accessed=1 << 20, transcendentals=0),
+    )(parts)
+
+
 def after(value, *others):
     return lax.optimization_barrier((value, *others))[0]
 
@@ -323,9 +347,10 @@
 
     partial = apply_terms(place, field, [kept, *passed])
     half = apply_terms(place, field, [kept], near, kind=F32)
-    first = reduce_chunks(after(partial, *near).reshape(8, 1, CHUNK, BLOCK))
-    first, half = lax.optimization_barrier((first, half))
-    first_field = spread(first[0])
+    parts = exchange(after(partial, *near).reshape(8, 1, CHUNK, BLOCK), HOLDERS)
+    parts, half = lax.optimization_barrier((parts, half))
+    first, copies = sum_and_copy(parts)
+    first_field = exchange(copies, HOLDERS).reshape(LOCAL * BLOCK, BLOCK)
     partial = apply_terms(place, first_field, [kept, *passed])
     partial = apply_terms(place, after(field, partial), passed, far, half, partial)
     images = jnp.concatenate([first, reduce_chunks(partial)])

time: 200 us -> 202 us (1.010)
    unnamed x14 -> x18, local copies, waits for them, and re-layouts: 4.25 us -> 5.04 us
  transfers between devices with their start and end apart: 19 -> 19, of which waited for: 5 -> 5; matrix products, arithmetic and copies ran while one was open for 3% -> 3% of each run, Pallas kernels for 30% -> 31%
where the time goes in v5:
time: 202 us; the launch traced here: 201 us
  Pallas kernels  71.7 us (35%)
  starting transfers between devices  51.1 us (25%)
  waiting for transfers between devices  43.3 us (21%)
  blocking collectives  21.8 us (11%)
  local copies, waits for them, and re-layouts  11.1 us (5%)
    pallas_call x4, Pallas kernels, apply_terms(): pl.pallas_call(functools.partial(apply_kernel, at_ops, at_renewed, starts...  48.5 us
    all_to_all x4, starting transfers between devices, exchange(): return lax.all_to_all(value, 'op', 0, 0, axis_index_groups=groups)  26.1 us
    ppermute x2, waiting for transfers between devices, shards(): lax.ppermute(value, 'sect', [(0, 1), (1, 0)]).reshape(4, STACK, BLOCK)  22.8 us
    all_to_all x1, blocking collectives, exchange(): return lax.all_to_all(value, 'op', 0, 0, axis_index_groups=groups)  21.8 us
    pallas_call x2, Pallas kernels, renew(): pl.pallas_call(renew_kernel, grid_spec=grid_spec, out_shape=jax.ShapeDtyp...  14.4 us
    ppermute x1, waiting for transfers between devices, shards(): images = lax.ppermute(images, 'op', TO_OWNERS)  12.9 us
    all_to_all x4, waiting for transfers between devices, exchange(): return lax.all_to_all(value, 'op', 0, 0, axis_index_groups=groups)  7.67 us
    pallas_call x1, Pallas kernels, pack(): pl.pallas_call(pack_kernel, in_specs=[SMEM, SMEM, SMEM, SMEM, ANY, ANY],...  6.78 us
  transfers between devices with their start and end apart: 19, of which 5 were waited for; matrix products, arithmetic and copies ran while one was open for 3% of the time, Pallas kernels for 31%

profile of v5, /device:TPU:120, one launch (start us, length us, event | category | flops | bytes accessed | tf_op | source)
XLA Modules:
  0.0 200.7 jit_solution(17901873185089994989)
XLA Ops:
  0.6 4.8 %collective-permute-start = (bf16[128,256]{1,0:T(8,128)(2,1)}, bf16[128,256]{1,0:T(8,128)(2,1)S(1)}, u32[]{:S(2)}, u32[]{:S(2)}) collective-permute-start(bf16[128,256]{1,0:T(8,128)(2,1)} %bitcast.31), channel_id=1, source_target_pairs={{0,0},{1,8},{2,22},{3,30},{4,36},{5,44},{6,50},{7,58},{8,1},{9,9},... | collective-permute-start | bytes 196616 | tf_op jit(solution)/shard_map/ppermute | solution.py:324
  5.4 0.7 pad_add_fusion.place
  6.1 7.2 %renew_kept.1 = bf16[4,3,256,256]{3,2,1,0:T(8,128)(2,1)} custom-call(s32[3]{0:T(128)} %pad_add_fusion.place, s32[8]{0:T(128)} %bitcast.28, bf16[1,3,8,256,256]{4,3,2,1,0:T(8,128)(2,1)} %left.5, bf16[1,8,4,256,256]{4,3,2,1,0:T(8,128)(2,1)} %tensor.3), custom_call_target="tpu_custom_call" | custom-call | flops 3221225472 | bytes 20971520 | tf_op jit(solution)/shard_map/renew_kept/pallas_call | solution.py:162
  13.3 0.0 collective-permute-done
  13.3 0.8 broadcast_in_dim.2
  14.1 6.8 %all-to-all-start = ((bf16[8,128,256]{2,1,0:T(8,128)(2,1)}), bf16[8,128,256]{2,1,0:T(8,128)(2,1)S(1)}, u32[]{:S(2)}, u32[]{:S(2)}) async-start(bf16[8,128,256]{2,1,0:T(8,128)(2,1)} %broadcast_in_dim.2), calls=%async_computation | async-start | bytes 1048576 | tf_op jit(solution)/shard_map/all_to_all | solution.py:57
  20.9 0.6 reshape.37.site
  21.5 6.8 %pack.1 = (bf16[4,1552,256]{2,1,0:T(8,128)(2,1)}, bf16[1552,256]{1,0:T(8,128)(2,1)}, bf16[1552,256]{1,0:T(8,128)(2,1)}, bf16[1552,256]{1,0:T(8,128)(2,1)}, bf16[1552,256]{1,0:T(8,128)(2,1)}) custom-call(s32[3]{0:T(128)} %pad_add_fusion.place, s32[8]{0:T(128)} %bitcast.29, f32[48]{0:T(128)} %reshape.37.site, s32[3]{0:T(128)} %bitcast.27, ...), custom_call_target="tpu_custom_call" | custom-call | flops 1048576 | bytes 65536 | tf_op jit(solution)/shard_map/pack/pallas_call | solution.py:111
  28.3 4.1 %all-to-all-done = bf16[8,128,256]{2,1,0:T(8,128)(2,1)S(1)} async-done(((bf16[8,128,256]{2,1,0:T(8,128)(2,1)}), bf16[8,128,256]{2,1,0:T(8,128)(2,1)S(1)}, u32[]{:S(2)}, u32[]{:S(2)}) %all-to-all-start) | async-done | bytes 524320 | tf_op jit(solution)/shard_map/all_to_all | solution.py:57
  32.4 0.8 copy-done.2
  33.2 3.7 %all-to-all-start.1 = ((bf16[4,1552,256]{2,1,0:T(8,128)(2,1)}), bf16[4,1552,256]{2,1,0:T(8,128)(2,1)S(1)}, u32[]{:S(2)}, u32[]{:S(2)}) async-start(bf16[4,1552,256]{2,1,0:T(8,128)(2,1)} %get-tuple-element.32), calls=%async_computation.1 | async-start | bytes 6356992 | tf_op jit(solution)/shard_map/all_to_all | solution.py:57
  36.9 0.9 collective-permute-start.5
  37.8 0.7 collective-permute-start.1
  38.5 3.2 %collective-permute-start.2 = (bf16[1552,256]{1,0:T(8,128)(2,1)}, bf16[1552,256]{1,0:T(8,128)(2,1)}, u32[]{:S(2)}, u32[]{:S(2)}) collective-permute-start(bf16[1552,256]{1,0:T(8,128)(2,1)} %get-tuple-element.34), channel_id=1, source_target_pairs={{0,33},{1,4},{2,35},{3,6},{4,37},{5,0},{6,39},{7,2},{8,41},{9,12},... | collective-permute-start | bytes 2383880 | tf_op jit(solution)/shard_map/ppermute | solution.py:339
  41.7 0.9 collective-permute-start.3
  42.6 0.5 collective-permute-start.4
  43.1 7.2 %renew_swapped.1 = bf16[4,3,256,256]{3,2,1,0:T(8,128)(2,1)} custom-call(s32[3]{0:T(128)} %pad_add_fusion.place, s32[8]{0:T(128)} %bitcast.30, bf16[1,3,8,256,256]{4,3,2,1,0:T(8,128)(2,1)} %left.5, bf16[1,8,4,256,256]{4,3,2,1,0:T(8,128)(2,1)} %tensor.3), custom_call_target="tpu_custom_call" | custom-call | flops 3221225472 | bytes 20971520 | tf_op jit(solution)/shard_map/renew_swapped/pallas_call | solution.py:162
  50.3 22.8 %collective-permute-done.5 = bf16[4,3,256,256]{3,2,1,0:T(8,128)(2,1)} collective-permute-done((bf16[4,3,256,256]{3,2,1,0:T(8,128)(2,1)}, bf16[4,3,256,256]{3,2,1,0:T(8,128)(2,1)}, u32[]{:S(2)}, u32[]{:S(2)}) %collective-permute-start.5) | collective-permute-done | bytes 1572896 | tf_op jit(solution)/shard_map/ppermute | solution.py:342
  73.0 1.7 collective-permute-start.9
  74.8 2.5 %fusion.1 = (bf16[1,3,256,256]{3,2,1,0:T(8,128)(2,1)}, bf16[1,3,256,256]{3,2,1,0:T(8,128)(2,1)}, bf16[1,3,256,256]{3,2,1,0:T(8,128)(2,1)}, bf16[1,3,256,256]{3,2,1,0:T(8,128)(2,1)}) fusion(bf16[4,3,256,256]{3,2,1,0:T(8,128)(2,1)} %collective-permute-done.5), kind=kLoop, calls=%fused_computation.3 | loop fusion | bytes 3145728 | tf_op jit(solution)/shard_map/slice | solution.py:345
  77.3 0.0 collective-permute-done.1.refs_1_.refs_0_
  77.3 1.0 collective-permute-start.6
  78.3 0.0 collective-permute-done.2.refs_2_.refs_1_
  78.3 1.8 collective-permute-start.7
  80.1 0.0 collective-permute-done.3.refs_3_.refs_2_
  80.1 1.2 collective-permute-start.8
  81.4 0.0 collective-permute-done.4.refs_4_.refs_3_
  81.4 0.0 all-to-all-done.1.refs_0_
  81.4 1.6 copy-done
  83.0 14.9 %apply_terms_8.2 = bf16[1024,256]{1,0:T(8,128)(2,1)} custom-call(s32[3]{0:T(128)} %pad_add_fusion.place, bf16[1024,256]{1,0:T(8,128)(2,1)} %bitcast.17, bf16[4,1552,256]{2,1,0:T(8,128)(2,1)} %copy-done, bf16[1552,256]{1,0:T(8,128)(2,1)} %collective-permute-done.1.refs_1_.refs_0_, bf16[1552,256]{1,0:T(8,128)(2,1)} %collective-permute-done.2.refs_2_.refs_1_, ...), custom_call_target="tpu_custom_call" | custom-call | flops 6442450944 | bytes 50331648 | tf_op jit(solution)/shard_map/apply_terms_8/pallas_call | solution.py:261
  97.9 0.0 collective-permute-done.6.refs_1_
  97.9 0.0 collective-permute-done.7.refs_2_
  97.9 0.0 collective-permute-done.8.refs_3_
  97.9 7.2 %all-to-all-start.2 = ((bf16[8,1,128,256]{3,2,1,0:T(8,128)(2,1)}), bf16[8,1,128,256]{3,2,1,0:T(8,128)(2,1)S(1)}, u32[]{:S(2)}, u32[]{:S(2)}) async-start(bf16[8,1,128,256]{3,2,1,0:T(8,128)(2,1)} %bitcast.21), calls=%async_computation.2 | async-start | bytes 1048576 | tf_op jit(solution)/shard_map/all_to_all | solution.py:57
  105.2 9.2 %apply_moved_4.2.refs_8_ = f32[1024,256]{1,0:T(8,128)} custom-call(s32[3]{0:T(128)} %pad_add_fusion.place, bf16[1024,256]{1,0:T(8,128)(2,1)} %bitcast.18, bf16[4,1552,256]{2,1,0:T(8,128)(2,1)} %copy-done, bf16[768,256]{1,0:T(8,128)(2,1)} %collective-permute-done.6.refs_1_, bf16[768,256]{1,0:T(8,128)(2,1)} %collective-permute-done.7.refs_2_, ...), custom_call_target="tpu_custom_call" | custom-call | flops 3221225472 | bytes 50331648 | tf_op jit(solution)/shard_map/apply_moved_4/pallas_call | solution.py:261
  114.3 1.3 all-to-all-done.2.parts
  115.7 0.8 copy-done.1
  116.5 2.0 sum_and_copy.1
  118.5 8.3 %all-to-all-start.3 = ((bf16[8,128,256]{2,1,0:T(8,128)(2,1)}), bf16[8,128,256]{2,1,0:T(8,128)(2,1)S(1)}, u32[]{:S(2)}, u32[]{:S(2)}) async-start(bf16[8,128,256]{2,1,0:T(8,128)(2,1)} %get-tuple-element.41), calls=%async_computation.3 | async-start | bytes 1048576 | tf_op jit(solution)/shard_map/all_to_all | solution.py:57
  126.7 0.0 collective-permute-done.9
  126.7 1.5 fusion
  128.2 0.1 collective-permute-start.10
  128.3 4.9 %collective-permute-start.11 = (bf16[768,256]{1,0:T(8,128)(2,1)S(1)}, bf16[768,256]{1,0:T(8,128)(2,1)S(1)}, u32[]{:S(2)}, u32[]{:S(2)}) collective-permute-start(bf16[768,256]{1,0:T(8,128)(2,1)S(1)} %bitcast.25), channel_id=1, source_target_pairs={{0,33},{1,4},{2,35},{3,6},{4,37},{5,0},{6,39},{7,2},{8,41},{9,12},... | collective-permute-start | bytes 1179656 | tf_op jit(solution)/shard_map/ppermute | solution.py:346
  133.2 0.6 collective-permute-start.12
  133.7 0.9 collective-permute-start.13
  134.6 2.2 %all-to-all-done.3 = bf16[8,128,256]{2,1,0:T(8,128)(2,1)S(1)} async-done(((bf16[8,128,256]{2,1,0:T(8,128)(2,1)}), bf16[8,128,256]{2,1,0:T(8,128)(2,1)S(1)}, u32[]{:S(2)}, u32[]{:S(2)}) %all-to-all-start.3) | async-done | bytes 524320 | tf_op jit(solution)/shard_map/all_to_all | solution.py:57
  136.8 0.8 copy-done.3
  137.6 14.9 %apply_terms_8.3.refs_9_ = bf16[1024,256]{1,0:T(8,128)(2,1)} custom-call(s32[3]{0:T(128)} %pad_add_fusion.place, bf16[1024,256]{1,0:T(8,128)(2,1)} %bitcast.20, bf16[4,1552,256]{2,1,0:T(8,128)(2,1)} %copy-done, bf16[1552,256]{1,0:T(8,128)(2,1)} %collective-permute-done.1.refs_1_.refs_0_, bf16[1552,256]{1,0:T(8,128)(2,1)} %collective-permute-done.2.refs_2_.refs_1_, ...), custom_call_target="tpu_custom_call" | custom-call | flops 6442450944 | bytes 50331648 | tf_op jit(solution)/shard_map/apply_terms_8/pallas_call | solution.py:261
  152.5 0.0 collective-permute-done.10.refs_4_
  152.5 0.0 copy-start.6
  152.5 0.0 collective-permute-done.11.refs_5_
  152.6 0.0 collective-permute-done.12.refs_6_
  152.6 0.0 collective-permute-done.13.refs_7_
  152.6 0.7 copy-done.6
  153.3 0.1 copy-done.7
  153.4 0.2 copy-done.8
  153.6 9.6 %apply_moved_4.3 = bf16[8,2,128,256]{3,2,1,0:T(8,128)(2,1)} custom-call(s32[3]{0:T(128)} %pad_add_fusion.place, bf16[1024,256]{1,0:T(8,128)(2,1)} %bitcast.19, bf16[1552,256]{1,0:T(8,128)(2,1)} %collective-permute-done.1.refs_1_.refs_0_, bf16[1552,256]{1,0:T(8,128)(2,1)} %collective-permute-done.2.refs_2_.refs_1_, ...), custom_call_target="tpu_custom_call" | custom-call | flops 3221225472 | bytes 50331648 | tf_op jit(solution)/shard_map/apply_moved_4/pallas_call | solution.py:261
  163.2 0.0 copy-start.4
  163.2 21.8 %all_to_all.25 = bf16[8,2,128,256]{3,2,1,0:T(8,128)(2,1)S(1)} all-to-all(bf16[8,2,128,256]{3,2,1,0:T(8,128)(2,1)} %apply_moved_4.3), channel_id=1, replica_groups={{0,8,22,30,36,44,50,58},{1,9,23,31,37,45,51,59},{2,10,16,24,38,46,52,60..., dimensions={0} | all-to-all | bytes 2097152 | tf_op jit(solution)/shard_map/all_to_all | solution.py:57
  185.1 0.1 reduce_sum.12
  185.2 0.0 copy-done.4
  185.3 1.9 collective-permute-start.14
  187.2 12.9 %collective-permute-done.14 = bf16[3,128,256]{2,1,0:T(8,128)(2,1)S(1)} collective-permute-done((bf16[3,128,256]{2,1,0:T(8,128)(2,1)S(1)}, bf16[3,128,256]{2,1,0:T(8,128)(2,1)S(1)}, u32[]{:S(2)}, u32[]{:S(2)}) %collective-permute-start.14) | collective-permute-done | bytes 196640 | tf_op jit(solution)/shard_map/ppermute | solution.py:357
  200.0 0.7 fusion.2
  (9 shorter events, 0.0 us)
Async XLA Ops:
  0.6 12.6 %collective-permute-start = (bf16[128,256]{1,0:T(8,128)(2,1)}, bf16[128,256]{1,0:T(8,128)(2,1)S(1)}, u32[]{:S(2)}, u32[]{:S(2)}) collective-permute-start(bf16[128,256]{1,0:T(8,128)(2,1)} %bitcast.31), channel_id=1, source_target_pairs={{0,0},{1,8},{2,22},{3,30},{4,36},{5,44},{6,50},{7,58},{8,1},{9,9},... | collective-permute-start | bytes 196616 | tf_op jit(solution)/shard_map/ppermute | solution.py:324
  13.3 7.7 %copy-start.5 = (f32[1,3,4,4]{3,2,1,0:T(4,128)S(1)}, f32[1,3,4,4]{3,2,1,0:T(4,128)}, u32[]{:S(2)}) copy-start(f32[1,3,4,4]{3,2,1,0:T(4,128)} %param.10) | copy-start | bytes 580
  14.1 18.3 %all-to-all-start = ((bf16[8,128,256]{2,1,0:T(8,128)(2,1)}), bf16[8,128,256]{2,1,0:T(8,128)(2,1)S(1)}, u32[]{:S(2)}, u32[]{:S(2)}) async-start(bf16[8,128,256]{2,1,0:T(8,128)(2,1)} %broadcast_in_dim.2), calls=%async_computation | async-start | bytes 1048576 | tf_op jit(solution)/shard_map/all_to_all | solution.py:57
  32.4 0.8 copy-start.2
  33.2 48.2 %all-to-all-start.1 = ((bf16[4,1552,256]{2,1,0:T(8,128)(2,1)}), bf16[4,1552,256]{2,1,0:T(8,128)(2,1)S(1)}, u32[]{:S(2)}, u32[]{:S(2)}) async-start(bf16[4,1552,256]{2,1,0:T(8,128)(2,1)} %get-tuple-element.32), calls=%async_computation.1 | async-start | bytes 6356992 | tf_op jit(solution)/shard_map/all_to_all | solution.py:57
  36.9 36.1 %collective-permute-start.5 = (bf16[4,3,256,256]{3,2,1,0:T(8,128)(2,1)}, bf16[4,3,256,256]{3,2,1,0:T(8,128)(2,1)}, u32[]{:S(2)}, u32[]{:S(2)}) collective-permute-start(bf16[4,3,256,256]{3,2,1,0:T(8,128)(2,1)} %renew_kept.1), channel_id=1, source_target_pairs={{0,64},{64,0},{1,65},{65,1},{2,66},{66,2},{3,67},{67,3},{4,68},{68... | collective-permute-start | bytes 4718600 | tf_op jit(solution)/shard_map/ppermute | solution.py:342
  37.8 39.5 %collective-permute-start.1 = (bf16[1552,256]{1,0:T(8,128)(2,1)}, bf16[1552,256]{1,0:T(8,128)(2,1)}, u32[]{:S(2)}, u32[]{:S(2)}) collective-permute-start(bf16[1552,256]{1,0:T(8,128)(2,1)} %get-tuple-element.33), channel_id=1, source_target_pairs={{0,17},{1,2},{2,19},{3,4},{4,21},{5,6},{6,23},{7,0},{8,25},{9,10},... | collective-permute-start | bytes 2383880 | tf_op jit(solution)/shard_map/ppermute | solution.py:339
  38.5 39.8 %collective-permute-start.2 = (bf16[1552,256]{1,0:T(8,128)(2,1)}, bf16[1552,256]{1,0:T(8,128)(2,1)}, u32[]{:S(2)}, u32[]{:S(2)}) collective-permute-start(bf16[1552,256]{1,0:T(8,128)(2,1)} %get-tuple-element.34), channel_id=1, source_target_pairs={{0,33},{1,4},{2,35},{3,6},{4,37},{5,0},{6,39},{7,2},{8,41},{9,12},... | collective-permute-start | bytes 2383880 | tf_op jit(solution)/shard_map/ppermute | solution.py:339
  41.7 38.5 %collective-permute-start.3 = (bf16[1552,256]{1,0:T(8,128)(2,1)}, bf16[1552,256]{1,0:T(8,128)(2,1)}, u32[]{:S(2)}, u32[]{:S(2)}) collective-permute-start(bf16[1552,256]{1,0:T(8,128)(2,1)} %get-tuple-element.35), channel_id=1, source_target_pairs={{0,49},{1,6},{2,51},{3,0},{4,53},{5,2},{6,55},{7,4},{8,57},{9,14},... | collective-permute-start | bytes 2383880 | tf_op jit(solution)/shard_map/ppermute | solution.py:339
  42.6 38.8 %collective-permute-start.4 = (bf16[1552,256]{1,0:T(8,128)(2,1)}, bf16[1552,256]{1,0:T(8,128)(2,1)}, u32[]{:S(2)}, u32[]{:S(2)}) collective-permute-start(bf16[1552,256]{1,0:T(8,128)(2,1)} %get-tuple-element.36), channel_id=1, source_target_pairs={{0,1},{1,0},{2,3},{3,2},{4,5},{5,4},{6,7},{7,6},{8,9},{9,8},{10,11... | collective-permute-start | bytes 2383880 | tf_op jit(solution)/shard_map/ppermute | solution.py:339
  73.0 53.7 %collective-permute-start.9 = (bf16[4,3,256,256]{3,2,1,0:T(8,128)(2,1)}, bf16[4,3,256,256]{3,2,1,0:T(8,128)(2,1)}, u32[]{:S(2)}, u32[]{:S(2)}) collective-permute-start(bf16[4,3,256,256]{3,2,1,0:T(8,128)(2,1)} %renew_swapped.1), channel_id=1, source_target_pairs={{0,64},{64,0},{1,65},{65,1},{2,66},{66,2},{3,67},{67,3},{4,68},{68... | collective-permute-start | bytes 4718600 | tf_op jit(solution)/shard_map/ppermute | solution.py:342
  77.3 20.6 %collective-permute-start.6 = (bf16[768,256]{1,0:T(8,128)(2,1)}, bf16[768,256]{1,0:T(8,128)(2,1)}, u32[]{:S(2)}, u32[]{:S(2)}) collective-permute-start(bf16[768,256]{1,0:T(8,128)(2,1)} %bitcast.7), channel_id=1, source_target_pairs={{0,16},{1,3},{2,18},{3,5},{4,20},{5,7},{6,22},{7,1},{8,24},{9,11},... | collective-permute-start | bytes 1179656 | tf_op jit(solution)/shard_map/ppermute | solution.py:345
  78.3 19.6 %collective-permute-start.7 = (bf16[768,256]{1,0:T(8,128)(2,1)}, bf16[768,256]{1,0:T(8,128)(2,1)}, u32[]{:S(2)}, u32[]{:S(2)}) collective-permute-start(bf16[768,256]{1,0:T(8,128)(2,1)} %bitcast.8), channel_id=1, source_target_pairs={{0,32},{1,5},{2,34},{3,7},{4,36},{5,1},{6,38},{7,3},{8,40},{9,13},... | collective-permute-start | bytes 1179656 | tf_op jit(solution)/shard_map/ppermute | solution.py:345
  80.1 17.8 %collective-permute-start.8 = (bf16[768,256]{1,0:T(8,128)(2,1)}, bf16[768,256]{1,0:T(8,128)(2,1)}, u32[]{:S(2)}, u32[]{:S(2)}) collective-permute-start(bf16[768,256]{1,0:T(8,128)(2,1)} %bitcast.9), channel_id=1, source_target_pairs={{0,48},{1,7},{2,50},{3,1},{4,52},{5,3},{6,54},{7,5},{8,56},{9,15},... | collective-permute-start | bytes 1179656 | tf_op jit(solution)/shard_map/ppermute | solution.py:345
  81.4 1.6 copy-start
  97.9 17.8 %all-to-all-start.2 = ((bf16[8,1,128,256]{3,2,1,0:T(8,128)(2,1)}), bf16[8,1,128,256]{3,2,1,0:T(8,128)(2,1)S(1)}, u32[]{:S(2)}, u32[]{:S(2)}) async-start(bf16[8,1,128,256]{3,2,1,0:T(8,128)(2,1)} %bitcast.21), calls=%async_computation.2 | async-start | bytes 1048576 | tf_op jit(solution)/shard_map/all_to_all | solution.py:57
  115.7 0.8 copy-start.1
  118.5 18.4 %all-to-all-start.3 = ((bf16[8,128,256]{2,1,0:T(8,128)(2,1)}), bf16[8,128,256]{2,1,0:T(8,128)(2,1)S(1)}, u32[]{:S(2)}, u32[]{:S(2)}) async-start(bf16[8,128,256]{2,1,0:T(8,128)(2,1)} %get-tuple-element.41), calls=%async_computation.3 | async-start | bytes 1048576 | tf_op jit(solution)/shard_map/all_to_all | solution.py:57
  128.2 24.3 %collective-permute-start.10 = (bf16[768,256]{1,0:T(8,128)(2,1)S(1)}, bf16[768,256]{1,0:T(8,128)(2,1)S(1)}, u32[]{:S(2)}, u32[]{:S(2)}) collective-permute-start(bf16[768,256]{1,0:T(8,128)(2,1)S(1)} %bitcast.26), channel_id=1, source_target_pairs={{0,17},{1,2},{2,19},{3,4},{4,21},{5,6},{6,23},{7,0},{8,25},{9,10},... | collective-permute-start | bytes 1179656 | tf_op jit(solution)/shard_map/ppermute | solution.py:346
  128.3 24.2 %collective-permute-start.11 = (bf16[768,256]{1,0:T(8,128)(2,1)S(1)}, bf16[768,256]{1,0:T(8,128)(2,1)S(1)}, u32[]{:S(2)}, u32[]{:S(2)}) collective-permute-start(bf16[768,256]{1,0:T(8,128)(2,1)S(1)} %bitcast.25), channel_id=1, source_target_pairs={{0,33},{1,4},{2,35},{3,6},{4,37},{5,0},{6,39},{7,2},{8,41},{9,12},... | collective-permute-start | bytes 1179656 | tf_op jit(solution)/shard_map/ppermute | solution.py:346
  133.2 19.4 %collective-permute-start.12 = (bf16[768,256]{1,0:T(8,128)(2,1)S(1)}, bf16[768,256]{1,0:T(8,128)(2,1)S(1)}, u32[]{:S(2)}, u32[]{:S(2)}) collective-permute-start(bf16[768,256]{1,0:T(8,128)(2,1)S(1)} %bitcast.24), channel_id=1, source_target_pairs={{0,49},{1,6},{2,51},{3,0},{4,53},{5,2},{6,55},{7,4},{8,57},{9,14},... | collective-permute-start | bytes 1179656 | tf_op jit(solution)/shard_map/ppermute | solution.py:346
  133.7 18.9 %collective-permute-start.13 = (bf16[768,256]{1,0:T(8,128)(2,1)S(1)}, bf16[768,256]{1,0:T(8,128)(2,1)}, u32[]{:S(2)}, u32[]{:S(2)}) collective-permute-start(bf16[768,256]{1,0:T(8,128)(2,1)S(1)} %bitcast.23), channel_id=1, source_target_pairs={{0,1},{1,0},{2,3},{3,2},{4,5},{5,4},{6,7},{7,6},{8,9},{9,8},{10,11... | collective-permute-start | bytes 1179656 | tf_op jit(solution)/shard_map/ppermute | solution.py:346
  136.8 0.8 copy-start.3
  152.5 0.8 copy-start.6
  152.5 0.9 copy-start.7
  152.6 1.0 copy-start.8
  163.2 22.0 %copy-start.4 = (bf16[1,128,256]{2,1,0:T(8,128)(2,1)S(1)}, bf16[1,128,256]{2,1,0:T(8,128)(2,1)}, u32[]{:S(2)}) copy-start(bf16[1,128,256]{2,1,0:T(8,128)(2,1)} %get-tuple-element.40) | copy-start | bytes 196612
  185.3 14.8 %collective-permute-start.14 = (bf16[3,128,256]{2,1,0:T(8,128)(2,1)S(1)}, bf16[3,128,256]{2,1,0:T(8,128)(2,1)S(1)}, u32[]{:S(2)}, u32[]{:S(2)}) collective-permute-start(bf16[3,128,256]{2,1,0:T(8,128)(2,1)S(1)} %pad_maximum_fusion), channel_id=1, source_target_pairs={{0,0},{8,1},{22,2},{30,3},{36,4},{44,5},{50,6},{58,7},{1,8},{9,9},... | collective-permute-start | bytes 589832 | tf_op jit(solution)/shard_map/ppermute | solution.py:357
